TPU v7x, 128 devices: a whole 4x4x4 slice. The times are simulated.
128 devices in a mesh: lat: 8 (over x_lo, y), lon: 16 (over z, x_hi, core).
Axes of the slice: x: 4 (x_hi: 2, x_lo: 2; x = x_hi * 2 + x_lo), y: 4, z: 4, core: 2. Of those that a mesh axis runs over, the one named last changes fastest.
Arguments:
- grad_rows: bfloat16 [131072, 128], P(('lat', 'lon')), may hold values from -6 to 6
- owner: int32 [131072, 1], P(('lat', 'lon')), may hold values from 0 to 127; in each aligned block of 1024 rows (0 to 1023, 1024 to 2047, ...) at most 16 rows name the same one
- lat_offset: int32 [131072], P(('lat', 'lon')), may hold values from 0 to 63
- lon_offset: int32 [131072], P(('lat', 'lon')), may hold values from 0 to 127
- position: bfloat16 [131072, 2], P(('lat', 'lon')), may hold values from 0 to 1
- live_count: int32 [128], P(('lat', 'lon')), may hold values from 512 to 1024
- features: bfloat16 [512, 2048, 128], P('lat', 'lon'), may hold values from -6 to 6
- conv_weight: bfloat16 [3, 3, 128, 128], replicated, may hold values from -0.1875 to 0.1875
Outputs:
- input_grad: bfloat16 [512, 2048, 128], P('lat', 'lon')
- weight_grad: float32 [3, 3, 128, 128], replicated
Inputs may be any that keep to these rules, and one draw needn't show every extreme that they name: `owner`: among the 1024 rows of one device no tile is named more than 16 times, a bound that some block reaches. `live_count`: entry k counts the real rows among the rows of device k, which come first.
All inputs are finite; a program needn't handle non-finite values.
Results may differ from a plain program's by a relative error of at most 0.012.
Values may be sent and summed in bfloat16 or wider, within the bound.
No kernel may reach another device: no remote copies, remote signals or barrier semaphores. Data moves between devices by JAX's collectives and lax.ppermute only.
A program may use at most 128 MiB of HBM per device.

v0:
```python
import math

import jax
import jax.numpy as jnp
from jax import lax
from jax.sharding import PartitionSpec as P

rbf_scale = 1.5


def padded_2(cells, sides, width, closed):
    for axis, dim in sides:
        count = lax.axis_size(axis)
        ends = count if closed else count - 1
        head = lax.slice_in_dim(cells, 0, width, axis=dim)
        tail = lax.slice_in_dim(cells, cells.shape[dim] - width, cells.shape[dim], axis=dim)
        cells = jnp.concatenate(
            [
                lax.ppermute(tail, axis, [(i, (i + 1) % count) for i in range(ends)]),
                cells,
                lax.ppermute(head, axis, [((i + 1) % count, i) for i in range(ends)]),
            ],
            axis=dim,
        )
    return cells


def cut_along(value, dim, count):
    before, after = (value.shape[:dim], value.shape[dim + 1 :])
    return jnp.moveaxis(value.reshape(*before, count, -1, *after), dim, 0)


def in_order(parts, dim):
    shape = list(parts.shape[1:])
    shape[dim] *= parts.shape[0]
    return jnp.moveaxis(parts, 0, dim).reshape(shape)


def one_exchange(value, axis, axes, splits, concats):
    sizes = [lax.axis_size(a) for a in axes]
    parts = cut_along(value, splits[0], sizes[0])
    parts = jnp.moveaxis(cut_along(parts, splits[1] + 1, sizes[1]), 0, 1)
    inside = parts.shape[2:]
    parts = parts.reshape(-1, *inside)
    parts = lax.all_to_all(parts, axis, split_axis=0, concat_axis=0, tiled=True)
    parts = in_order(parts.reshape(*sizes, *inside), concats[0] + 1)
    return in_order(parts, concats[1])


def profile(frac):
    tap_index = jnp.arange(8).astype(frac.dtype)
    return jnp.exp(
        -jnp.square(tap_index[None, :] - 3.0 - frac[:, None]) / (2.0 * rbf_scale * rbf_scale)
    )


def clear_rim(padded):
    lat_index = lax.axis_index("lat")
    lat_count = lax.axis_size("lat")
    row_line = jnp.arange(padded.shape[0], dtype=jnp.int32)
    masked = (row_line == 0) & (lat_index == 0) | (row_line == padded.shape[0] - 1) & (
        lat_index == lat_count - 1
    )
    return jnp.where(masked[:, None, None], jnp.zeros_like(padded), padded)


def tap_matrix(offsets, weights, extent):
    tap_ints = jnp.arange(8, dtype=jnp.int32)
    cells = offsets[:, None] + tap_ints[None, :] + 1
    line = jnp.arange(extent, dtype=jnp.int32)
    picked = jnp.where(
        cells[:, :, None] == line[None, None, :], weights.astype(jnp.float32)[:, :, None], 0.0
    )
    return jnp.sum(picked, axis=1).astype(jnp.bfloat16)


def shards(grad_rows, owner, lat_offset, lon_offset, position, live_count, features, conv_weight):
    lat_total = lax.axis_size("lat")
    lon_total = lax.axis_size("lon")
    device_total = lat_total * lon_total
    row_total = grad_rows.shape[0]
    channels = grad_rows.shape[1]
    tile_lat = features.shape[0]
    tile_lon = features.shape[1]
    capacity = max(2, 2 * row_total // device_total)
    input_padded = clear_rim(padded_2(features, (("lat", 0), ("lon", 1)), 1, True))
    owner_tile = owner[:, 0]
    is_live = jnp.arange(row_total, dtype=jnp.int32) < live_count[0]
    matches = (
        (owner_tile[:, None] == jnp.arange(device_total, dtype=jnp.int32)[None, :])
        & is_live[:, None]
    ).astype(jnp.int32)
    earlier = jnp.cumsum(matches, axis=0) - matches
    slot_rank = jnp.sum(earlier * matches, axis=1)
    slot_index = jnp.where(is_live, owner_tile * capacity + slot_rank, device_total * capacity)
    outgoing = (
        jnp.zeros((device_total * capacity, channels), jnp.bfloat16)
        .at[slot_index]
        .set(grad_rows, mode="drop")
    )
    geometry = jnp.stack(
        [
            position[:, 0],
            position[:, 1],
            lat_offset.astype(jnp.bfloat16),
            lon_offset.astype(jnp.bfloat16),
        ],
        axis=1,
    )
    place_out = (
        jnp.zeros((device_total * capacity, 4), jnp.bfloat16)
        .at[slot_index]
        .set(geometry, mode="drop")
    )
    incoming, place_in = (
        one_exchange(
            outgoing.reshape(lat_total, lon_total, capacity, channels),
            ("lat", "lon"),
            ("lat", "lon"),
            (0, 1),
            (0, 1),
        ),
        one_exchange(
            place_out.reshape(lat_total, lon_total, capacity, 4),
            ("lat", "lon"),
            ("lat", "lon"),
            (0, 1),
            (0, 1),
        ),
    )
    incoming = incoming.reshape(-1, channels)
    place_in = place_in.reshape(-1, 4).astype(jnp.float32)
    padded_lat = tile_lat + 8
    padded_lon = tile_lon + 8
    slot_total = incoming.shape[0]
    block_rows = math.gcd(slot_total, 256)

    def accumulate(canvas, payload):
        rows_blk, place_blk = payload
        lat_weight = profile(place_blk[:, 0]).astype(jnp.bfloat16)
        lon_weight = profile(place_blk[:, 1]).astype(jnp.bfloat16)
        lat_matrix = tap_matrix(place_blk[:, 2].astype(jnp.int32), lat_weight, padded_lat)
        lon_matrix = tap_matrix(place_blk[:, 3].astype(jnp.int32), lon_weight, padded_lon)
        spread = (lon_matrix[:, :, None] * rows_blk[:, None, :]).reshape(
            rows_blk.shape[0], padded_lon * channels
        )
        canvas = canvas + lax.dot_general(
            lat_matrix, spread, (((0,), (0,)), ((), ())), preferred_element_type=jnp.float32
        )
        return (canvas, None)

    canvas, _ = lax.scan(
        accumulate,
        jnp.zeros((padded_lat, padded_lon * channels), jnp.float32),
        (incoming.reshape(-1, block_rows, channels), place_in.reshape(-1, block_rows, 4)),
    )
    canvas = canvas.reshape(padded_lat, padded_lon, channels)
    edge_rows = jnp.concatenate([canvas[:5], canvas[-5:]], axis=0)
    edge_rows = padded_2(edge_rows.astype(jnp.bfloat16), (("lat", 0),), 5, False).astype(
        edge_rows.dtype
    )
    inner = canvas[4:-4]
    inner = inner.at[:4].add(edge_rows[1:5]).at[-4:].add(edge_rows[15:19])
    rim_top = edge_rows[0] + canvas[3]
    rim_bottom = canvas[-4] + edge_rows[19]
    tall = jnp.concatenate([rim_top[None], inner, rim_bottom[None]], axis=0)
    side_cols = jnp.concatenate([tall[:, :5], tall[:, -5:]], axis=1)
    side_cols = padded_2(side_cols.astype(jnp.bfloat16), (("lon", 1),), 5, True).astype(
        side_cols.dtype
    )
    middle = tall[:, 4:-4]
    middle = middle.at[:, :4].add(side_cols[:, 1:5]).at[:, -4:].add(side_cols[:, 15:19])
    rim_left = side_cols[:, 0] + tall[:, 3]
    rim_right = tall[:, -4] + side_cols[:, 19]
    whole = jnp.concatenate([rim_left[:, None], middle, rim_right[:, None]], axis=1)
    grid_padded = clear_rim(whole.astype(jnp.bfloat16))
    grid_grad = grid_padded[1:-1, 1:-1]
    flat_grad = grid_grad.reshape(-1, channels)
    input_grad = jnp.zeros((tile_lat * tile_lon, channels), jnp.float32)
    weight_parts = []
    for a in range(3):
        for b in range(3):
            shifted = grid_padded[2 - a : 2 - a + tile_lat, 2 - b : 2 - b + tile_lon].reshape(
                -1, channels
            )
            input_grad = input_grad + lax.dot_general(
                shifted,
                conv_weight[a, b],
                (((1,), (1,)), ((), ())),
                preferred_element_type=jnp.float32,
            )
            window = input_padded[a : a + tile_lat, b : b + tile_lon].reshape(-1, channels)
            weight_parts.append(
                lax.dot_general(
                    window, flat_grad, (((0,), (0,)), ((), ())), preferred_element_type=jnp.float32
                )
            )
    weight_grad = lax.psum(
        jnp.stack(weight_parts).reshape(3, 3, channels, channels), ("lat", "lon")
    )
    return (input_grad.reshape(tile_lat, tile_lon, channels).astype(jnp.bfloat16), weight_grad)


def solution(mesh):
    placed = (
        P(("lat", "lon"), None),
        P(("lat", "lon"), None),
        P(("lat", "lon")),
        P(("lat", "lon")),
        P(("lat", "lon"), None),
        P(("lat", "lon")),
        P("lat", "lon", None),
        P(),
    )
    return jax.shard_map(
        shards, mesh=mesh, in_specs=placed, out_specs=(P("lat", "lon", None), P()), check_vma=False
    )
```

profile of v0, /device:TPU:1, one launch (start us, length us, event | category | flops | bytes accessed | tf_op | source)
XLA Modules:
  0.0 357.4 jit_solution(9674923736870181824)
XLA Ops:
  8.0 4.5 %collective-permute-start.5 = (bf16[1,128,128]{2,1,0:T(8,128)(2,1)S(1)}, bf16[1,128,128]{2,1,0:T(8,128)(2,1)S(1)}, u32[]{:S(2)}, u32[]{:S(2)}) collective-permute-start(bf16[1,128,128]{2,1,0:T(8,128)(2,1)S(1)} %get-tuple-element.168), channel_id=1, source_target_pairs={{16,0},{32,16},{48,32},{64,48},{80,64},{96,80},{112,96},{0,112},{1... | collective-permute-start | bytes 98312 | tf_op jit(solution)/shard_map/ppermute | solution.py:21
  17.3 3.3 scatter_custom_fusion
  22.2 11.0 %all-to-all-start = ((bf16[128,1,1,16,4]{3,4,2,1,0:T(4,128)(2,1)}), bf16[128,1,1,16,4]{3,4,2,1,0:T(4,128)(2,1)S(1)}, u32[]{:S(2)}, u32[]{:S(2)}) async-start(bf16[128,1,1,16,4]{3,4,2,1,0:T(4,128)(2,1)} %copy.87), calls=%async_computation | async-start | bytes 262144 | tf_op jit(solution)/shard_map/all_to_all | solution.py:45
  33.2 4.3 %scatter_custom_fusion.1 = bf16[2048,128]{1,0:T(8,128)(2,1)} fusion(s32[1024]{0:T(1024)S(1)} %bitcast.226, bf16[1024,128]{1,0:T(8,128)(2,1)} %param.18, bf16[]{:T(256)} %constant.168.clone.1), kind=kCustom, calls=%fused_computation.87 | custom fusion | bytes 524800 | tf_op jit(solution)/shard_map/scatter | solution.py:99
  37.5 5.6 %all-to-all-done = bf16[128,1,1,16,4]{3,4,2,1,0:T(4,128)(2,1)S(1)} async-done(((bf16[128,1,1,16,4]{3,4,2,1,0:T(4,128)(2,1)}), bf16[128,1,1,16,4]{3,4,2,1,0:T(4,128)(2,1)S(1)}, u32[]{:S(2)}, u32[]{:S(2)}) %all-to-all-start) | async-done | bytes 16416 | tf_op jit(solution)/shard_map/all_to_all | solution.py:45
  43.1 4.2 %all-to-all-start.1 = ((bf16[128,1,1,16,128]{4,3,2,1,0:T(8,128)(2,1)}), bf16[128,1,1,16,128]{4,3,2,1,0:T(8,128)(2,1)S(1)}, u32[]{:S(2)}, u32[]{:S(2)}) async-start(bf16[128,1,1,16,128]{4,3,2,1,0:T(8,128)(2,1)} %bitcast.13), calls=%async_computation.1 | async-start | bytes 1048576 | tf_op jit(solution)/shard_map/all_to_all | solution.py:45
  50.0 3.2 collective-permute-start.6
  53.2 8.2 %all-to-all-done.1 = bf16[128,1,1,16,128]{4,3,2,1,0:T(8,128)(2,1)S(1)} async-done(((bf16[128,1,1,16,128]{4,3,2,1,0:T(8,128)(2,1)}), bf16[128,1,1,16,128]{4,3,2,1,0:T(8,128)(2,1)S(1)}, u32[]{:S(2)}, u32[]{:S(2)}) %all-to-all-start.1) | async-done | bytes 524320 | tf_op jit(solution)/shard_map/all_to_all | solution.py:45
  61.4 91.8 %while.17 = (s32[]{:T(128)}, f32[72,17408]{1,0:T(8,128)}, f32[8,256,4]{1,2,0:T(4,128)S(1)}, bf16[8,256,128]{2,1,0:T(8,128)(2,1)S(1)}, s32[]{:T(128)}, /*index=5*/s32[]{:T(128)}) while((s32[]{:T(128)}, f32[72,17408]{1,0:T(8,128)}, f32[8,256,4]{1,2,0:T(4,128)S(1)}, bf16[8,256,128]{2,1,0:T(8,128)(2,1)S(1)}, s32[]{:T(128)}, ...), condition=%wide.region_8.9_spmd.clone, body=%wide.region_5.8_spmd.clone.sunk | while | flops 649949696 | bytes 63582440 | solution.py:152
  61.9 5.2 %broadcast_multiply_fusion.2 = bf16[256,136,128]{2,1,0:T(8,128)(2,1)S(1)} fusion(bf16[256,128]{1,0:T(8,128)(2,1)S(1)} %dynamic-slice_bitcast_fusion.4, bf16[256,136]{1,0:T(8,128)(2,1)S(1)} %copy.129), kind=kLoop, calls=%fused_computation.5.clone.1 | loop fusion | flops 4456448 | bytes 9048064 | tf_op jit(solution)/shard_map/while/body/eval_jaxpr/mul | solution.py:144
  67.1 3.6 convolution_add_fusion.10
  73.4 5.2 %broadcast_multiply_fusion.2 = bf16[256,136,128]{2,1,0:T(8,128)(2,1)S(1)} fusion(bf16[256,128]{1,0:T(8,128)(2,1)S(1)} %dynamic-slice_bitcast_fusion.4, bf16[256,136]{1,0:T(8,128)(2,1)S(1)} %copy.129), kind=kLoop, calls=%fused_computation.5.clone.1 | loop fusion | flops 4456448 | bytes 9048064 | tf_op jit(solution)/shard_map/while/body/eval_jaxpr/mul | solution.py:144
  78.6 3.6 convolution_add_fusion.10
  84.8 5.2 %broadcast_multiply_fusion.2 = bf16[256,136,128]{2,1,0:T(8,128)(2,1)S(1)} fusion(bf16[256,128]{1,0:T(8,128)(2,1)S(1)} %dynamic-slice_bitcast_fusion.4, bf16[256,136]{1,0:T(8,128)(2,1)S(1)} %copy.129), kind=kLoop, calls=%fused_computation.5.clone.1 | loop fusion | flops 4456448 | bytes 9048064 | tf_op jit(solution)/shard_map/while/body/eval_jaxpr/mul | solution.py:144
  90.1 3.6 convolution_add_fusion.10
  96.3 5.2 %broadcast_multiply_fusion.2 = bf16[256,136,128]{2,1,0:T(8,128)(2,1)S(1)} fusion(bf16[256,128]{1,0:T(8,128)(2,1)S(1)} %dynamic-slice_bitcast_fusion.4, bf16[256,136]{1,0:T(8,128)(2,1)S(1)} %copy.129), kind=kLoop, calls=%fused_computation.5.clone.1 | loop fusion | flops 4456448 | bytes 9048064 | tf_op jit(solution)/shard_map/while/body/eval_jaxpr/mul | solution.py:144
  101.5 3.6 convolution_add_fusion.10
  107.8 5.2 %broadcast_multiply_fusion.2 = bf16[256,136,128]{2,1,0:T(8,128)(2,1)S(1)} fusion(bf16[256,128]{1,0:T(8,128)(2,1)S(1)} %dynamic-slice_bitcast_fusion.4, bf16[256,136]{1,0:T(8,128)(2,1)S(1)} %copy.129), kind=kLoop, calls=%fused_computation.5.clone.1 | loop fusion | flops 4456448 | bytes 9048064 | tf_op jit(solution)/shard_map/while/body/eval_jaxpr/mul | solution.py:144
  113.0 3.6 convolution_add_fusion.10
  119.3 5.2 %broadcast_multiply_fusion.2 = bf16[256,136,128]{2,1,0:T(8,128)(2,1)S(1)} fusion(bf16[256,128]{1,0:T(8,128)(2,1)S(1)} %dynamic-slice_bitcast_fusion.4, bf16[256,136]{1,0:T(8,128)(2,1)S(1)} %copy.129), kind=kLoop, calls=%fused_computation.5.clone.1 | loop fusion | flops 4456448 | bytes 9048064 | tf_op jit(solution)/shard_map/while/body/eval_jaxpr/mul | solution.py:144
  124.5 3.6 convolution_add_fusion.10
  130.8 5.2 %broadcast_multiply_fusion.2 = bf16[256,136,128]{2,1,0:T(8,128)(2,1)S(1)} fusion(bf16[256,128]{1,0:T(8,128)(2,1)S(1)} %dynamic-slice_bitcast_fusion.4, bf16[256,136]{1,0:T(8,128)(2,1)S(1)} %copy.129), kind=kLoop, calls=%fused_computation.5.clone.1 | loop fusion | flops 4456448 | bytes 9048064 | tf_op jit(solution)/shard_map/while/body/eval_jaxpr/mul | solution.py:144
  136.0 3.6 convolution_add_fusion.10
  142.2 5.2 %broadcast_multiply_fusion.2 = bf16[256,136,128]{2,1,0:T(8,128)(2,1)S(1)} fusion(bf16[256,128]{1,0:T(8,128)(2,1)S(1)} %dynamic-slice_bitcast_fusion.4, bf16[256,136]{1,0:T(8,128)(2,1)S(1)} %copy.129), kind=kLoop, calls=%fused_computation.5.clone.1 | loop fusion | flops 4456448 | bytes 9048064 | tf_op jit(solution)/shard_map/while/body/eval_jaxpr/mul | solution.py:144
  147.4 3.6 convolution_add_fusion.10
  154.6 2.8 convert.27
  161.1 4.0 %collective-permute-start = (bf16[5,136,128]{2,1,0:T(8,128)(2,1)S(1)}, bf16[5,136,128]{2,1,0:T(8,128)(2,1)S(1)}, u32[]{:S(2)}, u32[]{:S(2)}) collective-permute-start(bf16[5,136,128]{2,1,0:T(8,128)(2,1)S(1)} %bitcast.203), channel_id=1, source_target_pairs={{0,16},{16,32},{32,48},{48,64},{64,80},{80,96},{96,112},{1,17},{17... | collective-permute-start | bytes 522248 | tf_op jit(solution)/shard_map/ppermute | solution.py:19
  172.8 4.2 %collective-permute-done.3 = bf16[66,5,128]{2,1,0:T(8,128)(2,1)S(1)} collective-permute-done((bf16[66,5,128]{2,1,0:T(8,128)(2,1)S(1)}, bf16[66,5,128]{2,1,0:T(8,128)(2,1)S(1)}, u32[]{:S(2)}, u32[]{:S(2)}) %collective-permute-start.3) | collective-permute-done | bytes 84512 | tf_op jit(solution)/shard_map/ppermute | solution.py:21
  178.0 3.1 maximum_select_fusion.1
  181.1 7.0 %fusion.129 = (bf16[64,128,128]{2,1,0:T(8,128)(2,1)}, bf16[64,128,128]{2,1,0:T(8,128)(2,1)S(1)}, bf16[64,128,128]{2,1,0:T(8,128)(2,1)}, bf16[64,128,128]{2,1,0:T...) fusion(bf16[66,130,128]{2,1,0:T(8,128)(2,1)S(1)} %get-tuple-ele, ...), kind=kLoop, calls=%fused_computation.153 | loop fusion | bytes 37748736 | tf_op jit(solution)/shard_map/slice | solution.py:183
  199.5 2.4 fusion.107
  214.3 134.3 %all-reduce.2.cloned.1.call-done = f32[3,3,128,128]{3,2,1,0:T(8,128)} async-done(((f32[3,3,128,128]{3,2,1,0:T(8,128)}), f32[3,3,128,128]{3,2,1,0:T(8,128)}) %all-reduce.2.cloned.1.call-update) | async-done | bytes 589840 | tf_op jit(solution)/shard_map/psum | solution.py:198
  (237 shorter events, 69.3 us)
Async XLA Ops:
  7.2 9.6 %copy-start.11 = (s32[1024,1]{0,1:T(1,128)S(1)}, s32[1024,1]{0,1:T(1,128)}, u32[]{:S(2)}) copy-start(s32[1024,1]{0,1:T(1,128)} %param.19) | copy-start | bytes 12292
  8.0 41.9 %collective-permute-start.5 = (bf16[1,128,128]{2,1,0:T(8,128)(2,1)S(1)}, bf16[1,128,128]{2,1,0:T(8,128)(2,1)S(1)}, u32[]{:S(2)}, u32[]{:S(2)}) collective-permute-start(bf16[1,128,128]{2,1,0:T(8,128)(2,1)S(1)} %get-tuple-element.168), channel_id=1, source_target_pairs={{16,0},{32,16},{48,32},{64,48},{80,64},{96,80},{112,96},{0,112},{1... | collective-permute-start | bytes 98312 | tf_op jit(solution)/shard_map/ppermute | solution.py:21
  12.5 35.4 %collective-permute-start.4 = (bf16[1,128,128]{2,1,0:T(8,128)(2,1)S(1)}, bf16[1,128,128]{2,1,0:T(8,128)(2,1)S(1)}, u32[]{:S(2)}, u32[]{:S(2)}) collective-permute-start(bf16[1,128,128]{2,1,0:T(8,128)(2,1)S(1)} %get-tuple-element.169), channel_id=1, source_target_pairs={{0,16},{16,32},{32,48},{48,64},{64,80},{80,96},{96,112},{112,0},{1... | collective-permute-start | bytes 98312 | tf_op jit(solution)/shard_map/ppermute | solution.py:19
  22.2 20.9 %all-to-all-start = ((bf16[128,1,1,16,4]{3,4,2,1,0:T(4,128)(2,1)}), bf16[128,1,1,16,4]{3,4,2,1,0:T(4,128)(2,1)S(1)}, u32[]{:S(2)}, u32[]{:S(2)}) async-start(bf16[128,1,1,16,4]{3,4,2,1,0:T(4,128)(2,1)} %copy.87), calls=%async_computation | async-start | bytes 262144 | tf_op jit(solution)/shard_map/all_to_all | solution.py:45
  43.1 18.3 %all-to-all-start.1 = ((bf16[128,1,1,16,128]{4,3,2,1,0:T(8,128)(2,1)}), bf16[128,1,1,16,128]{4,3,2,1,0:T(8,128)(2,1)S(1)}, u32[]{:S(2)}, u32[]{:S(2)}) async-start(bf16[128,1,1,16,128]{4,3,2,1,0:T(8,128)(2,1)} %bitcast.13), calls=%async_computation.1 | async-start | bytes 1048576 | tf_op jit(solution)/shard_map/all_to_all | solution.py:45
  47.3 301.3 %all-reduce.2.cloned.1.call-start = ((), (), s32[]{:S(2)}) async-start(), calls=%async_computation.2 | async-start | bytes 1179648 | tf_op jit(solution)/shard_map/psum | solution.py:198
  50.0 128.0 %collective-permute-start.6 = (bf16[66,1,128]{2,1,0:T(2,128)(2,1)S(1)}, bf16[66,1,128]{2,1,0:T(2,128)(2,1)S(1)}, u32[]{:S(2)}, u32[]{:S(2)}) collective-permute-start(bf16[66,1,128]{2,1,0:T(2,128)(2,1)S(1)} %get-tuple-element.166), channel_id=1, source_target_pairs={{0,1},{1,2},{2,3},{3,4},{4,5},{5,6},{6,7},{7,8},{8,9},{9,10},{10,1... | collective-permute-start | bytes 50696 | tf_op jit(solution)/shard_map/ppermute | solution.py:19
  53.2 124.8 %collective-permute-start.7 = (bf16[66,1,128]{2,1,0:T(2,128)(2,1)S(1)}, bf16[66,1,128]{2,1,0:T(2,128)(2,1)S(1)}, u32[]{:S(2)}, u32[]{:S(2)}) collective-permute-start(bf16[66,1,128]{2,1,0:T(2,128)(2,1)S(1)} %get-tuple-element.167), channel_id=1, source_target_pairs={{1,0},{2,1},{3,2},{4,3},{5,4},{6,5},{7,6},{8,7},{9,8},{10,9},{11,1... | collective-permute-start | bytes 50696 | tf_op jit(solution)/shard_map/ppermute | solution.py:21
  61.8 5.2 %slice-start = ((s8[5013504]{0:T(1024)(128)(4,1)}), s8[4194304]{0:T(1024)(128)(4,1)S(1)}, s32[]{:S(2)}) async-start(s8[5013504]{0:T(1024)(128)(4,1)} %bitcast.191), calls=%async_computation.3 | async-start | bytes 8388608 | tf_op jit(solution)/shard_map/while
  61.9 5.2 %slice-start.1 = ((s8[5013504]{0:T(1024)(128)(4,1)}), s8[819200]{0:T(1024)(128)(4,1)S(1)}, s32[]{:S(2)}) async-start(s8[5013504]{0:T(1024)(128)(4,1)} %bitcast.191), calls=%async_computation.4 | async-start | bytes 1638400 | tf_op jit(solution)/shard_map/while
  73.3 5.2 %slice-start = ((s8[5013504]{0:T(1024)(128)(4,1)}), s8[4194304]{0:T(1024)(128)(4,1)S(1)}, s32[]{:S(2)}) async-start(s8[5013504]{0:T(1024)(128)(4,1)} %bitcast.191), calls=%async_computation.3 | async-start | bytes 8388608 | tf_op jit(solution)/shard_map/while
  73.4 5.2 %slice-start.1 = ((s8[5013504]{0:T(1024)(128)(4,1)}), s8[819200]{0:T(1024)(128)(4,1)S(1)}, s32[]{:S(2)}) async-start(s8[5013504]{0:T(1024)(128)(4,1)} %bitcast.191), calls=%async_computation.4 | async-start | bytes 1638400 | tf_op jit(solution)/shard_map/while
  82.1 2.2 copy-start
  84.8 5.2 %slice-start = ((s8[5013504]{0:T(1024)(128)(4,1)}), s8[4194304]{0:T(1024)(128)(4,1)S(1)}, s32[]{:S(2)}) async-start(s8[5013504]{0:T(1024)(128)(4,1)} %bitcast.191), calls=%async_computation.3 | async-start | bytes 8388608 | tf_op jit(solution)/shard_map/while
  84.8 5.2 %slice-start.1 = ((s8[5013504]{0:T(1024)(128)(4,1)}), s8[819200]{0:T(1024)(128)(4,1)S(1)}, s32[]{:S(2)}) async-start(s8[5013504]{0:T(1024)(128)(4,1)} %bitcast.191), calls=%async_computation.4 | async-start | bytes 1638400 | tf_op jit(solution)/shard_map/while
  96.3 5.2 %slice-start = ((s8[5013504]{0:T(1024)(128)(4,1)}), s8[4194304]{0:T(1024)(128)(4,1)S(1)}, s32[]{:S(2)}) async-start(s8[5013504]{0:T(1024)(128)(4,1)} %bitcast.191), calls=%async_computation.3 | async-start | bytes 8388608 | tf_op jit(solution)/shard_map/while
  96.3 5.2 %slice-start.1 = ((s8[5013504]{0:T(1024)(128)(4,1)}), s8[819200]{0:T(1024)(128)(4,1)S(1)}, s32[]{:S(2)}) async-start(s8[5013504]{0:T(1024)(128)(4,1)} %bitcast.191), calls=%async_computation.4 | async-start | bytes 1638400 | tf_op jit(solution)/shard_map/while
  107.8 5.2 %slice-start = ((s8[5013504]{0:T(1024)(128)(4,1)}), s8[4194304]{0:T(1024)(128)(4,1)S(1)}, s32[]{:S(2)}) async-start(s8[5013504]{0:T(1024)(128)(4,1)} %bitcast.191), calls=%async_computation.3 | async-start | bytes 8388608 | tf_op jit(solution)/shard_map/while
  107.8 5.2 %slice-start.1 = ((s8[5013504]{0:T(1024)(128)(4,1)}), s8[819200]{0:T(1024)(128)(4,1)S(1)}, s32[]{:S(2)}) async-start(s8[5013504]{0:T(1024)(128)(4,1)} %bitcast.191), calls=%async_computation.4 | async-start | bytes 1638400 | tf_op jit(solution)/shard_map/while
  119.2 5.2 %slice-start = ((s8[5013504]{0:T(1024)(128)(4,1)}), s8[4194304]{0:T(1024)(128)(4,1)S(1)}, s32[]{:S(2)}) async-start(s8[5013504]{0:T(1024)(128)(4,1)} %bitcast.191), calls=%async_computation.3 | async-start | bytes 8388608 | tf_op jit(solution)/shard_map/while
  119.3 5.2 %slice-start.1 = ((s8[5013504]{0:T(1024)(128)(4,1)}), s8[819200]{0:T(1024)(128)(4,1)S(1)}, s32[]{:S(2)}) async-start(s8[5013504]{0:T(1024)(128)(4,1)} %bitcast.191), calls=%async_computation.4 | async-start | bytes 1638400 | tf_op jit(solution)/shard_map/while
  128.1 2.2 copy-start
  130.7 5.2 %slice-start = ((s8[5013504]{0:T(1024)(128)(4,1)}), s8[4194304]{0:T(1024)(128)(4,1)S(1)}, s32[]{:S(2)}) async-start(s8[5013504]{0:T(1024)(128)(4,1)} %bitcast.191), calls=%async_computation.3 | async-start | bytes 8388608 | tf_op jit(solution)/shard_map/while
  130.7 5.2 %slice-start.1 = ((s8[5013504]{0:T(1024)(128)(4,1)}), s8[819200]{0:T(1024)(128)(4,1)S(1)}, s32[]{:S(2)}) async-start(s8[5013504]{0:T(1024)(128)(4,1)} %bitcast.191), calls=%async_computation.4 | async-start | bytes 1638400 | tf_op jit(solution)/shard_map/while
  142.2 5.2 %slice-start = ((s8[5013504]{0:T(1024)(128)(4,1)}), s8[4194304]{0:T(1024)(128)(4,1)S(1)}, s32[]{:S(2)}) async-start(s8[5013504]{0:T(1024)(128)(4,1)} %bitcast.191), calls=%async_computation.3 | async-start | bytes 8388608 | tf_op jit(solution)/shard_map/while
  142.2 5.2 %slice-start.1 = ((s8[5013504]{0:T(1024)(128)(4,1)}), s8[819200]{0:T(1024)(128)(4,1)S(1)}, s32[]{:S(2)}) async-start(s8[5013504]{0:T(1024)(128)(4,1)} %bitcast.191), calls=%async_computation.4 | async-start | bytes 1638400 | tf_op jit(solution)/shard_map/while
  154.6 3.9 %copy-start.1 = (f32[72,17408]{1,0:T(8,128)S(1)}, f32[72,17408]{1,0:T(8,128)}, u32[]{:S(2)}) copy-start(f32[72,17408]{1,0:T(8,128)} %get-tuple-element.103) | copy-start | bytes 15040516
  159.8 7.7 %collective-permute-start.1 = (bf16[5,136,128]{2,1,0:T(8,128)(2,1)S(1)}, bf16[5,136,128]{2,1,0:T(8,128)(2,1)S(1)}, u32[]{:S(2)}, u32[]{:S(2)}) collective-permute-start(bf16[5,136,128]{2,1,0:T(8,128)(2,1)S(1)} %bitcast.207), channel_id=1, source_target_pairs={{16,0},{32,16},{48,32},{64,48},{80,64},{96,80},{112,96},{17,1},{33... | collective-permute-start | bytes 522248 | tf_op jit(solution)/shard_map/ppermute | solution.py:21
  161.1 7.2 %collective-permute-start = (bf16[5,136,128]{2,1,0:T(8,128)(2,1)S(1)}, bf16[5,136,128]{2,1,0:T(8,128)(2,1)S(1)}, u32[]{:S(2)}, u32[]{:S(2)}) collective-permute-start(bf16[5,136,128]{2,1,0:T(8,128)(2,1)S(1)} %bitcast.203), channel_id=1, source_target_pairs={{0,16},{16,32},{32,48},{48,64},{64,80},{80,96},{96,112},{1,17},{17... | collective-permute-start | bytes 522248 | tf_op jit(solution)/shard_map/ppermute | solution.py:19
  168.8 3.9 %collective-permute-start.2 = (bf16[66,5,128]{2,1,0:T(8,128)(2,1)S(1)}, bf16[66,5,128]{2,1,0:T(8,128)(2,1)S(1)}, u32[]{:S(2)}, u32[]{:S(2)}) collective-permute-start(bf16[66,5,128]{2,1,0:T(8,128)(2,1)S(1)} %get-tuple-element.164), channel_id=1, source_target_pairs={{0,1},{1,2},{2,3},{3,4},{4,5},{5,6},{6,7},{7,8},{8,9},{9,10},{10,1... | collective-permute-start | bytes 253448 | tf_op jit(solution)/shard_map/ppermute | solution.py:19
  170.8 6.2 %collective-permute-start.3 = (bf16[66,5,128]{2,1,0:T(8,128)(2,1)S(1)}, bf16[66,5,128]{2,1,0:T(8,128)(2,1)S(1)}, u32[]{:S(2)}, u32[]{:S(2)}) collective-permute-start(bf16[66,5,128]{2,1,0:T(8,128)(2,1)S(1)} %get-tuple-element.165), channel_id=1, source_target_pairs={{1,0},{2,1},{3,2},{4,3},{5,4},{6,5},{7,6},{8,7},{9,8},{10,9},{11,1... | collective-permute-start | bytes 253448 | tf_op jit(solution)/shard_map/ppermute | solution.py:21
  199.5 2.5 copy-start.7
  (14 other events, 26.0 us)
Sparse Core Ops, SparseCore 0:
  199.6 148.9 all-reduce.1
where the time goes:
time: 358 us; the launch traced here: 357 us
  waiting for transfers between devices  157 us (44%)
  other arithmetic  54.3 us (15%)
  local copies, waits for them, and re-layouts  51.6 us (14%)
  matrix products  48.7 us (14%)
  starting transfers between devices  30.1 us (8%)
  between operations  15.2 us (4%)
    psum x1, waiting for transfers between devices, shards(): lax.psum(jnp.stack(weight_parts).reshape(3, 3, channels, channels), ('lat...  134 us
    mul x8, other arithmetic, accumulate(): lon_matrix[:, :, None] * rows_blk[:, None, :]  41.4 us
    dot_general x8, matrix products, accumulate(): lax.dot_general(lat_matrix, spread, (((0,), (0,)), ((), ())), preferred_e...  28.5 us
    while x48, local copies, waits for them, and re-layouts  17.9 us
    all_to_all x2, starting transfers between devices, one_exchange(): parts = lax.all_to_all(parts, axis, split_axis=0, concat_axis=0, tiled=True)  15.1 us
    all_to_all x2, waiting for transfers between devices, one_exchange(): parts = lax.all_to_all(parts, axis, split_axis=0, concat_axis=0, tiled=True)  13.8 us
    unnamed x33, local copies, waits for them, and re-layouts  12.4 us
    dot_general x9, matrix products, shards(): lax.dot_general(window, flat_grad, (((0,), (0,)), ((), ())), preferred_el...  10.5 us
  transfers between devices with their start and end apart: 11, of which 7 were waited for; matrix products, arithmetic and copies ran while one was open for 30% of the time, Pallas kernels for 0%

commit v1 on v0

v1 whole, which is shorter than its diff:
```python
import functools

import jax
import jax.numpy as jnp
from jax import lax
from jax.experimental import pallas as pl
from jax.experimental.pallas import tpu as pltpu
from jax.sharding import PartitionSpec as P

AXES = ("lat", "lon")
BF16 = jnp.bfloat16
F32 = jnp.float32
SLOTS = 16
CHUNK = 24
TILES = 128
GAUSS = 2.0 * 1.5 * 1.5


def nt(lhs, rhs):
    return lax.dot_general(lhs, rhs, (((1,), (1,)), ((), ())), preferred_element_type=F32)


def mm(lhs, rhs):
    return jnp.dot(lhs, rhs, preferred_element_type=F32)


def pack_kernel(live_ref, own_ref, lat_ref, lon_ref, pos_ref, rows_ref, out_ref):
    count = own_ref.shape[1]
    lane = lax.broadcasted_iota(jnp.int32, (1, count), 1)
    own = jnp.where(lane < live_ref[0], own_ref[...], TILES)
    tile_line = lax.broadcasted_iota(jnp.int32, (TILES, count), 0)
    named = jnp.where(own == tile_line, 1.0, 0.0)
    named_b = named.astype(BF16)
    block = 256
    upper = jnp.where(
        lax.broadcasted_iota(jnp.int32, (block, block), 0)
        < lax.broadcasted_iota(jnp.int32, (block, block), 1),
        1.0,
        0.0,
    ).astype(BF16)
    ones = jnp.ones((block, block), BF16)
    before = jnp.zeros((TILES, block), F32)
    ranks = []
    for b in range(count // block):
        part = named_b[:, b * block : (b + 1) * block]
        earlier = mm(part, upper) + before
        ranks.append(
            jnp.sum(earlier * named[:, b * block : (b + 1) * block], axis=0, keepdims=True)
        )
        before = before + mm(part, ones)
    rank = jnp.concatenate(ranks, axis=1).astype(jnp.int32)
    slot = own * SLOTS + rank
    rows = rows_ref[...]
    step = 1024
    for q in range(TILES * SLOTS // step):
        line = lax.broadcasted_iota(jnp.int32, (step, count), 0) + q * step
        picked = jnp.where(slot == line, 1.0, 0.0).astype(BF16)
        moved = mm(picked, rows).astype(BF16)
        out_ref[q * step // SLOTS : (q + 1) * step // SLOTS, 0:SLOTS, :] = moved.reshape(
            step // SLOTS, SLOTS, 128
        )
    at_rank = lax.broadcasted_iota(jnp.int32, (SLOTS, count), 0) == rank
    pos = pos_ref[...].astype(F32)
    fields = (
        lat_ref[...].astype(F32),
        lon_ref[...].astype(F32),
        pos[0:1, :],
        pos[1:2, :],
    )
    spots = [jnp.where(at_rank, f, 0.0) for f in fields]
    spots.append(jnp.zeros((128 - SLOTS * len(fields), count), F32))
    cells = nt(named_b, jnp.concatenate(spots, axis=0).astype(BF16)).astype(BF16)
    out_ref[:, SLOTS:CHUNK, :] = jnp.broadcast_to(
        cells.astype(F32)[:, None, :], (TILES, CHUNK - SLOTS, 128)
    ).astype(BF16)


def pack(live, own, lat, lon, pos, rows):
    vmem = pl.BlockSpec(memory_space=pltpu.VMEM)
    return pl.pallas_call(
        pack_kernel,
        out_shape=jax.ShapeDtypeStruct((TILES, CHUNK, 128), BF16),
        in_specs=[pl.BlockSpec(memory_space=pltpu.SMEM)] + [vmem] * 5,
        out_specs=vmem,
        cost_estimate=pl.CostEstimate(flops=700_000_000, bytes_accessed=1_500_000, transcendentals=0),
        name="pack",
    )(live, own, lat, lon, pos, rows)


def tap_weights(cell, frac, offset):
    tap = offset - cell + 3.0
    dist = tap - 3.0 - frac
    weight = jnp.exp(-(dist * dist) / GAUSS)
    return jnp.where((tap >= 0.0) & (tap <= 7.0), weight, 0.0)


def scatter_kernel(edge_ref, in_ref, canvas_ref, rows_ref, lat_w, lon_w, side_w):
    total = TILES * SLOTS
    rows_ref[...] = in_ref[:, 0:SLOTS, :].reshape(total, 128)
    tail = in_ref[:, SLOTS:CHUNK, :].reshape(TILES * (CHUNK - SLOTS), 128)
    first = jnp.where(
        lax.broadcasted_iota(jnp.int32, (TILES, tail.shape[0]), 1)
        == (CHUNK - SLOTS) * lax.broadcasted_iota(jnp.int32, (TILES, tail.shape[0]), 0),
        1.0,
        0.0,
    ).astype(BF16)
    cells = mm(first, tail)
    cells_t = cells.T.astype(BF16)[: 4 * SLOTS]
    slot_lane = lax.broadcasted_iota(jnp.int32, (TILES, total), 1)
    spread = jnp.where(
        (slot_lane // SLOTS) == lax.broadcasted_iota(jnp.int32, (TILES, total), 0), 1.0, 0.0
    ).astype(BF16)
    wide = mm(cells_t, spread)
    own_slot = (
        lax.broadcasted_iota(jnp.int32, (SLOTS, total), 1) % SLOTS
        == lax.broadcasted_iota(jnp.int32, (SLOTS, total), 0)
    )
    cell_lat, cell_lon, frac_lat, frac_lon = [
        jnp.sum(
            jnp.where(own_slot, wide[f * SLOTS : (f + 1) * SLOTS], 0.0), axis=0, keepdims=True
        )
        for f in range(4)
    ]
    line = lax.broadcasted_iota(jnp.int32, (72, total), 0)
    kept = (line >= edge_ref[0]) & (line < edge_ref[1])
    lat_w[...] = jnp.where(
        kept, tap_weights(cell_lat, frac_lat, line.astype(F32) - 4.0), 0.0
    )
    column = lax.broadcasted_iota(jnp.int32, (128, total), 0).astype(F32)
    lon_w[...] = tap_weights(cell_lon, frac_lon, column).astype(BF16)
    line8 = lax.broadcasted_iota(jnp.int32, (8, total), 0)
    column = jnp.where(line8 < 4, line8 - 4, line8 + 124).astype(F32)
    side_w[...] = tap_weights(cell_lon, frac_lon, column).astype(BF16).astype(F32)

    def eight_lines(step, carry):
        start = pl.multiple_of(step * 8, 8)
        lat8 = lat_w[pl.ds(start, 8), :]
        acc = jnp.zeros((8 * 128, 128), F32)
        side = jnp.zeros((8 * 8, 128), F32)
        for k in range(total // 256):
            cols = slice(k * 256, (k + 1) * 256)
            lon = lon_w[:, cols].reshape(8, 16, 256)
            parts = []
            side_parts = []
            side_lon = side_w[:, cols]
            for i in range(8):
                one = jnp.broadcast_to(lat8[i : i + 1, cols], (16, 256)).astype(BF16)
                parts.append((lon * one[None]).reshape(128, 256))
                one8 = jnp.broadcast_to(
                    lat8[i : i + 1, cols].astype(BF16).astype(F32), (8, 256)
                )
                side_parts.append(side_lon * one8)
            rows = rows_ref[cols, :]
            acc = acc + mm(jnp.concatenate(parts, axis=0), rows)
            side = side + mm(jnp.concatenate(side_parts, axis=0).astype(BF16), rows)
        canvas_ref[pl.ds(start, 8), 0:128, :] = acc.astype(BF16).reshape(8, 128, 128)
        canvas_ref[pl.ds(start, 8), 128:136, :] = side.reshape(8, 8, 128).astype(BF16)
        return carry

    lax.fori_loop(0, 9, eight_lines, 0)


def scatter(edge, incoming):
    vmem = pl.BlockSpec(memory_space=pltpu.VMEM)
    total = TILES * SLOTS
    return pl.pallas_call(
        scatter_kernel,
        out_shape=jax.ShapeDtypeStruct((72, 136, 128), BF16),
        in_specs=[pl.BlockSpec(memory_space=pltpu.SMEM), vmem],
        out_specs=vmem,
        scratch_shapes=[
            pltpu.VMEM((total, 128), BF16),
            pltpu.VMEM((72, total), F32),
            pltpu.VMEM((128, total), BF16),
            pltpu.VMEM((8, total), F32),
        ],
        compiler_params=pltpu.CompilerParams(vmem_limit_bytes=40 << 20),
        cost_estimate=pl.CostEstimate(
            flops=5_200_000_000, bytes_accessed=3_500_000, transcendentals=500_000
        ),
        name="scatter",
    )(edge, incoming)


def padded_2(cells, sides, width, closed):
    for axis, dim in sides:
        count = lax.axis_size(axis)
        ends = count if closed else count - 1
        head = lax.slice_in_dim(cells, 0, width, axis=dim)
        tail = lax.slice_in_dim(cells, cells.shape[dim] - width, cells.shape[dim], axis=dim)
        cells = jnp.concatenate(
            [
                lax.ppermute(tail, axis, [(i, (i + 1) % count) for i in range(ends)]),
                cells,
                lax.ppermute(head, axis, [((i + 1) % count, i) for i in range(ends)]),
            ],
            axis=dim,
        )
    return cells


def clear_rim(padded):
    lat_index = lax.axis_index("lat")
    lat_count = lax.axis_size("lat")
    row_line = jnp.arange(padded.shape[0], dtype=jnp.int32)
    masked = (row_line == 0) & (lat_index == 0) | (row_line == padded.shape[0] - 1) & (
        lat_index == lat_count - 1
    )
    return jnp.where(masked[:, None, None], jnp.zeros_like(padded), padded)


def total_sum(parts):
    padded = jnp.pad(parts.astype(BF16), ((0, TILES * 16 - parts.shape[0]), (0, 0)))
    got = lax.all_to_all(padded.reshape(TILES, 16, 128), AXES, 0, 0, tiled=True)
    mine = jnp.sum(got.astype(F32), axis=0).astype(BF16)
    every = jnp.broadcast_to(mine[None], (TILES, 16, 128))
    every = lax.all_to_all(every, AXES, 0, 0, tiled=True)
    return every.reshape(TILES * 16, 128)[: parts.shape[0]].astype(F32)


def shards(grad_rows, owner, lat_offset, lon_offset, position, live_count, features, conv_weight):
    channels = grad_rows.shape[1]
    tile_lat = features.shape[0]
    tile_lon = features.shape[1]
    input_padded = clear_rim(padded_2(features, (("lat", 0), ("lon", 1)), 1, True))
    count = grad_rows.shape[0]
    outgoing = pack(
        live_count,
        owner.reshape(1, count),
        lat_offset.reshape(1, count),
        lon_offset.reshape(1, count),
        position.T,
        grad_rows,
    )
    incoming = lax.all_to_all(outgoing, AXES, 0, 0, tiled=True)
    lat_index = lax.axis_index("lat")
    edge = jnp.stack(
        [
            jnp.where(lat_index == 0, 4, 0),
            jnp.where(lat_index == lax.axis_size("lat") - 1, 68, 72),
        ]
    ).astype(jnp.int32)
    canvas = scatter(edge, incoming).astype(F32)
    canvas = jnp.concatenate([canvas[:, 128:132], canvas[:, :128], canvas[:, 132:]], axis=1)
    edge_rows = jnp.concatenate([canvas[:5], canvas[-5:]], axis=0)
    edge_rows = padded_2(edge_rows.astype(jnp.bfloat16), (("lat", 0),), 5, False).astype(
        edge_rows.dtype
    )
    inner = canvas[4:-4]
    inner = inner.at[:4].add(edge_rows[1:5]).at[-4:].add(edge_rows[15:19])
    rim_top = edge_rows[0] + canvas[3]
    rim_bottom = canvas[-4] + edge_rows[19]
    tall = jnp.concatenate([rim_top[None], inner, rim_bottom[None]], axis=0)
    side_cols = jnp.concatenate([tall[:, :5], tall[:, -5:]], axis=1)
    side_cols = padded_2(side_cols.astype(jnp.bfloat16), (("lon", 1),), 5, True).astype(
        side_cols.dtype
    )
    middle = tall[:, 4:-4]
    middle = middle.at[:, :4].add(side_cols[:, 1:5]).at[:, -4:].add(side_cols[:, 15:19])
    rim_left = side_cols[:, 0] + tall[:, 3]
    rim_right = tall[:, -4] + side_cols[:, 19]
    whole = jnp.concatenate([rim_left[:, None], middle, rim_right[:, None]], axis=1)
    grid_padded = clear_rim(whole.astype(jnp.bfloat16))
    grid_grad = grid_padded[1:-1, 1:-1]
    flat_grad = grid_grad.reshape(-1, channels)
    input_grad = jnp.zeros((tile_lat * tile_lon, channels), jnp.float32)
    weight_parts = []
    for a in range(3):
        for b in range(3):
            shifted = grid_padded[2 - a : 2 - a + tile_lat, 2 - b : 2 - b + tile_lon].reshape(
                -1, channels
            )
            input_grad = input_grad + lax.dot_general(
                shifted,
                conv_weight[a, b],
                (((1,), (1,)), ((), ())),
                preferred_element_type=jnp.float32,
            )
            window = input_padded[a : a + tile_lat, b : b + tile_lon].reshape(-1, channels)
            weight_parts.append(
                lax.dot_general(
                    window, flat_grad, (((0,), (0,)), ((), ())), preferred_element_type=jnp.float32
                )
            )
    weight_grad = total_sum(jnp.concatenate(weight_parts, axis=0))
    return (
        input_grad.reshape(tile_lat, tile_lon, channels).astype(jnp.bfloat16),
        weight_grad.reshape(3, 3, channels, channels),
    )


def solution(mesh):
    placed = (
        P(("lat", "lon"), None),
        P(("lat", "lon"), None),
        P(("lat", "lon")),
        P(("lat", "lon")),
        P(("lat", "lon"), None),
        P(("lat", "lon")),
        P("lat", "lon", None),
        P(),
    )
    return jax.shard_map(
        shards, mesh=mesh, in_specs=placed, out_specs=(P("lat", "lon", None), P()), check_vma=False
    )
```

time: 358 us -> 145 us (0.41)
  waiting for transfers between devices: 157 us -> 31 us
  other arithmetic: 54.3 us -> 7.42 us
  local copies, waits for them, and re-layouts: 51.6 us -> 17.6 us
  matrix products: 48.7 us -> 24.3 us
  Pallas kernels: 0 us -> 17.6 us
  starting transfers between devices: 30.1 us -> 45.1 us
  between operations: 15.2 us -> 1.63 us
    psum x1 -> x0, waiting for transfers between devices: 134 us -> none  [shards(): lax.psum(jnp.stack(weight_parts).reshape(3, 3, channels, channels), ('lat...]
    mul x8 -> x0, other arithmetic: 41.4 us -> none  [accumulate(): lon_matrix[:, :, None] * rows_blk[:, None, :]]
    dot_general x8 -> x0, matrix products: 28.5 us -> none  [accumulate(): lax.dot_general(lat_matrix, spread, (((0,), (0,)), ((), ())), preferred_e...]
    while x48 -> x0, local copies, waits for them, and re-layouts: 17.9 us -> none
    pallas_call x0 -> x2, Pallas kernels: none -> 17.6 us  [the longest x1 14.1 us: scatter(): pl.pallas_call(scatter_kernel, out_shape=jax.ShapeDtypeStruct((72, 136, 1...]
    all_to_all x2 -> x3, starting transfers between devices: 15.1 us -> 32 us  [the longest x1 12 us: total_sum(): got = lax.all_to_all(padded.reshape(TILES, 16, 128), AXES, 0, 0, tiled=True)]
    scatter x2 -> x0, local copies, waits for them, and re-layouts: 7.66 us -> none  [the longest x1 4.33 us: shards(): outgoing = jnp.zeros((device_total * capacity, channels), jnp.bfloat16).a...]
    all_to_all x2 -> x3, waiting for transfers between devices: 13.8 us -> 20.9 us  [the longest x1 11.4 us: shards(): incoming = lax.all_to_all(outgoing, AXES, 0, 0, tiled=True)]
  transfers between devices with their start and end apart: 11 -> 11, of which waited for: 7 -> 7; matrix products, arithmetic and copies ran while one was open for 30% -> 14% of each run, Pallas kernels for 0% -> 12%
where the time goes in v1:
time: 145 us
  starting transfers between devices  45.1 us (31%)
  waiting for transfers between devices  31 us (21%)
  matrix products  24.3 us (17%)
  local copies, waits for them, and re-layouts  17.6 us (12%)
  Pallas kernels  17.6 us (12%)
  other arithmetic  7.42 us (5%)
  between operations  1.63 us (1%)
    pallas_call x1, Pallas kernels, scatter(): pl.pallas_call(scatter_kernel, out_shape=jax.ShapeDtypeStruct((72, 136, 1...  14.1 us
    dot_general x9, matrix products, shards(): lax.dot_general(shifted, conv_weight[a, b], (((1,), (1,)), ((), ())), pre...  13.7 us
    all_to_all x1, starting transfers between devices, total_sum(): got = lax.all_to_all(padded.reshape(TILES, 16, 128), AXES, 0, 0, tiled=True)  12 us
    all_to_all x1, waiting for transfers between devices, shards(): incoming = lax.all_to_all(outgoing, AXES, 0, 0, tiled=True)  11.4 us
    all_to_all x1, starting transfers between devices, shards(): incoming = lax.all_to_all(outgoing, AXES, 0, 0, tiled=True)  11 us
    dot_general x9, matrix products, shards(): lax.dot_general(window, flat_grad, (((0,), (0,)), ((), ())), preferred_el...  10.6 us
    all_to_all x1, starting transfers between devices, total_sum(): every = lax.all_to_all(every, AXES, 0, 0, tiled=True)  9.01 us
    all_to_all x1, waiting for transfers between devices, total_sum(): every = lax.all_to_all(every, AXES, 0, 0, tiled=True)  8.76 us
  transfers between devices with their start and end apart: 11, of which 7 were waited for; matrix products, arithmetic and copies ran while one was open for 14% of the time, Pallas kernels for 12%

profile of v1, /device:TPU:1, one launch (start us, length us, event | category | flops | bytes accessed | tf_op | source)
XLA Modules:
  0.0 144.7 jit_solution(16043451070849740526)
XLA Ops:
  1.4 4.5 %collective-permute-start.5 = (bf16[1,128,128]{2,1,0:T(8,128)(2,1)S(1)}, bf16[1,128,128]{2,1,0:T(8,128)(2,1)S(1)}, u32[]{:S(2)}, u32[]{:S(2)}) collective-permute-start(bf16[1,128,128]{2,1,0:T(8,128)(2,1)S(1)} %get-tuple-element.71), channel_id=1, source_target_pairs={{16,0},{32,16},{48,32},{64,48},{80,64},{96,80},{112,96},{0,112},{1... | collective-permute-start | bytes 98312 | tf_op jit(solution)/shard_map/ppermute | solution.py:195
  6.6 3.5 %pack.1 = bf16[128,24,128]{2,1,0:T(8,128)(2,1)} custom-call(s32[1]{0:T(128)S(6)} %copy.42.live_ref, s32[1,1024]{1,0:T(1,128)} %bitcast.120, s32[1,1024]{1,0:T(1,128)} %bitcast.121, s32[1,1024]{1,0:T(1,128)} %bitcast.122, bf16[2,1024]{1,0:T(2,128)(2,1)} %bitcast.123, bf16[1024,128]{1,0:T(8,128)(2,1)} %rows_ref.1), custom_call_target="tpu_custom_call" | custom-call | flops 700000000 | bytes 1500000 | tf_op jit(solution)/shard_map/pack/pallas_call | solution.py:80
  10.0 11.0 %all-to-all-start = ((bf16[128,24,128]{2,1,0:T(8,128)(2,1)}), bf16[128,24,128]{2,1,0:T(8,128)(2,1)S(1)}, u32[]{:S(2)}, u32[]{:S(2)}) async-start(bf16[128,24,128]{2,1,0:T(8,128)(2,1)} %pack.1), calls=%async_computation | async-start | bytes 1572864 | tf_op jit(solution)/shard_map/all_to_all | solution.py:235
  21.1 2.0 %constant_dynamic-update-slice_fusion.1 = bf16[66,128,128]{2,1,0:T(8,128)(2,1)S(1)} fusion(bf16[66,128,128]{2,1,0:T(8,128)(2,1)S(1)} %constant_dynamic-update-slice_fusion.2, bf16[64,128,128]{2,1,0:T(8,128)(2,1)} %param.22), kind=kLoop, calls=%fused_computation.99 | loop fusion | bytes 4194304
  23.2 3.2 %collective-permute-start.6 = (bf16[66,1,128]{2,1,0:T(2,128)(2,1)S(1)}, bf16[66,1,128]{2,1,0:T(2,128)(2,1)S(1)}, u32[]{:S(2)}, u32[]{:S(2)}) collective-permute-start(bf16[66,1,128]{2,1,0:T(2,128)(2,1)S(1)} %get-tuple-element.69), channel_id=1, source_target_pairs={{0,1},{1,2},{2,3},{3,4},{4,5},{5,6},{6,7},{7,8},{8,9},{9,10},{10,1... | collective-permute-start | bytes 50696 | tf_op jit(solution)/shard_map/ppermute | solution.py:193
  26.4 11.4 %all-to-all-done.in_ref = bf16[128,24,128]{2,1,0:T(8,128)(2,1)S(1)} async-done(((bf16[128,24,128]{2,1,0:T(8,128)(2,1)}), bf16[128,24,128]{2,1,0:T(8,128)(2,1)S(1)}, u32[]{:S(2)}, u32[]{:S(2)}) %all-to-all-start) | async-done | bytes 786464 | tf_op jit(solution)/shard_map/all_to_all | solution.py:235
  37.8 14.1 %scatter.1 = bf16[72,136,128]{2,1,0:T(8,128)(2,1)S(1)} custom-call(s32[2]{0:T(128)S(1)} %pad_add_fusion.edge_ref, bf16[128,24,128]{2,1,0:T(8,128)(2,1)S(1)} %all-to-all-done.in_ref), custom_call_target="tpu_custom_call" | custom-call | flops 5200000000 | bytes 3500000 | tf_op jit(solution)/shard_map/scatter/pallas_call | solution.py:166
  53.4 1.3 collective-permute-start
  54.7 1.3 collective-permute-start.1
  57.1 0.9 collective-permute-done
  58.1 3.8 %collective-permute-done.1 = bf16[5,136,128]{2,1,0:T(8,128)(2,1)S(1)} collective-permute-done((bf16[5,136,128]{2,1,0:T(8,128)(2,1)S(1)}, bf16[5,136,128]{2,1,0:T(8,128)(2,1)S(1)}, u32[]{:S(2)}, u32[]{:S(2)}) %collective-permute-start.1) | collective-permute-done | bytes 174112 | tf_op jit(solution)/shard_map/ppermute | solution.py:195
  62.4 2.9 %collective-permute-start.2 = (bf16[66,5,128]{2,1,0:T(8,128)(2,1)S(1)}, bf16[66,5,128]{2,1,0:T(8,128)(2,1)S(1)}, u32[]{:S(2)}, u32[]{:S(2)}) collective-permute-start(bf16[66,5,128]{2,1,0:T(8,128)(2,1)S(1)} %get-tuple-element.67), channel_id=1, source_target_pairs={{0,1},{1,2},{2,3},{3,4},{4,5},{5,6},{6,7},{7,8},{8,9},{9,10},{10,1... | collective-permute-start | bytes 253448 | tf_op jit(solution)/shard_map/ppermute | solution.py:193
  66.2 1.1 collective-permute-done.2
  67.2 4.2 %collective-permute-done.3 = bf16[66,5,128]{2,1,0:T(8,128)(2,1)S(1)} collective-permute-done((bf16[66,5,128]{2,1,0:T(8,128)(2,1)S(1)}, bf16[66,5,128]{2,1,0:T(8,128)(2,1)S(1)}, u32[]{:S(2)}, u32[]{:S(2)}) %collective-permute-start.3) | collective-permute-done | bytes 84512 | tf_op jit(solution)/shard_map/ppermute | solution.py:195
  72.5 3.1 %maximum_select_fusion.1 = (bf16[66,130,128]{2,1,0:T(8,128)(2,1)S(1)}, bf16[66,130,128]{2,1,0:T(8,128)(2,1)S(1)}) fusion(bf16[66,1,128]{2,1,0:T(2,128)(2,1)S(1)} %collective-permute-done.7, bf16[66,128,128]{2,1,0:T(8,128)(2,1)S(1)} %constant_dynamic-update-slice_fusion, bf16[66,1,128]{2,1,0:T(2,128)(2,1)S(1)} %collective-permute-done.6, ...), kind=kLoop, calls=%fused_computation.12 | loop fusion | flops 15375360 | bytes 8785986 | tf_op jit(solution)/shard_map/jit(_where)/select_n | solution.py:209
  75.6 7.0 %fusion.140 = (bf16[64,128,128]{2,1,0:T(8,128)(2,1)}, bf16[64,128,128]{2,1,0:T(8,128)(2,1)S(1)}, bf16[64,128,128]{2,1,0:T(8,128)(2,1)}, bf16[64,128,128]{2,1,0:T...) fusion(bf16[66,130,128]{2,1,0:T(8,128)(2,1)S(1)} %get-tuple-ele, ...), kind=kLoop, calls=%fused_computation.116 | loop fusion | bytes 37748736 | tf_op jit(solution)/shard_map/slice | solution.py:270
  83.4 1.4 fusion.82
  84.8 1.4 fusion.91
  87.0 1.4 fusion.67
  88.3 1.4 fusion.94
  90.5 1.4 fusion.52
  91.9 1.4 fusion.97
  94.1 12.0 %all-to-all-start.1 = ((bf16[128,16,128]{2,1,0:T(8,128)(2,1)}), bf16[128,16,128]{2,1,0:T(8,128)(2,1)S(1)}, u32[]{:S(2)}, u32[]{:S(2)}) async-start(bf16[128,16,128]{2,1,0:T(8,128)(2,1)} %bitcast.34), calls=%async_computation.1 | async-start | bytes 1048576 | tf_op jit(solution)/shard_map/all_to_all | solution.py:214
  106.1 2.4 %fusion.116 = f32[8192,128]{1,0:T(8,128)S(1)} fusion(bf16[8192,128]{1,0:T(8,128)(2,1)} %bitcast.116, bf16[3,3,128,128]{3,2,1,0:T(8,128)(2,1)S(1)} %copy-done.7), kind=kOutput, calls=%fused_computation.87 | convolution fusion | flops 268435456 | bytes 6324224 | tf_op jit(solution)/shard_map/dot_general | solution.py:273
  110.9 0.9 copy-done.3
  112.5 0.9 copy-done.2
  114.1 0.9 copy-done.1
  116.5 2.6 %convolution_add_fusion.2 = f32[8192,128]{1,0:T(8,128)} fusion(f32[8192,128]{1,0:T(8,128)S(1)} %convolution_add_fusion.3, bf16[8192,128]{1,0:T(8,128)(2,1)S(1)} %bitcast.110, bf16[3,3,128,128]{3,2,1,0:T(8,128)(2,1)S(1)} %copy-done.7), kind=kOutput, calls=%fused_computation.2 | convolution fusion | flops 269484032 | bytes 10518528 | tf_op jit(solution)/shard_map/dot_general | solution.py:273
  120.9 9.0 %all-to-all-start.2 = ((bf16[128,16,128]{2,1,0:T(8,128)(2,1)}), bf16[128,16,128]{2,1,0:T(8,128)(2,1)S(1)}, u32[]{:S(2)}, u32[]{:S(2)}) async-start(bf16[128,16,128]{2,1,0:T(8,128)(2,1)} %broadcast_in_dim.14), calls=%async_computation.2 | async-start | bytes 1048576 | tf_op jit(solution)/shard_map/all_to_all | solution.py:217
  130.0 3.0 %convolution_add_fusion.1 = f32[8192,128]{1,0:T(8,128)S(1)} fusion(f32[8192,128]{1,0:T(8,128)} %convolution_add_fusion.2, bf16[8192,128]{1,0:T(8,128)(2,1)S(1)} %bitcast.109, bf16[3,3,128,128]{3,2,1,0:T(8,128)(2,1)S(1)} %copy-done.7), kind=kOutput, calls=%fused_computation.1 | convolution fusion | flops 269484032 | bytes 10518528 | tf_op jit(solution)/shard_map/dot_general | solution.py:273
  133.0 2.0 %fusion = bf16[8192,128]{1,0:T(8,128)(2,1)} fusion(f32[8192,128]{1,0:T(8,128)S(1)} %convolution_add_fusion.1, bf16[8192,128]{1,0:T(8,128)(2,1)S(1)} %bitcast.117, bf16[3,3,128,128]{3,2,1,0:T(8,128)(2,1)S(1)} %copy-done.7), kind=kOutput, calls=%fused_computation.8 | convolution fusion | flops 270532608 | bytes 8421376 | tf_op jit(solution)/shard_map/dot_general | solution.py:273
  135.1 8.8 %all-to-all-done.2 = bf16[128,16,128]{2,1,0:T(8,128)(2,1)S(1)} async-done(((bf16[128,16,128]{2,1,0:T(8,128)(2,1)}), bf16[128,16,128]{2,1,0:T(8,128)(2,1)S(1)}, u32[]{:S(2)}, u32[]{:S(2)}) %all-to-all-start.2) | async-done | bytes 524320 | tf_op jit(solution)/shard_map/all_to_all | solution.py:217
  (57 shorter events, 17.1 us)
Async XLA Ops:
  1.4 21.7 %collective-permute-start.5 = (bf16[1,128,128]{2,1,0:T(8,128)(2,1)S(1)}, bf16[1,128,128]{2,1,0:T(8,128)(2,1)S(1)}, u32[]{:S(2)}, u32[]{:S(2)}) collective-permute-start(bf16[1,128,128]{2,1,0:T(8,128)(2,1)S(1)} %get-tuple-element.71), channel_id=1, source_target_pairs={{16,0},{32,16},{48,32},{64,48},{80,64},{96,80},{112,96},{0,112},{1... | collective-permute-start | bytes 98312 | tf_op jit(solution)/shard_map/ppermute | solution.py:195
  5.9 15.2 %collective-permute-start.4 = (bf16[1,128,128]{2,1,0:T(8,128)(2,1)S(1)}, bf16[1,128,128]{2,1,0:T(8,128)(2,1)S(1)}, u32[]{:S(2)}, u32[]{:S(2)}) collective-permute-start(bf16[1,128,128]{2,1,0:T(8,128)(2,1)S(1)} %get-tuple-element.72), channel_id=1, source_target_pairs={{0,16},{16,32},{32,48},{48,64},{64,80},{80,96},{96,112},{112,0},{1... | collective-permute-start | bytes 98312 | tf_op jit(solution)/shard_map/ppermute | solution.py:193
  10.0 27.8 %all-to-all-start = ((bf16[128,24,128]{2,1,0:T(8,128)(2,1)}), bf16[128,24,128]{2,1,0:T(8,128)(2,1)S(1)}, u32[]{:S(2)}, u32[]{:S(2)}) async-start(bf16[128,24,128]{2,1,0:T(8,128)(2,1)} %pack.1), calls=%async_computation | async-start | bytes 1572864 | tf_op jit(solution)/shard_map/all_to_all | solution.py:235
  23.2 49.2 %collective-permute-start.6 = (bf16[66,1,128]{2,1,0:T(2,128)(2,1)S(1)}, bf16[66,1,128]{2,1,0:T(2,128)(2,1)S(1)}, u32[]{:S(2)}, u32[]{:S(2)}) collective-permute-start(bf16[66,1,128]{2,1,0:T(2,128)(2,1)S(1)} %get-tuple-element.69), channel_id=1, source_target_pairs={{0,1},{1,2},{2,3},{3,4},{4,5},{5,6},{6,7},{7,8},{8,9},{9,10},{10,1... | collective-permute-start | bytes 50696 | tf_op jit(solution)/shard_map/ppermute | solution.py:193
  26.4 46.0 %collective-permute-start.7 = (bf16[66,1,128]{2,1,0:T(2,128)(2,1)S(1)}, bf16[66,1,128]{2,1,0:T(2,128)(2,1)S(1)}, u32[]{:S(2)}, u32[]{:S(2)}) collective-permute-start(bf16[66,1,128]{2,1,0:T(2,128)(2,1)S(1)} %get-tuple-element.70), channel_id=1, source_target_pairs={{1,0},{2,1},{3,2},{4,3},{5,4},{6,5},{7,6},{8,7},{9,8},{10,9},{11,1... | collective-permute-start | bytes 50696 | tf_op jit(solution)/shard_map/ppermute | solution.py:195
  53.4 4.6 %collective-permute-start = (bf16[5,136,128]{2,1,0:T(8,128)(2,1)S(1)}, bf16[5,136,128]{2,1,0:T(8,128)(2,1)S(1)}, u32[]{:S(2)}, u32[]{:S(2)}) collective-permute-start(bf16[5,136,128]{2,1,0:T(8,128)(2,1)S(1)} %get-tuple-element.54), channel_id=1, source_target_pairs={{0,16},{16,32},{32,48},{48,64},{64,80},{80,96},{96,112},{1,17},{17... | collective-permute-start | bytes 522248 | tf_op jit(solution)/shard_map/ppermute | solution.py:193
  54.7 7.1 %collective-permute-start.1 = (bf16[5,136,128]{2,1,0:T(8,128)(2,1)S(1)}, bf16[5,136,128]{2,1,0:T(8,128)(2,1)S(1)}, u32[]{:S(2)}, u32[]{:S(2)}) collective-permute-start(bf16[5,136,128]{2,1,0:T(8,128)(2,1)S(1)} %get-tuple-element.55), channel_id=1, source_target_pairs={{16,0},{32,16},{48,32},{64,48},{80,64},{96,80},{112,96},{17,1},{33... | collective-permute-start | bytes 522248 | tf_op jit(solution)/shard_map/ppermute | solution.py:195
  62.4 4.8 %collective-permute-start.2 = (bf16[66,5,128]{2,1,0:T(8,128)(2,1)S(1)}, bf16[66,5,128]{2,1,0:T(8,128)(2,1)S(1)}, u32[]{:S(2)}, u32[]{:S(2)}) collective-permute-start(bf16[66,5,128]{2,1,0:T(8,128)(2,1)S(1)} %get-tuple-element.67), channel_id=1, source_target_pairs={{0,1},{1,2},{2,3},{3,4},{4,5},{5,6},{6,7},{7,8},{8,9},{9,10},{10,1... | collective-permute-start | bytes 253448 | tf_op jit(solution)/shard_map/ppermute | solution.py:193
  65.3 6.2 %collective-permute-start.3 = (bf16[66,5,128]{2,1,0:T(8,128)(2,1)S(1)}, bf16[66,5,128]{2,1,0:T(8,128)(2,1)S(1)}, u32[]{:S(2)}, u32[]{:S(2)}) collective-permute-start(bf16[66,5,128]{2,1,0:T(8,128)(2,1)S(1)} %get-tuple-element.68), channel_id=1, source_target_pairs={{1,0},{2,1},{3,2},{4,3},{5,4},{6,5},{7,6},{8,7},{9,8},{10,9},{11,1... | collective-permute-start | bytes 253448 | tf_op jit(solution)/shard_map/ppermute | solution.py:195
  91.9 14.2 %copy-start.7 = (bf16[3,3,128,128]{3,2,1,0:T(8,128)(2,1)S(1)}, bf16[3,3,128,128]{3,2,1,0:T(8,128)(2,1)}, u32[]{:S(2)}) copy-start(bf16[3,3,128,128]{3,2,1,0:T(8,128)(2,1)} %param.23) | copy-start | bytes 884740
  94.1 25.8 %all-to-all-start.1 = ((bf16[128,16,128]{2,1,0:T(8,128)(2,1)}), bf16[128,16,128]{2,1,0:T(8,128)(2,1)S(1)}, u32[]{:S(2)}, u32[]{:S(2)}) async-start(bf16[128,16,128]{2,1,0:T(8,128)(2,1)} %bitcast.34), calls=%async_computation.1 | async-start | bytes 1048576 | tf_op jit(solution)/shard_map/all_to_all | solution.py:214
  106.1 2.5 %copy-start.5 = (bf16[64,128,128]{2,1,0:T(8,128)(2,1)S(1)}, bf16[64,128,128]{2,1,0:T(8,128)(2,1)}, u32[]{:S(2)}) copy-start(bf16[64,128,128]{2,1,0:T(8,128)(2,1)} %get-tuple-element.65) | copy-start | bytes 6291460
  108.6 1.6 %copy-start.4 = (bf16[64,128,128]{2,1,0:T(8,128)(2,1)S(1)}, bf16[64,128,128]{2,1,0:T(8,128)(2,1)}, u32[]{:S(2)}) copy-start(bf16[64,128,128]{2,1,0:T(8,128)(2,1)} %get-tuple-element.64) | copy-start | bytes 6291460
  110.2 1.6 %copy-start.3 = (bf16[64,128,128]{2,1,0:T(8,128)(2,1)S(1)}, bf16[64,128,128]{2,1,0:T(8,128)(2,1)}, u32[]{:S(2)}) copy-start(bf16[64,128,128]{2,1,0:T(8,128)(2,1)} %get-tuple-element.63) | copy-start | bytes 6291460
  111.8 1.6 %copy-start.2 = (bf16[64,128,128]{2,1,0:T(8,128)(2,1)S(1)}, bf16[64,128,128]{2,1,0:T(8,128)(2,1)}, u32[]{:S(2)}) copy-start(bf16[64,128,128]{2,1,0:T(8,128)(2,1)} %get-tuple-element.62) | copy-start | bytes 6291460
  113.3 1.6 %copy-start.1 = (bf16[64,128,128]{2,1,0:T(8,128)(2,1)S(1)}, bf16[64,128,128]{2,1,0:T(8,128)(2,1)}, u32[]{:S(2)}) copy-start(bf16[64,128,128]{2,1,0:T(8,128)(2,1)} %get-tuple-element.61) | copy-start | bytes 6291460
  114.9 1.6 %copy-start = (bf16[64,128,128]{2,1,0:T(8,128)(2,1)S(1)}, bf16[64,128,128]{2,1,0:T(8,128)(2,1)}, u32[]{:S(2)}) copy-start(bf16[64,128,128]{2,1,0:T(8,128)(2,1)} %get-tuple-element.60) | copy-start | bytes 6291460
  120.9 22.9 %all-to-all-start.2 = ((bf16[128,16,128]{2,1,0:T(8,128)(2,1)}), bf16[128,16,128]{2,1,0:T(8,128)(2,1)S(1)}, u32[]{:S(2)}, u32[]{:S(2)}) async-start(bf16[128,16,128]{2,1,0:T(8,128)(2,1)} %broadcast_in_dim.14), calls=%async_computation.2 | async-start | bytes 1048576 | tf_op jit(solution)/shard_map/all_to_all | solution.py:217
  130.0 3.1 %copy-start.6 = (bf16[64,128,128]{2,1,0:T(8,128)(2,1)S(1)}, bf16[64,128,128]{2,1,0:T(8,128)(2,1)}, u32[]{:S(2)}) copy-start(bf16[64,128,128]{2,1,0:T(8,128)(2,1)} %get-tuple-element.58) | copy-start | bytes 6291460

commit v2 on v1

--- a/solution.py
+++ b/solution.py
@@ -94,7 +94,92 @@
     return jnp.where((tap >= 0.0) & (tap <= 7.0), weight, 0.0)
 
 
-def scatter_kernel(edge_ref, in_ref, canvas_ref, rows_ref, lat_w, lon_w, side_w):
+def prep_kernel(feat_ref, above_ref, below_ref, left_ref, right_ref, out_ref, side_ref):
+    eye = jnp.where(
+        lax.broadcasted_iota(jnp.int32, (128, 128), 0)
+        == lax.broadcasted_iota(jnp.int32, (128, 128), 1),
+        1.0,
+        0.0,
+    ).astype(BF16)
+    spot = lax.broadcasted_iota(jnp.int32, (144, 384), 0)
+    want = lax.broadcasted_iota(jnp.int32, (144, 384), 1)
+    want = want % 128 + want // 128 - 1
+    want = jnp.where(want < 0, 135, jnp.where(want == 128, 136, want))
+    shift = jnp.where(spot == want, 1.0, 0.0).astype(BF16)
+
+    def lines(take, start, count):
+        turned = []
+        for i in range(count):
+            ext = jnp.concatenate(
+                [take(i), jnp.concatenate([left_ref[start + i], right_ref[start + i]], axis=0)],
+                axis=0,
+            )
+            turned.append(nt(eye, ext).astype(BF16))
+        moved = mm(jnp.concatenate(turned, axis=0), shift).astype(BF16)
+        out_ref[pl.ds(start, count)] = moved.reshape(count, 128, 384)
+
+    lines(lambda i: above_ref[i], 0, 5)
+
+    def body(step, carry):
+        lines(lambda i: feat_ref[step * 8 + i], step * 8 + 5, 8)
+        return carry
+
+    lax.fori_loop(0, 8, body, 0)
+    lines(lambda i: below_ref[i], 69, 5)
+    left = left_ref[...].astype(F32)
+    right = right_ref[...].astype(F32)
+    first = jnp.concatenate(
+        [above_ref[:, 0:8, :], feat_ref[:, 0:8, :], below_ref[:, 0:8, :]], axis=0
+    ).astype(F32)
+    last = jnp.concatenate(
+        [above_ref[:, 120:128, :], feat_ref[:, 120:128, :], below_ref[:, 120:128, :]], axis=0
+    ).astype(F32)
+    groups = (
+        (left[:, 3:7], last[:, 7:8], right[:, 0:3]),
+        (left[:, 4:8], right[:, 0:4]),
+        (left[:, 5:8], first[:, 0:1], right[:, 1:5]),
+    )
+    for b in range(3):
+        eight = jnp.concatenate(groups[b], axis=1).reshape(592, 128)
+        eight = jnp.concatenate([eight, jnp.zeros((48, 128), F32)], axis=0)
+        side_ref[b * 128 : (b + 1) * 128, :] = eight.T.astype(BF16)
+
+
+def prep(features, above, below, left, right):
+    vmem = pl.BlockSpec(memory_space=pltpu.VMEM)
+    return pl.pallas_call(
+        prep_kernel,
+        out_shape=(
+            jax.ShapeDtypeStruct((74, 128, 384), BF16),
+            jax.ShapeDtypeStruct((384, 640), BF16),
+        ),
+        in_specs=[vmem] * 5,
+        out_specs=(vmem, vmem),
+        compiler_params=pltpu.CompilerParams(vmem_limit_bytes=24 << 20),
+        cost_estimate=pl.CostEstimate(
+            flops=2_500_000_000, bytes_accessed=10_000_000, transcendentals=0
+        ),
+        name="prep",
+    )(features, above, below, left, right)
+
+
+def scatter_kernel(
+    edge_ref,
+    in_ref,
+    feat_ref,
+    feat_side_ref,
+    canvas_ref,
+    up_ref,
+    down_ref,
+    sum_ref,
+    rows_ref,
+    lat_w,
+    lon_w,
+    side_w,
+    three,
+    three_side,
+    acc_ref,
+):
     total = TILES * SLOTS
     rows_ref[...] = in_ref[:, 0:SLOTS, :].reshape(total, 128)
     tail = in_ref[:, SLOTS:CHUNK, :].reshape(TILES * (CHUNK - SLOTS), 128)
@@ -131,6 +216,27 @@
     line8 = lax.broadcasted_iota(jnp.int32, (8, total), 0)
     column = jnp.where(line8 < 4, line8 - 4, line8 + 124).astype(F32)
     side_w[...] = tap_weights(cell_lon, frac_lon, column).astype(BF16).astype(F32)
+    blank = jnp.zeros((2, 128, 128), BF16)
+    three[0:2, :, 256:384] = blank
+    three[72:74, :, 0:128] = blank
+    three[0:1, :, 128:256] = blank[:1]
+    three[73:74, :, 128:256] = blank[:1]
+    three_side[...] = jnp.zeros_like(three_side)
+    acc_ref[...] = jnp.zeros_like(acc_ref)
+
+    def weight_part(start, count):
+        parts = []
+        for b in range(3):
+            parts.append(
+                jnp.concatenate(
+                    [feat_ref[start + i, :, b * 128 : (b + 1) * 128] for i in range(count)],
+                    axis=1,
+                )
+            )
+        acc_ref[...] += mm(
+            jnp.concatenate(parts, axis=0),
+            three[pl.ds(start, count)].reshape(count * 128, 384),
+        )
 
     def eight_lines(step, carry):
         start = pl.multiple_of(step * 8, 8)
@@ -153,77 +259,205 @@
             rows = rows_ref[cols, :]
             acc = acc + mm(jnp.concatenate(parts, axis=0), rows)
             side = side + mm(jnp.concatenate(side_parts, axis=0).astype(BF16), rows)
-        canvas_ref[pl.ds(start, 8), 0:128, :] = acc.astype(BF16).reshape(8, 128, 128)
-        canvas_ref[pl.ds(start, 8), 128:136, :] = side.reshape(8, 8, 128).astype(BF16)
+        main = acc.astype(BF16).reshape(8, 128, 128)
+        canvas_ref[pl.ds(start, 8), 0:128, :] = main
+        for a in range(3):
+            three[pl.ds(start + a, 8), :, a * 128 : (a + 1) * 128] = main
+        side = side.reshape(8, 8, 128)
+        canvas_ref[pl.ds(start, 8), 128:136, :] = side.astype(BF16)
+        for a in range(3):
+            three_side[pl.ds(start + a, 8), :, a * 128 : (a + 1) * 128] = side
+        weight_part(start, 8)
         return carry
 
     lax.fori_loop(0, 9, eight_lines, 0)
-
-
-def scatter(edge, incoming):
+    weight_part(72, 2)
+    acc = acc_ref[...] + mm(
+        feat_side_ref[...], three_side[...].reshape(640, 384).astype(BF16)
+    )
+    for a in range(3):
+        for b in range(3):
+            at = (a * 3 + b) * 128
+            sum_ref[at : at + 128, :] = acc[
+                b * 128 : (b + 1) * 128, a * 128 : (a + 1) * 128
+            ].astype(BF16)
+    sum_ref[1152:, :] = jnp.zeros((2048 - 1152, 128), BF16)
+    up_ref[...] = canvas_ref[1:5]
+    down_ref[...] = canvas_ref[67:72]
+
+
+def scatter(edge, incoming, feat, feat_side):
     vmem = pl.BlockSpec(memory_space=pltpu.VMEM)
     total = TILES * SLOTS
     return pl.pallas_call(
         scatter_kernel,
-        out_shape=jax.ShapeDtypeStruct((72, 136, 128), BF16),
-        in_specs=[pl.BlockSpec(memory_space=pltpu.SMEM), vmem],
-        out_specs=vmem,
+        out_shape=(
+            jax.ShapeDtypeStruct((72, 136, 128), BF16),
+            jax.ShapeDtypeStruct((4, 136, 128), BF16),
+            jax.ShapeDtypeStruct((5, 136, 128), BF16),
+            jax.ShapeDtypeStruct((2048, 128), BF16),
+        ),
+        in_specs=[pl.BlockSpec(memory_space=pltpu.SMEM), vmem, vmem, vmem],
+        out_specs=(vmem,) * 4,
         scratch_shapes=[
             pltpu.VMEM((total, 128), BF16),
             pltpu.VMEM((72, total), F32),
             pltpu.VMEM((128, total), BF16),
             pltpu.VMEM((8, total), F32),
+            pltpu.VMEM((74, 128, 384), BF16),
+            pltpu.VMEM((80, 8, 384), F32),
+            pltpu.VMEM((384, 384), F32),
         ],
-        compiler_params=pltpu.CompilerParams(vmem_limit_bytes=40 << 20),
+        compiler_params=pltpu.CompilerParams(vmem_limit_bytes=44 << 20),
         cost_estimate=pl.CostEstimate(
-            flops=5_200_000_000, bytes_accessed=3_500_000, transcendentals=500_000
+            flops=8_200_000_000, bytes_accessed=12_000_000, transcendentals=500_000
         ),
         name="scatter",
-    )(edge, incoming)
-
-
-def padded_2(cells, sides, width, closed):
-    for axis, dim in sides:
-        count = lax.axis_size(axis)
-        ends = count if closed else count - 1
-        head = lax.slice_in_dim(cells, 0, width, axis=dim)
-        tail = lax.slice_in_dim(cells, cells.shape[dim] - width, cells.shape[dim], axis=dim)
-        cells = jnp.concatenate(
+    )(edge, incoming, feat, feat_side)
+
+
+def sides_kernel(canvas_ref, above_ref, below_ref, right_ref, left_ref):
+    def tall(cols):
+        block = canvas_ref[3:69, cols, :].astype(F32)
+        return jnp.concatenate(
             [
-                lax.ppermute(tail, axis, [(i, (i + 1) % count) for i in range(ends)]),
-                cells,
-                lax.ppermute(head, axis, [((i + 1) % count, i) for i in range(ends)]),
+                block[0:5] + above_ref[:, cols, :].astype(F32),
+                block[5:62],
+                block[62:66] + below_ref[:, cols, :].astype(F32),
             ],
-            axis=dim,
-        )
-    return cells
-
-
-def clear_rim(padded):
+            axis=0,
+        )
+
+    side = tall(slice(128, 136))
+    last = tall(slice(120, 128))
+    head = tall(slice(0, 8))
+    blank = jnp.zeros((66, 4, 128), F32)
+    right_ref[...] = jnp.concatenate([last[:, 7:8], side[:, 4:8], blank[:, :3]], axis=1).astype(
+        BF16
+    )
+    left_ref[...] = jnp.concatenate([side[:, 1:4], head[:, 0:1], blank], axis=1).astype(BF16)
+
+
+def sides(canvas, above, below):
+    vmem = pl.BlockSpec(memory_space=pltpu.VMEM)
+    shape = jax.ShapeDtypeStruct((66, 8, 128), BF16)
+    return pl.pallas_call(
+        sides_kernel,
+        out_shape=(shape, shape),
+        in_specs=[vmem] * 3,
+        out_specs=(vmem, vmem),
+        cost_estimate=pl.CostEstimate(flops=1_000_000, bytes_accessed=1_000_000, transcendentals=0),
+        name="sides",
+    )(canvas, above, below)
+
+
+def conv_kernel(canvas_ref, above_ref, below_ref, left_ref, right_ref, weight_ref, out_ref, grid):
+    @pl.when(pl.program_id(0) == 0)
+    def _():
+        grid[5:62, 0:128, :] = canvas_ref[8:65, 0:128, :]
+        grid[0:5, 0:128, :] = (
+            canvas_ref[3:8, 0:128, :].astype(F32) + above_ref[:, 0:128, :].astype(F32)
+        ).astype(BF16)
+        grid[62:66, 0:128, :] = (
+            canvas_ref[65:69, 0:128, :].astype(F32) + below_ref[:, 0:128, :].astype(F32)
+        ).astype(BF16)
+        left = left_ref[...].astype(F32)
+        right = right_ref[...].astype(F32)
+        blank = jnp.zeros((66, 14, 128), F32)
+        grid[:, 0:16, :] = (
+            grid[:, 0:16, :].astype(F32)
+            + jnp.concatenate([left[:, 1:5], blank[:, :12]], axis=1)
+        ).astype(BF16)
+        grid[:, 112:128, :] = (
+            grid[:, 112:128, :].astype(F32)
+            + jnp.concatenate([blank[:, :13], right[:, 0:3]], axis=1)
+        ).astype(BF16)
+        side = canvas_ref[3:69, 128:136, :].astype(F32)
+        side = jnp.concatenate(
+            [
+                side[0:5] + above_ref[:, 128:136, :].astype(F32),
+                side[5:62],
+                side[62:66] + below_ref[:, 128:136, :].astype(F32),
+            ],
+            axis=0,
+        )
+        grid[:, 128:144, :] = jnp.concatenate(
+            [side[:, 4:5] + right[:, 3:4], blank, side[:, 3:4] + left[:, 0:1]], axis=1
+        ).astype(BF16)
+
+    start = pl.program_id(0) * 8
+    taps = jnp.concatenate(
+        [grid[pl.ds(start + 2 - a, 8)].reshape(8 * 144, 128) for a in range(3)], axis=1
+    )
+    weight = jnp.concatenate([weight_ref[a].reshape(384, 128) for a in range(3)], axis=1)
+    every = nt(taps, weight).reshape(8, 144, 384)
+    for i in range(8):
+        one = every[i]
+        got = (
+            one[:, 128:256]
+            + pltpu.roll(one[:, 0:128], 143, 0)
+            + pltpu.roll(one[:, 256:384], 1, 0)
+        )
+        out_ref[i] = got[0:128].astype(BF16)
+
+
+def conv(canvas, above, below, left, right, weight):
+    def whole(x):
+        return pl.BlockSpec(
+            x.shape, lambda i: (0,) * x.ndim, pipeline_mode=pl.Buffered(1)
+        )
+
+    args = (canvas, above, below, left, right, weight)
+    return pl.pallas_call(
+        conv_kernel,
+        grid=(8,),
+        out_shape=jax.ShapeDtypeStruct((64, 128, 128), BF16),
+        in_specs=[whole(x) for x in args],
+        out_specs=pl.BlockSpec((8, 128, 128), lambda i: (i, 0, 0)),
+        scratch_shapes=[pltpu.VMEM((66, 144, 128), BF16)],
+        compiler_params=pltpu.CompilerParams(vmem_limit_bytes=24 << 20),
+        cost_estimate=pl.CostEstimate(
+            flops=2_700_000_000, bytes_accessed=4_500_000, transcendentals=0
+        ),
+        name="conv",
+    )(*args)
+
+
+def gather_kernel(in_ref, out_ref):
+    mine = jnp.sum(in_ref[...].astype(F32), axis=0)
+    out_ref[...] = jnp.broadcast_to(mine.astype(BF16)[None], out_ref.shape)
+
+
+def share(got):
+    vmem = pl.BlockSpec(memory_space=pltpu.VMEM)
+    return pl.pallas_call(
+        gather_kernel,
+        out_shape=jax.ShapeDtypeStruct(got.shape, BF16),
+        in_specs=[vmem],
+        out_specs=vmem,
+        cost_estimate=pl.CostEstimate(flops=300_000, bytes_accessed=1_000_000, transcendentals=0),
+        name="share",
+    )(got)
+
+
+def both_ways(forth, back, axis, closed):
+    count = lax.axis_size(axis)
+    ends = count if closed else count - 1
+    return (
+        lax.ppermute(forth, axis, [(i, (i + 1) % count) for i in range(ends)]),
+        lax.ppermute(back, axis, [((i + 1) % count, i) for i in range(ends)]),
+    )
+
+
+def shards(grad_rows, owner, lat_offset, lon_offset, position, live_count, features, conv_weight):
+    count = grad_rows.shape[0]
     lat_index = lax.axis_index("lat")
-    lat_count = lax.axis_size("lat")
-    row_line = jnp.arange(padded.shape[0], dtype=jnp.int32)
-    masked = (row_line == 0) & (lat_index == 0) | (row_line == padded.shape[0] - 1) & (
-        lat_index == lat_count - 1
-    )
-    return jnp.where(masked[:, None, None], jnp.zeros_like(padded), padded)
-
-
-def total_sum(parts):
-    padded = jnp.pad(parts.astype(BF16), ((0, TILES * 16 - parts.shape[0]), (0, 0)))
-    got = lax.all_to_all(padded.reshape(TILES, 16, 128), AXES, 0, 0, tiled=True)
-    mine = jnp.sum(got.astype(F32), axis=0).astype(BF16)
-    every = jnp.broadcast_to(mine[None], (TILES, 16, 128))
-    every = lax.all_to_all(every, AXES, 0, 0, tiled=True)
-    return every.reshape(TILES * 16, 128)[: parts.shape[0]].astype(F32)
-
-
-def shards(grad_rows, owner, lat_offset, lon_offset, position, live_count, features, conv_weight):
-    channels = grad_rows.shape[1]
-    tile_lat = features.shape[0]
-    tile_lon = features.shape[1]
-    input_padded = clear_rim(padded_2(features, (("lat", 0), ("lon", 1)), 1, True))
-    count = grad_rows.shape[0]
+    edge = jnp.stack(
+        [
+            jnp.where(lat_index == 0, 4, 0),
+            jnp.where(lat_index == lax.axis_size("lat") - 1, 68, 72),
+        ]
+    ).astype(jnp.int32)
     outgoing = pack(
         live_count,
         owner.reshape(1, count),
@@ -233,60 +467,22 @@
         grad_rows,
     )
     incoming = lax.all_to_all(outgoing, AXES, 0, 0, tiled=True)
-    lat_index = lax.axis_index("lat")
-    edge = jnp.stack(
-        [
-            jnp.where(lat_index == 0, 4, 0),
-            jnp.where(lat_index == lax.axis_size("lat") - 1, 68, 72),
-        ]
-    ).astype(jnp.int32)
-    canvas = scatter(edge, incoming).astype(F32)
-    canvas = jnp.concatenate([canvas[:, 128:132], canvas[:, :128], canvas[:, 132:]], axis=1)
-    edge_rows = jnp.concatenate([canvas[:5], canvas[-5:]], axis=0)
-    edge_rows = padded_2(edge_rows.astype(jnp.bfloat16), (("lat", 0),), 5, False).astype(
-        edge_rows.dtype
-    )
-    inner = canvas[4:-4]
-    inner = inner.at[:4].add(edge_rows[1:5]).at[-4:].add(edge_rows[15:19])
-    rim_top = edge_rows[0] + canvas[3]
-    rim_bottom = canvas[-4] + edge_rows[19]
-    tall = jnp.concatenate([rim_top[None], inner, rim_bottom[None]], axis=0)
-    side_cols = jnp.concatenate([tall[:, :5], tall[:, -5:]], axis=1)
-    side_cols = padded_2(side_cols.astype(jnp.bfloat16), (("lon", 1),), 5, True).astype(
-        side_cols.dtype
-    )
-    middle = tall[:, 4:-4]
-    middle = middle.at[:, :4].add(side_cols[:, 1:5]).at[:, -4:].add(side_cols[:, 15:19])
-    rim_left = side_cols[:, 0] + tall[:, 3]
-    rim_right = tall[:, -4] + side_cols[:, 19]
-    whole = jnp.concatenate([rim_left[:, None], middle, rim_right[:, None]], axis=1)
-    grid_padded = clear_rim(whole.astype(jnp.bfloat16))
-    grid_grad = grid_padded[1:-1, 1:-1]
-    flat_grad = grid_grad.reshape(-1, channels)
-    input_grad = jnp.zeros((tile_lat * tile_lon, channels), jnp.float32)
-    weight_parts = []
-    for a in range(3):
-        for b in range(3):
-            shifted = grid_padded[2 - a : 2 - a + tile_lat, 2 - b : 2 - b + tile_lon].reshape(
-                -1, channels
-            )
-            input_grad = input_grad + lax.dot_general(
-                shifted,
-                conv_weight[a, b],
-                (((1,), (1,)), ((), ())),
-                preferred_element_type=jnp.float32,
-            )
-            window = input_padded[a : a + tile_lat, b : b + tile_lon].reshape(-1, channels)
-            weight_parts.append(
-                lax.dot_general(
-                    window, flat_grad, (((0,), (0,)), ((), ())), preferred_element_type=jnp.float32
-                )
-            )
-    weight_grad = total_sum(jnp.concatenate(weight_parts, axis=0))
-    return (
-        input_grad.reshape(tile_lat, tile_lon, channels).astype(jnp.bfloat16),
-        weight_grad.reshape(3, 3, channels, channels),
-    )
+    above, below = both_ways(features[59:64], features[0:5], "lat", False)
+    ends = [
+        jnp.concatenate([x[:, c : c + 8] for x in (above, features, below)], axis=0)
+        for c in (120, 0)
+    ]
+    left, right = both_ways(ends[0], ends[1], "lon", True)
+    feat, feat_side = prep(features, above, below, left, right)
+    canvas, up, down, part = scatter(edge, incoming, feat, feat_side)
+    got = lax.all_to_all(part.reshape(TILES, 16, 128), AXES, 0, 0, tiled=True)
+    grid_above, grid_below = both_ways(down, up, "lat", False)
+    send_right, send_left = sides(canvas, grid_above, grid_below)
+    from_left, from_right = both_ways(send_right, send_left, "lon", True)
+    every = lax.all_to_all(share(got), AXES, 0, 0, tiled=True)
+    input_grad = conv(canvas, grid_above, grid_below, from_left, from_right, conv_weight)
+    weight_grad = every.reshape(TILES * 16, 128)[:1152].astype(F32)
+    return input_grad, weight_grad.reshape(3, 3, 128, 128)
 
 
 def solution(mesh):

time: 145 us -> 135 us (0.931)
  Pallas kernels: 17.6 us -> 49.4 us
  matrix products: 24.3 us -> 0 us
  local copies, waits for them, and re-layouts: 17.6 us -> 11.6 us
  other arithmetic: 7.42 us -> 2.31 us
  waiting for transfers between devices: 31 us -> 26.5 us
  starting transfers between devices: 45.1 us -> 43.3 us
    pallas_call x1 -> x5, Pallas kernels: 14.1 us -> 45.9 us  [the longest x1 28.6 us: scatter(): pl.pallas_call(scatter_kernel, out_shape=(jax.ShapeDtypeStruct((72, 136,...]
    dot_general x18 -> x0, matrix products: 24.3 us -> none  [the longest x9 13.7 us: shards(): lax.dot_general(shifted, conv_weight[a, b], (((1,), (1,)), ((), ())), pre...]
    all_to_all x1, waiting for transfers between devices: 11.4 us -> 0.01 us  [shards(): incoming = lax.all_to_all(outgoing, AXES, 0, 0, tiled=True)]
    all_to_all x2, starting transfers between devices: 21 us -> 13 us  [the longest x1 8.11 us: shards(): got = lax.all_to_all(part.reshape(TILES, 16, 128), AXES, 0, 0, tiled=True)]
    slice x10 -> x5, local copies, waits for them, and re-layouts: 9.53 us -> 2.05 us  [the longest x1 1.02 us: shards(): above, below = both_ways(features[59:64], features[0:5], 'lat', False)]
    ppermute x8, waiting for transfers between devices: 10.1 us -> 17 us  [the longest x4 8.91 us: both_ways(): lax.ppermute(back, axis, [((i + 1) % count, i) for i in range(ends)])]
    ppermute x8, starting transfers between devices: 13.1 us -> 17 us  [the longest x4 14.3 us: both_ways(): lax.ppermute(forth, axis, [(i, (i + 1) % count) for i in range(ends)])]
    unnamed x18 -> x24, local copies, waits for them, and re-layouts: 6.36 us -> 9.51 us
  transfers between devices with their start and end apart: 11 -> 11, of which waited for: 7 -> 5; matrix products, arithmetic and copies ran while one was open for 14% -> 1% of each run, Pallas kernels for 12% -> 15%
where the time goes in v2:
time: 135 us
  Pallas kernels  49.4 us (37%)
  starting transfers between devices  43.3 us (32%)
  waiting for transfers between devices  26.5 us (20%)
  local copies, waits for them, and re-layouts  11.6 us (9%)
  other arithmetic  2.31 us (2%)
  between operations  1.46 us (1%)
    pallas_call x1, Pallas kernels, scatter(): pl.pallas_call(scatter_kernel, out_shape=(jax.ShapeDtypeStruct((72, 136,...  28.6 us
    ppermute x4, starting transfers between devices, both_ways(): lax.ppermute(forth, axis, [(i, (i + 1) % count) for i in range(ends)])  14.3 us
    all_to_all x1, starting transfers between devices, shards(): incoming = lax.all_to_all(outgoing, AXES, 0, 0, tiled=True)  13.3 us
    unnamed x24, local copies, waits for them, and re-layouts  9.51 us
    all_to_all x1, waiting for transfers between devices, shards(): got = lax.all_to_all(part.reshape(TILES, 16, 128), AXES, 0, 0, tiled=True)  9.51 us
    ppermute x4, waiting for transfers between devices, both_ways(): lax.ppermute(back, axis, [((i + 1) % count, i) for i in range(ends)])  8.91 us
    all_to_all x1, starting transfers between devices, shards(): got = lax.all_to_all(part.reshape(TILES, 16, 128), AXES, 0, 0, tiled=True)  8.11 us
    ppermute x4, waiting for transfers between devices, both_ways(): lax.ppermute(forth, axis, [(i, (i + 1) % count) for i in range(ends)])  8.1 us
  transfers between devices with their start and end apart: 11, of which 5 were waited for; matrix products, arithmetic and copies ran while one was open for 1% of the time, Pallas kernels for 15%

profile of v2, /device:TPU:1, one launch (start us, length us, event | category | flops | bytes accessed | tf_op | source)
XLA Modules:
  0.0 134.6 jit_solution(6135974401957043467)
XLA Ops:
  0.6 1.0 fusion.1
  1.7 1.4 %collective-permute-start.1 = (bf16[5,128,128]{2,1,0:T(8,128)(2,1)S(1)}, bf16[5,128,128]{2,1,0:T(8,128)(2,1)S(1)}, u32[]{:S(2)}, u32[]{:S(2)}) collective-permute-start(bf16[5,128,128]{2,1,0:T(8,128)(2,1)S(1)} %get-tuple-element.20), channel_id=1, source_target_pairs={{16,0},{32,16},{48,32},{64,48},{80,64},{96,80},{112,96},{17,1},{33... | collective-permute-start | bytes 491528 | tf_op jit(solution)/shard_map/ppermute | solution.py:448
  3.1 4.7 %collective-permute-start = (bf16[5,128,128]{2,1,0:T(8,128)(2,1)S(1)}, bf16[5,128,128]{2,1,0:T(8,128)(2,1)S(1)}, u32[]{:S(2)}, u32[]{:S(2)}) collective-permute-start(bf16[5,128,128]{2,1,0:T(8,128)(2,1)S(1)} %get-tuple-element.21), channel_id=1, source_target_pairs={{0,16},{16,32},{32,48},{48,64},{64,80},{80,96},{96,112},{1,17},{17... | collective-permute-start | bytes 491528 | tf_op jit(solution)/shard_map/ppermute | solution.py:447
  8.4 3.5 %pack.1 = bf16[128,24,128]{2,1,0:T(8,128)(2,1)} custom-call(s32[1]{0:T(128)S(6)} %copy.10.live_ref, s32[1,1024]{1,0:T(1,128)} %bitcast.10, s32[1,1024]{1,0:T(1,128)} %bitcast.11, s32[1,1024]{1,0:T(1,128)} %bitcast.12, bf16[2,1024]{1,0:T(2,128)(2,1)} %bitcast.13, bf16[1024,128]{1,0:T(8,128)(2,1)} %rows_ref.1), custom_call_target="tpu_custom_call" | custom-call | flops 700000000 | bytes 1500000 | tf_op jit(solution)/shard_map/pack/pallas_call | solution.py:80
  11.9 13.3 %all-to-all-start = ((bf16[128,24,128]{2,1,0:T(8,128)(2,1)}), bf16[128,24,128]{2,1,0:T(8,128)(2,1)S(1)}, u32[]{:S(2)}, u32[]{:S(2)}) async-start(bf16[128,24,128]{2,1,0:T(8,128)(2,1)} %pack.1), calls=%async_computation | async-start | bytes 1572864 | tf_op jit(solution)/shard_map/all_to_all | solution.py:469
  25.3 0.7 pad_maximum_fusion
  26.0 3.1 %collective-permute-start.2 = (bf16[74,8,128]{2,1,0:T(8,128)(2,1)}, bf16[74,8,128]{2,1,0:T(8,128)(2,1)S(1)}, u32[]{:S(2)}, u32[]{:S(2)}) collective-permute-start(bf16[74,8,128]{2,1,0:T(8,128)(2,1)} %pad_maximum_fusion), channel_id=1, source_target_pairs={{0,1},{1,2},{2,3},{3,4},{4,5},{5,6},{6,7},{7,8},{8,9},{9,10},{10,1... | collective-permute-start | bytes 454664 | tf_op jit(solution)/shard_map/ppermute | solution.py:447
  29.1 0.7 pad_maximum_fusion.1
  29.9 5.8 %collective-permute-done.2.left_ref = bf16[74,8,128]{2,1,0:T(8,128)(2,1)S(1)} collective-permute-done((bf16[74,8,128]{2,1,0:T(8,128)(2,1)}, bf16[74,8,128]{2,1,0:T(8,128)(2,1)S(1)}, u32[]{:S(2)}, u32[]{:S(2)}) %collective-permute-start.2) | collective-permute-done | bytes 151584 | tf_op jit(solution)/shard_map/ppermute | solution.py:447
  35.7 4.7 %collective-permute-done.3.right_ref = bf16[74,8,128]{2,1,0:T(8,128)(2,1)S(1)} collective-permute-done((bf16[74,8,128]{2,1,0:T(8,128)(2,1)}, bf16[74,8,128]{2,1,0:T(8,128)(2,1)S(1)}, u32[]{:S(2)}, u32[]{:S(2)}) %collective-permute-start.3) | collective-permute-done | bytes 151584 | tf_op jit(solution)/shard_map/ppermute | solution.py:448
  40.4 5.7 %prep.1 = (bf16[74,128,384]{2,1,0:T(8,128)(2,1)S(1)}, bf16[384,640]{1,0:T(8,128)(2,1)S(1)}) custom-call(bf16[64,128,128]{2,1,0:T(8,128)(2,1)S(1)} %copy-done.4, bf16[5,128,128]{2,1,0:T(8,128)(2,1)S(1)} %collective-permute-done.above_ref, bf16[5,128,128]{2,1,0:T(8,128)(2,1)S(1)} %collective-permute-done.1.below_ref, ...), custom_call_target="tpu_custom_call" | custom-call | flops 2500000000 | bytes 10000000 | tf_op jit(solution)/shard_map/prep/pallas_call | solution.py:150
  46.1 2.9 %copy-done.8 = bf16[74,128,384]{2,1,0:T(8,128)(2,1)} copy-done((bf16[74,128,384]{2,1,0:T(8,128)(2,1)}, bf16[74,128,384]{2,1,0:T(8,128)(2,1)S(1)}, u32[]{:S(2)}) %copy-start.8) | copy-done | bytes 7274520
  49.0 0.8 copy-done.9
  49.8 1.0 copy-done.10
  50.8 28.6 %scatter.1 = (bf16[72,136,128]{2,1,0:T(8,128)(2,1)S(1)}, bf16[4,136,128]{2,1,0:T(8,128)(2,1)S(1)}, bf16[5,136,128]{2,1,0:T(8,128)(2,1)S(1)}, bf16[2048,128]{1,0:T(8,128)(2,1)}) custom-call(s32[2]{0:T(128)S(1)} %pad_add_fusion.edge_ref, bf16[128,24,128]{2,1,0:T(8,128)(2,1)S(1)} %all-to-all-done.in_ref, bf16[74,128,384]{2,1,0:T(8,128)(2,1)} %copy-done.8, ...), custom_call_target="tpu_custom_call" | custom-call | flops 8200000000 | bytes 12000000 | tf_op jit(solution)/shard_map/scatter/pallas_call | solution.py:292
  79.3 1.5 %copy-done = bf16[72,136,128]{2,1,0:T(8,128)(2,1)} copy-done((bf16[72,136,128]{2,1,0:T(8,128)(2,1)}, bf16[72,136,128]{2,1,0:T(8,128)(2,1)S(1)}, u32[]{:S(2)}) %copy-start) | copy-done | bytes 2506776
  80.8 8.1 %all-to-all-start.1 = ((bf16[128,16,128]{2,1,0:T(8,128)(2,1)}), bf16[128,16,128]{2,1,0:T(8,128)(2,1)S(1)}, u32[]{:S(2)}, u32[]{:S(2)}) async-start(bf16[128,16,128]{2,1,0:T(8,128)(2,1)} %bitcast.6), calls=%async_computation.1 | async-start | bytes 1048576 | tf_op jit(solution)/shard_map/all_to_all | solution.py:478
  88.9 3.3 %collective-permute-start.4 = (bf16[5,136,128]{2,1,0:T(8,128)(2,1)S(1)}, bf16[5,136,128]{2,1,0:T(8,128)(2,1)S(1)}, u32[]{:S(2)}, u32[]{:S(2)}) collective-permute-start(bf16[5,136,128]{2,1,0:T(8,128)(2,1)S(1)} %get-tuple-element.13), channel_id=1, source_target_pairs={{0,16},{16,32},{32,48},{48,64},{64,80},{80,96},{96,112},{1,17},{17... | collective-permute-start | bytes 522248 | tf_op jit(solution)/shard_map/ppermute | solution.py:447
  92.2 1.3 collective-permute-start.5
  93.5 9.5 %all-to-all-done.1.in_ref = bf16[128,16,128]{2,1,0:T(8,128)(2,1)S(1)} async-done(((bf16[128,16,128]{2,1,0:T(8,128)(2,1)}), bf16[128,16,128]{2,1,0:T(8,128)(2,1)S(1)}, u32[]{:S(2)}, u32[]{:S(2)}) %all-to-all-start.1) | async-done | bytes 524320 | tf_op jit(solution)/shard_map/all_to_all | solution.py:478
  103.0 0.8 copy-done.11
  103.8 2.0 %share.1 = bf16[128,16,128]{2,1,0:T(8,128)(2,1)} custom-call(bf16[128,16,128]{2,1,0:T(8,128)(2,1)} %copy-done.11), custom_call_target="tpu_custom_call" | custom-call | flops 300000 | bytes 1000000 | tf_op jit(solution)/shard_map/share/pallas_call | solution.py:433
  105.8 4.9 %all-to-all-start.2 = ((bf16[128,16,128]{2,1,0:T(8,128)(2,1)}), bf16[128,16,128]{2,1,0:T(8,128)(2,1)}, u32[]{:S(2)}, u32[]{:S(2)}) async-start(bf16[128,16,128]{2,1,0:T(8,128)(2,1)} %share.1), calls=%async_computation.2 | async-start | bytes 1048576 | tf_op jit(solution)/shard_map/all_to_all | solution.py:482
  111.5 2.6 %sides.1 = (bf16[66,8,128]{2,1,0:T(8,128)(2,1)}, bf16[66,8,128]{2,1,0:T(8,128)(2,1)}) custom-call(bf16[72,136,128]{2,1,0:T(8,128)(2,1)} %copy-done, bf16[5,136,128]{2,1,0:T(8,128)(2,1)} %copy-done.2, bf16[4,136,128]{2,1,0:T(8,128)(2,1)} %copy-done.5), custom_call_target="tpu_custom_call" | custom-call | flops 1000000 | bytes 1000000 | tf_op jit(solution)/shard_map/sides/pallas_call | solution.py:344
  114.1 3.2 %collective-permute-start.6 = (bf16[66,8,128]{2,1,0:T(8,128)(2,1)}, bf16[66,8,128]{2,1,0:T(8,128)(2,1)S(1)}, u32[]{:S(2)}, u32[]{:S(2)}) collective-permute-start(bf16[66,8,128]{2,1,0:T(8,128)(2,1)} %get-tuple-element.15), channel_id=1, source_target_pairs={{0,1},{1,2},{2,3},{3,4},{4,5},{5,6},{6,7},{7,8},{8,9},{9,10},{10,1... | collective-permute-start | bytes 405512 | tf_op jit(solution)/shard_map/ppermute | solution.py:447
  117.2 2.3 %collective-permute-done.6.left_ref = bf16[66,8,128]{2,1,0:T(8,128)(2,1)S(1)} collective-permute-done((bf16[66,8,128]{2,1,0:T(8,128)(2,1)}, bf16[66,8,128]{2,1,0:T(8,128)(2,1)S(1)}, u32[]{:S(2)}, u32[]{:S(2)}) %collective-permute-start.6) | collective-permute-done | bytes 135200 | tf_op jit(solution)/shard_map/ppermute | solution.py:447
  119.5 4.2 %collective-permute-done.7.right_ref = bf16[66,8,128]{2,1,0:T(8,128)(2,1)S(1)} collective-permute-done((bf16[66,8,128]{2,1,0:T(8,128)(2,1)}, bf16[66,8,128]{2,1,0:T(8,128)(2,1)S(1)}, u32[]{:S(2)}, u32[]{:S(2)}) %collective-permute-start.7) | collective-permute-done | bytes 135200 | tf_op jit(solution)/shard_map/ppermute | solution.py:448
  123.8 0.9 copy-done.3
  124.7 0.9 copy-done.6
  125.6 7.1 %conv.1 = bf16[64,128,128]{2,1,0:T(8,128)(2,1)} custom-call(bf16[72,136,128]{2,1,0:T(8,128)(2,1)S(1)} %copy-done.1, bf16[5,136,128]{2,1,0:T(8,128)(2,1)S(1)} %copy-done.3, bf16[4,136,128]{2,1,0:T(8,128)(2,1)S(1)} %copy-done.6, bf16[66,8,128]{2,1,0:T(8,128)(2,1)S(1)} %collective-permute-done.6.left_ref, ...), custom_call_target="tpu_custom_call" | custom-call | flops 2700000000 | bytes 4500000 | tf_op jit(solution)/shard_map/conv/pallas_call | solution.py:411
  132.7 1.0 slice.41
  133.7 0.9 convert.1
  (29 shorter events, 0.9 us)
Async XLA Ops:
  1.7 23.6 %copy-start.4 = (bf16[64,128,128]{2,1,0:T(8,128)(2,1)S(1)}, bf16[64,128,128]{2,1,0:T(8,128)(2,1)}, u32[]{:S(2)}) copy-start(bf16[64,128,128]{2,1,0:T(8,128)(2,1)} %feat_ref.1) | copy-start | bytes 6291460
  1.7 23.6 %collective-permute-start.1 = (bf16[5,128,128]{2,1,0:T(8,128)(2,1)S(1)}, bf16[5,128,128]{2,1,0:T(8,128)(2,1)S(1)}, u32[]{:S(2)}, u32[]{:S(2)}) collective-permute-start(bf16[5,128,128]{2,1,0:T(8,128)(2,1)S(1)} %get-tuple-element.20), channel_id=1, source_target_pairs={{16,0},{32,16},{48,32},{64,48},{80,64},{96,80},{112,96},{17,1},{33... | collective-permute-start | bytes 491528 | tf_op jit(solution)/shard_map/ppermute | solution.py:448
  3.1 22.2 %collective-permute-start = (bf16[5,128,128]{2,1,0:T(8,128)(2,1)S(1)}, bf16[5,128,128]{2,1,0:T(8,128)(2,1)S(1)}, u32[]{:S(2)}, u32[]{:S(2)}) collective-permute-start(bf16[5,128,128]{2,1,0:T(8,128)(2,1)S(1)} %get-tuple-element.21), channel_id=1, source_target_pairs={{0,16},{16,32},{32,48},{48,64},{64,80},{80,96},{96,112},{1,17},{17... | collective-permute-start | bytes 491528 | tf_op jit(solution)/shard_map/ppermute | solution.py:447
  11.9 37.9 %all-to-all-start = ((bf16[128,24,128]{2,1,0:T(8,128)(2,1)}), bf16[128,24,128]{2,1,0:T(8,128)(2,1)S(1)}, u32[]{:S(2)}, u32[]{:S(2)}) async-start(bf16[128,24,128]{2,1,0:T(8,128)(2,1)} %pack.1), calls=%async_computation | async-start | bytes 1572864 | tf_op jit(solution)/shard_map/all_to_all | solution.py:469
  26.0 9.7 %collective-permute-start.2 = (bf16[74,8,128]{2,1,0:T(8,128)(2,1)}, bf16[74,8,128]{2,1,0:T(8,128)(2,1)S(1)}, u32[]{:S(2)}, u32[]{:S(2)}) collective-permute-start(bf16[74,8,128]{2,1,0:T(8,128)(2,1)} %pad_maximum_fusion), channel_id=1, source_target_pairs={{0,1},{1,2},{2,3},{3,4},{4,5},{5,6},{6,7},{7,8},{8,9},{9,10},{10,1... | collective-permute-start | bytes 454664 | tf_op jit(solution)/shard_map/ppermute | solution.py:447
  29.8 10.5 %collective-permute-start.3 = (bf16[74,8,128]{2,1,0:T(8,128)(2,1)}, bf16[74,8,128]{2,1,0:T(8,128)(2,1)S(1)}, u32[]{:S(2)}, u32[]{:S(2)}) collective-permute-start(bf16[74,8,128]{2,1,0:T(8,128)(2,1)} %pad_maximum_fusion.1), channel_id=1, source_target_pairs={{1,0},{2,1},{3,2},{4,3},{5,4},{6,5},{7,6},{8,7},{9,8},{10,9},{11,1... | collective-permute-start | bytes 454664 | tf_op jit(solution)/shard_map/ppermute | solution.py:448
  46.1 2.9 %copy-start.8 = (bf16[74,128,384]{2,1,0:T(8,128)(2,1)}, bf16[74,128,384]{2,1,0:T(8,128)(2,1)S(1)}, u32[]{:S(2)}) copy-start(bf16[74,128,384]{2,1,0:T(8,128)(2,1)S(1)} %get-tuple-element.10.feat_ref) | copy-start | bytes 21823492
  49.0 0.8 copy-start.9
  49.8 1.0 copy-start.10
  79.3 1.5 %copy-start = (bf16[72,136,128]{2,1,0:T(8,128)(2,1)}, bf16[72,136,128]{2,1,0:T(8,128)(2,1)S(1)}, u32[]{:S(2)}) copy-start(bf16[72,136,128]{2,1,0:T(8,128)(2,1)S(1)} %get-tuple-element.12.canvas_ref) | copy-start | bytes 7520260
  80.8 22.2 %all-to-all-start.1 = ((bf16[128,16,128]{2,1,0:T(8,128)(2,1)}), bf16[128,16,128]{2,1,0:T(8,128)(2,1)S(1)}, u32[]{:S(2)}, u32[]{:S(2)}) async-start(bf16[128,16,128]{2,1,0:T(8,128)(2,1)} %bitcast.6), calls=%async_computation.1 | async-start | bytes 1048576 | tf_op jit(solution)/shard_map/all_to_all | solution.py:478
  88.9 21.8 %collective-permute-start.4 = (bf16[5,136,128]{2,1,0:T(8,128)(2,1)S(1)}, bf16[5,136,128]{2,1,0:T(8,128)(2,1)S(1)}, u32[]{:S(2)}, u32[]{:S(2)}) collective-permute-start(bf16[5,136,128]{2,1,0:T(8,128)(2,1)S(1)} %get-tuple-element.13), channel_id=1, source_target_pairs={{0,16},{16,32},{32,48},{48,64},{64,80},{80,96},{96,112},{1,17},{17... | collective-permute-start | bytes 522248 | tf_op jit(solution)/shard_map/ppermute | solution.py:447
  92.2 18.5 %collective-permute-start.5 = (bf16[4,136,128]{2,1,0:T(8,128)(2,1)S(1)}, bf16[4,136,128]{2,1,0:T(8,128)(2,1)S(1)}, u32[]{:S(2)}, u32[]{:S(2)}) collective-permute-start(bf16[4,136,128]{2,1,0:T(8,128)(2,1)S(1)} %get-tuple-element.14), channel_id=1, source_target_pairs={{16,0},{32,16},{48,32},{64,48},{80,64},{96,80},{112,96},{17,1},{33... | collective-permute-start | bytes 417800 | tf_op jit(solution)/shard_map/ppermute | solution.py:448
  103.0 0.8 copy-start.11
  105.8 17.9 %copy-start.1 = (bf16[72,136,128]{2,1,0:T(8,128)(2,1)S(1)}, bf16[72,136,128]{2,1,0:T(8,128)(2,1)}, u32[]{:S(2)}) copy-start(bf16[72,136,128]{2,1,0:T(8,128)(2,1)} %copy-done) | copy-start | bytes 7520260
  105.8 17.9 %copy-start.7 = (bf16[3,3,128,128]{3,2,1,0:T(8,128)(2,1)S(1)}, bf16[3,3,128,128]{3,2,1,0:T(8,128)(2,1)}, u32[]{:S(2)}) copy-start(bf16[3,3,128,128]{3,2,1,0:T(8,128)(2,1)} %weight_ref.1) | copy-start | bytes 884740
  105.8 26.9 %all-to-all-start.2 = ((bf16[128,16,128]{2,1,0:T(8,128)(2,1)}), bf16[128,16,128]{2,1,0:T(8,128)(2,1)}, u32[]{:S(2)}, u32[]{:S(2)}) async-start(bf16[128,16,128]{2,1,0:T(8,128)(2,1)} %share.1), calls=%async_computation.2 | async-start | bytes 1048576 | tf_op jit(solution)/shard_map/all_to_all | solution.py:482
  110.8 0.7 copy-start.5
  110.8 0.7 copy-start.2
  114.1 5.5 %collective-permute-start.6 = (bf16[66,8,128]{2,1,0:T(8,128)(2,1)}, bf16[66,8,128]{2,1,0:T(8,128)(2,1)S(1)}, u32[]{:S(2)}, u32[]{:S(2)}) collective-permute-start(bf16[66,8,128]{2,1,0:T(8,128)(2,1)} %get-tuple-element.15), channel_id=1, source_target_pairs={{0,1},{1,2},{2,3},{3,4},{4,5},{5,6},{6,7},{7,8},{8,9},{9,10},{10,1... | collective-permute-start | bytes 405512 | tf_op jit(solution)/shard_map/ppermute | solution.py:447
  117.2 6.6 %collective-permute-start.7 = (bf16[66,8,128]{2,1,0:T(8,128)(2,1)}, bf16[66,8,128]{2,1,0:T(8,128)(2,1)S(1)}, u32[]{:S(2)}, u32[]{:S(2)}) collective-permute-start(bf16[66,8,128]{2,1,0:T(8,128)(2,1)} %get-tuple-element.16), channel_id=1, source_target_pairs={{1,0},{2,1},{3,2},{4,3},{5,4},{6,5},{7,6},{8,7},{9,8},{10,9},{11,1... | collective-permute-start | bytes 405512 | tf_op jit(solution)/shard_map/ppermute | solution.py:448
  123.8 0.9 copy-start.3
  124.7 0.9 copy-start.6

commit v3 on v2

--- a/solution.py
+++ b/solution.py
@@ -13,6 +13,7 @@
 SLOTS = 16
 CHUNK = 24
 TILES = 128
+MOST_VMEM = 62_600_000
 GAUSS = 2.0 * 1.5 * 1.5
 
 
@@ -94,84 +95,100 @@
     return jnp.where((tap >= 0.0) & (tap <= 7.0), weight, 0.0)
 
 
-def prep_kernel(feat_ref, above_ref, below_ref, left_ref, right_ref, out_ref, side_ref):
-    eye = jnp.where(
+def column_shift():
+    spot = lax.broadcasted_iota(jnp.int32, (128, 384), 0)
+    want = lax.broadcasted_iota(jnp.int32, (128, 384), 1)
+    want = want % 128 + want // 128 - 1
+    return jnp.where(spot == want, 1.0, 0.0).astype(BF16)
+
+
+def identity():
+    return jnp.where(
         lax.broadcasted_iota(jnp.int32, (128, 128), 0)
         == lax.broadcasted_iota(jnp.int32, (128, 128), 1),
         1.0,
         0.0,
     ).astype(BF16)
-    spot = lax.broadcasted_iota(jnp.int32, (144, 384), 0)
-    want = lax.broadcasted_iota(jnp.int32, (144, 384), 1)
-    want = want % 128 + want // 128 - 1
-    want = jnp.where(want < 0, 135, jnp.where(want == 128, 136, want))
-    shift = jnp.where(spot == want, 1.0, 0.0).astype(BF16)
-
-    def lines(take, start, count):
-        turned = []
-        for i in range(count):
-            ext = jnp.concatenate(
-                [take(i), jnp.concatenate([left_ref[start + i], right_ref[start + i]], axis=0)],
-                axis=0,
-            )
-            turned.append(nt(eye, ext).astype(BF16))
-        moved = mm(jnp.concatenate(turned, axis=0), shift).astype(BF16)
-        out_ref[pl.ds(start, count)] = moved.reshape(count, 128, 384)
-
-    lines(lambda i: above_ref[i], 0, 5)
-
-    def body(step, carry):
-        lines(lambda i: feat_ref[step * 8 + i], step * 8 + 5, 8)
-        return carry
-
-    lax.fori_loop(0, 8, body, 0)
-    lines(lambda i: below_ref[i], 69, 5)
+
+
+def turn_lines(lines, eye, shift):
+    turned = jnp.concatenate([nt(eye, x).astype(BF16) for x in lines], axis=0)
+    moved = mm(turned, shift).astype(BF16)
+    return [moved[:, b * 128 : (b + 1) * 128].reshape(len(lines), 128, 128) for b in range(3)]
+
+
+def prep_kernel(feat_ref, out_ref):
+    moved = turn_lines([feat_ref[i] for i in range(8)], identity(), column_shift())
+    for b in range(3):
+        out_ref[b] = moved[b]
+
+
+def prep(features):
+    return pl.pallas_call(
+        prep_kernel,
+        grid=(8,),
+        out_shape=jax.ShapeDtypeStruct((3, 64, 128, 128), BF16),
+        in_specs=[pl.BlockSpec((8, 128, 128), lambda i: (i, 0, 0))],
+        out_specs=pl.BlockSpec((3, 8, 128, 128), lambda i: (0, i, 0, 0)),
+        cost_estimate=pl.CostEstimate(
+            flops=2_200_000_000, bytes_accessed=8_000_000, transcendentals=0
+        ),
+        name="prep",
+    )(features)
+
+
+def prep_edge_kernel(head_ref, last_ref, above_ref, below_ref, left_ref, right_ref, out_ref, side_ref):
+    eye = identity()
+    shift = column_shift()
+    moved = turn_lines(
+        [above_ref[i] for i in range(5)] + [below_ref[i] for i in range(5)], eye, shift
+    )
+    for b in range(3):
+        out_ref[b] = moved[b]
     left = left_ref[...].astype(F32)
     right = right_ref[...].astype(F32)
-    first = jnp.concatenate(
-        [above_ref[:, 0:8, :], feat_ref[:, 0:8, :], below_ref[:, 0:8, :]], axis=0
-    ).astype(F32)
-    last = jnp.concatenate(
-        [above_ref[:, 120:128, :], feat_ref[:, 120:128, :], below_ref[:, 120:128, :]], axis=0
-    ).astype(F32)
+    first = head_ref[...].astype(F32)
+    last = last_ref[...].astype(F32)
+    none = jnp.zeros((74, 8, 128), F32)
     groups = (
-        (left[:, 3:7], last[:, 7:8], right[:, 0:3]),
-        (left[:, 4:8], right[:, 0:4]),
-        (left[:, 5:8], first[:, 0:1], right[:, 1:5]),
+        (left[:, 3:7], last[:, 7:8], right[:, 0:3], left[:, 7:8], none[:, :7]),
+        (left[:, 4:8], right[:, 0:4], none),
+        (left[:, 5:8], first[:, 0:1], right[:, 1:5], none[:, :1], right[:, 0:1], none[:, :6]),
     )
     for b in range(3):
-        eight = jnp.concatenate(groups[b], axis=1).reshape(592, 128)
-        eight = jnp.concatenate([eight, jnp.zeros((48, 128), F32)], axis=0)
-        side_ref[b * 128 : (b + 1) * 128, :] = eight.T.astype(BF16)
-
-
-def prep(features, above, below, left, right):
+        cells = jnp.concatenate(groups[b], axis=1).reshape(1184, 128)
+        cells = jnp.concatenate([cells, jnp.zeros((96, 128), F32)], axis=0).astype(BF16)
+        side_ref[b * 128 : (b + 1) * 128, :] = nt(eye, cells).astype(BF16)
+
+
+def prep_edge(head, last, above, below, left, right):
     vmem = pl.BlockSpec(memory_space=pltpu.VMEM)
     return pl.pallas_call(
-        prep_kernel,
+        prep_edge_kernel,
         out_shape=(
-            jax.ShapeDtypeStruct((74, 128, 384), BF16),
-            jax.ShapeDtypeStruct((384, 640), BF16),
+            jax.ShapeDtypeStruct((3, 10, 128, 128), BF16),
+            jax.ShapeDtypeStruct((384, 1280), BF16),
         ),
-        in_specs=[vmem] * 5,
+        in_specs=[vmem] * 6,
         out_specs=(vmem, vmem),
-        compiler_params=pltpu.CompilerParams(vmem_limit_bytes=24 << 20),
         cost_estimate=pl.CostEstimate(
-            flops=2_500_000_000, bytes_accessed=10_000_000, transcendentals=0
+            flops=500_000_000, bytes_accessed=3_000_000, transcendentals=0
         ),
-        name="prep",
-    )(features, above, below, left, right)
+        name="prep_edge",
+    )(head, last, above, below, left, right)
 
 
 def scatter_kernel(
     edge_ref,
     in_ref,
-    feat_ref,
-    feat_side_ref,
-    canvas_ref,
-    up_ref,
-    down_ref,
-    sum_ref,
+    feat_hbm,
+    feat_edge_hbm,
+    feat_side_hbm,
+    canvas_hbm,
+    rim_hbm,
+    up_hbm,
+    down_hbm,
+    sum_hbm,
     rows_ref,
     lat_w,
     lon_w,
@@ -179,7 +196,22 @@
     three,
     three_side,
     acc_ref,
+    feat_ref,
+    feat_edge_ref,
+    feat_side_ref,
+    canvas_ref,
+    rim_ref,
+    sum_ref,
+    load_sem,
+    store_sem,
 ):
+    loads = [
+        pltpu.make_async_copy(feat_hbm, feat_ref, load_sem.at[0]),
+        pltpu.make_async_copy(feat_edge_hbm, feat_edge_ref, load_sem.at[1]),
+        pltpu.make_async_copy(feat_side_hbm, feat_side_ref, load_sem.at[2]),
+    ]
+    for copy in loads:
+        copy.start()
     total = TILES * SLOTS
     rows_ref[...] = in_ref[:, 0:SLOTS, :].reshape(total, 128)
     tail = in_ref[:, SLOTS:CHUNK, :].reshape(TILES * (CHUNK - SLOTS), 128)
@@ -224,19 +256,12 @@
     three_side[...] = jnp.zeros_like(three_side)
     acc_ref[...] = jnp.zeros_like(acc_ref)
 
-    def weight_part(start, count):
-        parts = []
-        for b in range(3):
-            parts.append(
-                jnp.concatenate(
-                    [feat_ref[start + i, :, b * 128 : (b + 1) * 128] for i in range(count)],
-                    axis=1,
-                )
-            )
-        acc_ref[...] += mm(
-            jnp.concatenate(parts, axis=0),
-            three[pl.ds(start, count)].reshape(count * 128, 384),
-        )
+    def weight_part(take, at):
+        lhs = jnp.concatenate([jnp.concatenate(take(b), axis=1) for b in range(3)], axis=0)
+        rhs = jnp.concatenate(
+            [three[x:y].reshape((y - x) * 128, 384) for x, y in at], axis=0
+        )
+        acc_ref[...] += mm(lhs, rhs)
 
     def eight_lines(step, carry):
         start = pl.multiple_of(step * 8, 8)
@@ -265,15 +290,36 @@
             three[pl.ds(start + a, 8), :, a * 128 : (a + 1) * 128] = main
         side = side.reshape(8, 8, 128)
         canvas_ref[pl.ds(start, 8), 128:136, :] = side.astype(BF16)
+        ends = acc.reshape(8, 128, 128)
+        side = jnp.concatenate(
+            [side, ends[:, 0:1], ends[:, 127:128], jnp.zeros((8, 6, 128), F32)], axis=1
+        )
         for a in range(3):
             three_side[pl.ds(start + a, 8), :, a * 128 : (a + 1) * 128] = side
-        weight_part(start, 8)
+        rim_ref[pl.ds(start, 8), 0:8, :] = ends[:, 0:8].astype(BF16)
+        rim_ref[pl.ds(start, 8), 8:16, :] = ends[:, 120:128].astype(BF16)
+        rim_ref[pl.ds(start, 8), 16:24, :] = side[:, 0:8].astype(BF16)
         return carry
 
     lax.fori_loop(0, 9, eight_lines, 0)
-    weight_part(72, 2)
+    stores = [
+        pltpu.make_async_copy(canvas_ref, canvas_hbm, store_sem.at[0]),
+        pltpu.make_async_copy(rim_ref, rim_hbm, store_sem.at[1]),
+        pltpu.make_async_copy(canvas_ref.at[1:5], up_hbm, store_sem.at[2]),
+        pltpu.make_async_copy(canvas_ref.at[67:72], down_hbm, store_sem.at[3]),
+    ]
+    for copy in stores:
+        copy.start()
+    for copy in loads:
+        copy.wait()
+    for part in range(2):
+        weight_part(
+            lambda b: [feat_ref[b, part * 32 + i] for i in range(32)],
+            ((5 + part * 32, 37 + part * 32),),
+        )
+    weight_part(lambda b: [feat_edge_ref[b, i] for i in range(10)], ((0, 5), (69, 74)))
     acc = acc_ref[...] + mm(
-        feat_side_ref[...], three_side[...].reshape(640, 384).astype(BF16)
+        feat_side_ref[...], three_side[...].reshape(1280, 384).astype(BF16)
     )
     for a in range(3):
         for b in range(3):
@@ -282,55 +328,68 @@
                 b * 128 : (b + 1) * 128, a * 128 : (a + 1) * 128
             ].astype(BF16)
     sum_ref[1152:, :] = jnp.zeros((2048 - 1152, 128), BF16)
-    up_ref[...] = canvas_ref[1:5]
-    down_ref[...] = canvas_ref[67:72]
-
-
-def scatter(edge, incoming, feat, feat_side):
+    last = pltpu.make_async_copy(sum_ref, sum_hbm, store_sem.at[4])
+    last.start()
+    for copy in stores:
+        copy.wait()
+    last.wait()
+
+
+def scatter(edge, incoming, feat, feat_edge, feat_side):
     vmem = pl.BlockSpec(memory_space=pltpu.VMEM)
+    hbm = pl.BlockSpec(memory_space=pltpu.HBM)
     total = TILES * SLOTS
     return pl.pallas_call(
         scatter_kernel,
         out_shape=(
             jax.ShapeDtypeStruct((72, 136, 128), BF16),
+            jax.ShapeDtypeStruct((72, 24, 128), BF16),
             jax.ShapeDtypeStruct((4, 136, 128), BF16),
             jax.ShapeDtypeStruct((5, 136, 128), BF16),
             jax.ShapeDtypeStruct((2048, 128), BF16),
         ),
-        in_specs=[pl.BlockSpec(memory_space=pltpu.SMEM), vmem, vmem, vmem],
-        out_specs=(vmem,) * 4,
+        in_specs=[pl.BlockSpec(memory_space=pltpu.SMEM), vmem] + [hbm] * 3,
+        out_specs=(hbm,) * 5,
         scratch_shapes=[
             pltpu.VMEM((total, 128), BF16),
             pltpu.VMEM((72, total), F32),
             pltpu.VMEM((128, total), BF16),
             pltpu.VMEM((8, total), F32),
             pltpu.VMEM((74, 128, 384), BF16),
-            pltpu.VMEM((80, 8, 384), F32),
+            pltpu.VMEM((80, 16, 384), F32),
             pltpu.VMEM((384, 384), F32),
+            pltpu.VMEM((3, 64, 128, 128), BF16),
+            pltpu.VMEM((3, 10, 128, 128), BF16),
+            pltpu.VMEM((384, 1280), BF16),
+            pltpu.VMEM((72, 136, 128), BF16),
+            pltpu.VMEM((72, 24, 128), BF16),
+            pltpu.VMEM((2048, 128), BF16),
+            pltpu.SemaphoreType.DMA((3,)),
+            pltpu.SemaphoreType.DMA((5,)),
         ],
-        compiler_params=pltpu.CompilerParams(vmem_limit_bytes=44 << 20),
+        compiler_params=pltpu.CompilerParams(vmem_limit_bytes=MOST_VMEM),
         cost_estimate=pl.CostEstimate(
             flops=8_200_000_000, bytes_accessed=12_000_000, transcendentals=500_000
         ),
         name="scatter",
-    )(edge, incoming, feat, feat_side)
-
-
-def sides_kernel(canvas_ref, above_ref, below_ref, right_ref, left_ref):
-    def tall(cols):
-        block = canvas_ref[3:69, cols, :].astype(F32)
+    )(edge, incoming, feat, feat_edge, feat_side)
+
+
+def sides_kernel(rim_ref, above_ref, below_ref, right_ref, left_ref):
+    def tall(at, cols):
+        block = rim_ref[3:69, at : at + 8, :].astype(F32)
         return jnp.concatenate(
             [
-                block[0:5] + above_ref[:, cols, :].astype(F32),
+                block[0:5] + above_ref[:, cols : cols + 8, :].astype(F32),
                 block[5:62],
-                block[62:66] + below_ref[:, cols, :].astype(F32),
+                block[62:66] + below_ref[:, cols : cols + 8, :].astype(F32),
             ],
             axis=0,
         )
 
-    side = tall(slice(128, 136))
-    last = tall(slice(120, 128))
-    head = tall(slice(0, 8))
+    head = tall(0, 0)
+    last = tall(8, 120)
+    side = tall(16, 128)
     blank = jnp.zeros((66, 4, 128), F32)
     right_ref[...] = jnp.concatenate([last[:, 7:8], side[:, 4:8], blank[:, :3]], axis=1).astype(
         BF16
@@ -338,7 +397,7 @@
     left_ref[...] = jnp.concatenate([side[:, 1:4], head[:, 0:1], blank], axis=1).astype(BF16)
 
 
-def sides(canvas, above, below):
+def sides(rim, above, below):
     vmem = pl.BlockSpec(memory_space=pltpu.VMEM)
     shape = jax.ShapeDtypeStruct((66, 8, 128), BF16)
     return pl.pallas_call(
@@ -347,8 +406,9 @@
         in_specs=[vmem] * 3,
         out_specs=(vmem, vmem),
         cost_estimate=pl.CostEstimate(flops=1_000_000, bytes_accessed=1_000_000, transcendentals=0),
+        compiler_params=pltpu.CompilerParams(vmem_limit_bytes=4 << 20),
         name="sides",
-    )(canvas, above, below)
+    )(rim, above, below)
 
 
 def conv_kernel(canvas_ref, above_ref, below_ref, left_ref, right_ref, weight_ref, out_ref, grid):
@@ -415,7 +475,7 @@
         in_specs=[whole(x) for x in args],
         out_specs=pl.BlockSpec((8, 128, 128), lambda i: (i, 0, 0)),
         scratch_shapes=[pltpu.VMEM((66, 144, 128), BF16)],
-        compiler_params=pltpu.CompilerParams(vmem_limit_bytes=24 << 20),
+        compiler_params=pltpu.CompilerParams(vmem_limit_bytes=MOST_VMEM),
         cost_estimate=pl.CostEstimate(
             flops=2_700_000_000, bytes_accessed=4_500_000, transcendentals=0
         ),
@@ -436,8 +496,26 @@
         in_specs=[vmem],
         out_specs=vmem,
         cost_estimate=pl.CostEstimate(flops=300_000, bytes_accessed=1_000_000, transcendentals=0),
+        compiler_params=pltpu.CompilerParams(vmem_limit_bytes=3 << 20),
         name="share",
     )(got)
+
+
+def finish_kernel(in_ref, out_ref):
+    out_ref[...] = in_ref[...].reshape(384, 128).astype(F32)
+
+
+def finish(every):
+    return pl.pallas_call(
+        finish_kernel,
+        grid=(3,),
+        out_shape=jax.ShapeDtypeStruct((1152, 128), F32),
+        in_specs=[pl.BlockSpec((24, 16, 128), lambda i: (i, 0, 0))],
+        out_specs=pl.BlockSpec((384, 128), lambda i: (i, 0)),
+        compiler_params=pltpu.CompilerParams(vmem_limit_bytes=2 << 20),
+        cost_estimate=pl.CostEstimate(flops=0, bytes_accessed=900_000, transcendentals=0),
+        name="finish",
+    )(every)
 
 
 def both_ways(forth, back, axis, closed):
@@ -468,20 +546,22 @@
     )
     incoming = lax.all_to_all(outgoing, AXES, 0, 0, tiled=True)
     above, below = both_ways(features[59:64], features[0:5], "lat", False)
-    ends = [
+    last, head = [
         jnp.concatenate([x[:, c : c + 8] for x in (above, features, below)], axis=0)
         for c in (120, 0)
     ]
-    left, right = both_ways(ends[0], ends[1], "lon", True)
-    feat, feat_side = prep(features, above, below, left, right)
-    canvas, up, down, part = scatter(edge, incoming, feat, feat_side)
+    left, right = both_ways(last, head, "lon", True)
+    feat = prep(features)
+    feat_edge, feat_side = prep_edge(head, last, above, below, left, right)
+    canvas, rim, up, down, part = scatter(edge, incoming, feat, feat_edge, feat_side)
     got = lax.all_to_all(part.reshape(TILES, 16, 128), AXES, 0, 0, tiled=True)
     grid_above, grid_below = both_ways(down, up, "lat", False)
-    send_right, send_left = sides(canvas, grid_above, grid_below)
+    send_right, send_left = sides(rim, grid_above, grid_below)
+    got, send_right, send_left = lax.optimization_barrier((got, send_right, send_left))
     from_left, from_right = both_ways(send_right, send_left, "lon", True)
     every = lax.all_to_all(share(got), AXES, 0, 0, tiled=True)
     input_grad = conv(canvas, grid_above, grid_below, from_left, from_right, conv_weight)
-    weight_grad = every.reshape(TILES * 16, 128)[:1152].astype(F32)
+    weight_grad = finish(every)
     return input_grad, weight_grad.reshape(3, 3, 128, 128)
 
 

time: 135 us -> 124 us (0.919); the launches traced: 135 us -> 122 us
  waiting for transfers between devices: 26.5 us -> 18.4 us
  local copies, waits for them, and re-layouts: 11.6 us -> 6.06 us
  starting transfers between devices: 43.3 us -> 48.1 us
  Pallas kernels: 49.4 us -> 47.1 us
  other arithmetic: 2.31 us -> 0.62 us
    pallas_call x1, Pallas kernels: 28.6 us -> 20.1 us  [scatter(): pl.pallas_call(scatter_kernel, out_shape=(jax.ShapeDtypeStruct((72, 136,...]
    all_to_all x1, waiting for transfers between devices: 9.51 us -> 1.35 us  [shards(): got = lax.all_to_all(part.reshape(TILES, 16, 128), AXES, 0, 0, tiled=True)]
    pallas_call x1 -> x3, Pallas kernels: 5.69 us -> 13.3 us  [the longest x1 8.68 us: prep(): pl.pallas_call(prep_kernel, grid=(8,), out_shape=jax.ShapeDtypeStruct((3,...]
    unnamed x24, local copies, waits for them, and re-layouts: 9.51 us -> 4.03 us
    ppermute x4, waiting for transfers between devices: 8.1 us -> 3.71 us  [both_ways(): lax.ppermute(forth, axis, [(i, (i + 1) % count) for i in range(ends)])]
    ppermute x4, waiting for transfers between devices: 8.91 us -> 13.3 us  [both_ways(): lax.ppermute(back, axis, [((i + 1) % count, i) for i in range(ends)])]
    all_to_all x1, starting transfers between devices: 4.9 us -> 9.25 us  [shards(): every = lax.all_to_all(share(got), AXES, 0, 0, tiled=True)]
    pallas_call x1, Pallas kernels: 2.58 us -> 0.13 us  [sides(): pl.pallas_call(sides_kernel, out_shape=(shape, shape), in_specs=[vmem] *...]
  transfers between devices with their start and end apart: 11 -> 11, of which waited for: 5 -> 5; matrix products, arithmetic and copies ran while one was open for 1% -> 1% of each run, Pallas kernels for 15% -> 20%
where the time goes in v3:
time: 124 us; the launch traced here: 122 us
  starting transfers between devices  48.1 us (39%)
  Pallas kernels  47.1 us (38%)
  waiting for transfers between devices  18.4 us (15%)
  local copies, waits for them, and re-layouts  6.06 us (5%)
  between operations  1.47 us (1%)
    pallas_call x1, Pallas kernels, scatter(): pl.pallas_call(scatter_kernel, out_shape=(jax.ShapeDtypeStruct((72, 136,...  20.1 us
    ppermute x4, waiting for transfers between devices, both_ways(): lax.ppermute(back, axis, [((i + 1) % count, i) for i in range(ends)])  13.3 us
    ppermute x4, starting transfers between devices, both_ways(): lax.ppermute(forth, axis, [(i, (i + 1) % count) for i in range(ends)])  12.8 us
    all_to_all x1, starting transfers between devices, shards(): incoming = lax.all_to_all(outgoing, AXES, 0, 0, tiled=True)  12 us
    all_to_all x1, starting transfers between devices, shards(): got = lax.all_to_all(part.reshape(TILES, 16, 128), AXES, 0, 0, tiled=True)  10.3 us
    all_to_all x1, starting transfers between devices, shards(): every = lax.all_to_all(share(got), AXES, 0, 0, tiled=True)  9.25 us
    pallas_call x1, Pallas kernels, conv(): pl.pallas_call(conv_kernel, grid=(8,), out_shape=jax.ShapeDtypeStruct((64...  9.11 us
    pallas_call x1, Pallas kernels, prep(): pl.pallas_call(prep_kernel, grid=(8,), out_shape=jax.ShapeDtypeStruct((3,...  8.68 us
  transfers between devices with their start and end apart: 11, of which 5 were waited for; matrix products, arithmetic and copies ran while one was open for 1% of the time, Pallas kernels for 20%

profile of v3, /device:TPU:1, one launch (start us, length us, event | category | flops | bytes accessed | tf_op | source)
XLA Modules:
  0.0 121.7 jit_solution(1410931218836494125)
XLA Ops:
  0.6 1.0 fusion.1
  1.7 4.0 %collective-permute-start = (bf16[5,128,128]{2,1,0:T(8,128)(2,1)S(1)}, bf16[5,128,128]{2,1,0:T(8,128)(2,1)S(1)}, u32[]{:S(2)}, u32[]{:S(2)}) collective-permute-start(bf16[5,128,128]{2,1,0:T(8,128)(2,1)S(1)} %get-tuple-element.28), channel_id=1, source_target_pairs={{0,16},{16,32},{32,48},{48,64},{64,80},{80,96},{96,112},{1,17},{17... | collective-permute-start | bytes 491528 | tf_op jit(solution)/shard_map/ppermute | solution.py:525
  5.7 1.3 %collective-permute-start.1 = (bf16[5,128,128]{2,1,0:T(8,128)(2,1)S(1)}, bf16[5,128,128]{2,1,0:T(8,128)(2,1)S(1)}, u32[]{:S(2)}, u32[]{:S(2)}) collective-permute-start(bf16[5,128,128]{2,1,0:T(8,128)(2,1)S(1)} %get-tuple-element.29), channel_id=1, source_target_pairs={{16,0},{32,16},{48,32},{64,48},{80,64},{96,80},{112,96},{17,1},{33... | collective-permute-start | bytes 491528 | tf_op jit(solution)/shard_map/ppermute | solution.py:526
  7.6 3.5 %pack.1 = bf16[128,24,128]{2,1,0:T(8,128)(2,1)} custom-call(s32[1]{0:T(128)S(6)} %copy.10.live_ref, s32[1,1024]{1,0:T(1,128)} %bitcast.10, s32[1,1024]{1,0:T(1,128)} %bitcast.11, s32[1,1024]{1,0:T(1,128)} %bitcast.12, bf16[2,1024]{1,0:T(2,128)(2,1)} %bitcast.13, bf16[1024,128]{1,0:T(8,128)(2,1)} %rows_ref.1), custom_call_target="tpu_custom_call" | custom-call | flops 700000000 | bytes 1500000 | tf_op jit(solution)/shard_map/pack/pallas_call | solution.py:81
  11.1 12.0 %all-to-all-start = ((bf16[128,24,128]{2,1,0:T(8,128)(2,1)}), bf16[128,24,128]{2,1,0:T(8,128)(2,1)S(1)}, u32[]{:S(2)}, u32[]{:S(2)}) async-start(bf16[128,24,128]{2,1,0:T(8,128)(2,1)} %pack.1), calls=%async_computation | async-start | bytes 1572864 | tf_op jit(solution)/shard_map/all_to_all | solution.py:547
  23.2 1.0 fusion
  24.2 0.0 copy-start.6
  24.3 1.1 collective-permute-start.3
  25.4 2.3 %collective-permute-start.2 = (bf16[74,8,128]{2,1,0:T(8,128)(2,1)S(1)}, bf16[74,8,128]{2,1,0:T(8,128)(2,1)S(1)}, u32[]{:S(2)}, u32[]{:S(2)}) collective-permute-start(bf16[74,8,128]{2,1,0:T(8,128)(2,1)S(1)} %pad_maximum_fusion.1.last_ref), channel_id=1, source_target_pairs={{0,1},{1,2},{2,3},{3,4},{4,5},{5,6},{6,7},{7,8},{8,9},{9,10},{10,1... | collective-permute-start | bytes 454664 | tf_op jit(solution)/shard_map/ppermute | solution.py:525
  27.7 8.7 %prep.1.feat_hbm = bf16[3,64,128,128]{3,2,1,0:T(8,128)(2,1)} custom-call(bf16[64,128,128]{2,1,0:T(8,128)(2,1)} %feat_ref.1), custom_call_target="tpu_custom_call" | custom-call | flops 2200000000 | bytes 8000000 | tf_op jit(solution)/shard_map/prep/pallas_call | solution.py:127
  36.4 0.6 pad_add_fusion.edge_ref
  37.0 1.3 %collective-permute-done.3.right_ref = bf16[74,8,128]{2,1,0:T(8,128)(2,1)S(1)} collective-permute-done((bf16[74,8,128]{2,1,0:T(8,128)(2,1)S(1)}, bf16[74,8,128]{2,1,0:T(8,128)(2,1)S(1)}, u32[]{:S(2)}, u32[]{:S(2)}) %collective-permute-start.3) | collective-permute-done | bytes 151584 | tf_op jit(solution)/shard_map/ppermute | solution.py:526
  38.3 0.7 copy-done.8
  39.0 0.6 copy-done.9
  39.6 3.2 %prep_edge.1 = (bf16[3,10,128,128]{3,2,1,0:T(8,128)(2,1)}, bf16[384,1280]{1,0:T(8,128)(2,1)}) custom-call(bf16[74,8,128]{2,1,0:T(8,128)(2,1)} %copy-done.4, bf16[74,8,128]{2,1,0:T(8,128)(2,1)} %copy-done.5, bf16[5,128,128]{2,1,0:T(8,128)(2,1)} %copy-done.6, bf16[5,128,128]{2,1,0:T(8,128)(2,1)} %copy-done.7, bf16[74,8,128]{2,1,0:T(8,128)(2,1)} %copy-done.9, ...), custom_call_target="tpu_custom_call" | custom-call | flops 500000000 | bytes 3000000 | tf_op jit(solution)/shard_map/prep_edge/pallas_call | solution.py:166
  42.9 0.9 copy-done.3
  43.8 20.1 %scatter.1 = (bf16[72,136,128]{2,1,0:T(8,128)(2,1)}, bf16[72,24,128]{2,1,0:T(8,128)(2,1)}, bf16[4,136,128]{2,1,0:T(8,128)(2,1)}, bf16[5,136,128]{2,1,0:T(8,128)(2,1)}, bf16[2048,128]{1,0:T(8,128)(2,1)}) custom-call(s32[2]{0:T(128)} %pad_add_fusion.edge_ref, bf16[128,24,128]{2,1,0:T(8,128)(2,1)} %copy-done.3, bf16[3,64,128,128]{3,2,1,0:T(8,128)(2,1)} %prep.1.feat_hbm, ...), custom_call_target="tpu_custom_call" | custom-call | flops 8200000000 | bytes 12000000 | tf_op jit(solution)/shard_map/scatter/pallas_call | solution.py:342
  63.9 10.3 %all-to-all-start.1 = ((bf16[128,16,128]{2,1,0:T(8,128)(2,1)}), bf16[128,16,128]{2,1,0:T(8,128)(2,1)S(1)}, u32[]{:S(2)}, u32[]{:S(2)}) async-start(bf16[128,16,128]{2,1,0:T(8,128)(2,1)} %bitcast.9), calls=%async_computation.1 | async-start | bytes 1048576 | tf_op jit(solution)/shard_map/all_to_all | solution.py:557
  74.2 3.3 %collective-permute-start.4 = (bf16[5,136,128]{2,1,0:T(8,128)(2,1)}, bf16[5,136,128]{2,1,0:T(8,128)(2,1)S(1)}, u32[]{:S(2)}, u32[]{:S(2)}) collective-permute-start(bf16[5,136,128]{2,1,0:T(8,128)(2,1)} %get-tuple-element.17), channel_id=1, source_target_pairs={{0,16},{16,32},{32,48},{48,64},{64,80},{80,96},{96,112},{1,17},{17... | collective-permute-start | bytes 522248 | tf_op jit(solution)/shard_map/ppermute | solution.py:525
  77.5 1.3 %collective-permute-start.5 = (bf16[4,136,128]{2,1,0:T(8,128)(2,1)}, bf16[4,136,128]{2,1,0:T(8,128)(2,1)S(1)}, u32[]{:S(2)}, u32[]{:S(2)}) collective-permute-start(bf16[4,136,128]{2,1,0:T(8,128)(2,1)} %get-tuple-element.18), channel_id=1, source_target_pairs={{16,0},{32,16},{48,32},{64,48},{80,64},{96,80},{112,96},{17,1},{33... | collective-permute-start | bytes 417800 | tf_op jit(solution)/shard_map/ppermute | solution.py:526
  78.8 6.9 %collective-permute-done.5.below_ref = bf16[4,136,128]{2,1,0:T(8,128)(2,1)S(1)} collective-permute-done((bf16[4,136,128]{2,1,0:T(8,128)(2,1)}, bf16[4,136,128]{2,1,0:T(8,128)(2,1)S(1)}, u32[]{:S(2)}, u32[]{:S(2)}) %collective-permute-start.5) | collective-permute-done | bytes 139296 | tf_op jit(solution)/shard_map/ppermute | solution.py:526
  85.7 1.1 copy-done
  86.9 0.1 sides.1
  87.0 1.3 %all-to-all-done.1.in_ref = bf16[128,16,128]{2,1,0:T(8,128)(2,1)S(1)} async-done(((bf16[128,16,128]{2,1,0:T(8,128)(2,1)}), bf16[128,16,128]{2,1,0:T(8,128)(2,1)S(1)}, u32[]{:S(2)}, u32[]{:S(2)}) %all-to-all-start.1) | async-done | bytes 524320 | tf_op jit(solution)/shard_map/all_to_all | solution.py:557
  88.3 1.0 share.1
  89.3 9.3 %all-to-all-start.2 = ((bf16[128,16,128]{2,1,0:T(8,128)(2,1)}), bf16[128,16,128]{2,1,0:T(8,128)(2,1)S(1)}, u32[]{:S(2)}, u32[]{:S(2)}) async-start(bf16[128,16,128]{2,1,0:T(8,128)(2,1)} %share.1), calls=%async_computation.2 | async-start | bytes 1048576 | tf_op jit(solution)/shard_map/all_to_all | solution.py:562
  98.6 3.2 %collective-permute-start.6 = (bf16[66,8,128]{2,1,0:T(8,128)(2,1)S(1)}, bf16[66,8,128]{2,1,0:T(8,128)(2,1)S(1)}, u32[]{:S(2)}, u32[]{:S(2)}) collective-permute-start(bf16[66,8,128]{2,1,0:T(8,128)(2,1)S(1)} %get-tuple-element.23), channel_id=1, source_target_pairs={{0,1},{1,2},{2,3},{3,4},{4,5},{5,6},{6,7},{7,8},{8,9},{9,10},{10,1... | collective-permute-start | bytes 405512 | tf_op jit(solution)/shard_map/ppermute | solution.py:525
  101.8 3.7 %collective-permute-done.6.left_ref = bf16[66,8,128]{2,1,0:T(8,128)(2,1)S(1)} collective-permute-done((bf16[66,8,128]{2,1,0:T(8,128)(2,1)S(1)}, bf16[66,8,128]{2,1,0:T(8,128)(2,1)S(1)}, u32[]{:S(2)}, u32[]{:S(2)}) %collective-permute-start.6) | collective-permute-done | bytes 135200 | tf_op jit(solution)/shard_map/ppermute | solution.py:525
  105.5 5.1 %collective-permute-done.7.right_ref = bf16[66,8,128]{2,1,0:T(8,128)(2,1)S(1)} collective-permute-done((bf16[66,8,128]{2,1,0:T(8,128)(2,1)S(1)}, bf16[66,8,128]{2,1,0:T(8,128)(2,1)S(1)}, u32[]{:S(2)}, u32[]{:S(2)}) %collective-permute-start.7) | collective-permute-done | bytes 135200 | tf_op jit(solution)/shard_map/ppermute | solution.py:526
  110.6 0.6 copy-done.11
  111.2 9.1 %conv.1 = bf16[64,128,128]{2,1,0:T(8,128)(2,1)} custom-call(bf16[72,136,128]{2,1,0:T(8,128)(2,1)} %get-tuple-element.16.canvas_ref, bf16[5,136,128]{2,1,0:T(8,128)(2,1)} %copy-done.1, bf16[4,136,128]{2,1,0:T(8,128)(2,1)} %copy-done.2, bf16[66,8,128]{2,1,0:T(8,128)(2,1)} %copy-done.10, bf16[66,8,128]{2,1,0:T(8,128)(2,1)} %copy-done.11, ...), custom_call_target="tpu_custom_call" | custom-call | flops 2700000000 | bytes 4500000 | tf_op jit(solution)/shard_map/conv/pallas_call | solution.py:471
  120.3 1.4 %finish.1 = f32[1152,128]{1,0:T(8,128)} custom-call(bf16[128,16,128]{2,1,0:T(8,128)(2,1)S(1)} %all-to-all-done.2.in_ref), custom_call_target="tpu_custom_call" | custom-call | bytes 900000 | tf_op jit(solution)/shard_map/finish/pallas_call | solution.py:509
  (29 shorter events, 0.1 us)
Async XLA Ops:
  1.7 22.5 %collective-permute-start = (bf16[5,128,128]{2,1,0:T(8,128)(2,1)S(1)}, bf16[5,128,128]{2,1,0:T(8,128)(2,1)S(1)}, u32[]{:S(2)}, u32[]{:S(2)}) collective-permute-start(bf16[5,128,128]{2,1,0:T(8,128)(2,1)S(1)} %get-tuple-element.28), channel_id=1, source_target_pairs={{0,16},{16,32},{32,48},{48,64},{64,80},{80,96},{96,112},{1,17},{17... | collective-permute-start | bytes 491528 | tf_op jit(solution)/shard_map/ppermute | solution.py:525
  5.7 18.5 %collective-permute-start.1 = (bf16[5,128,128]{2,1,0:T(8,128)(2,1)S(1)}, bf16[5,128,128]{2,1,0:T(8,128)(2,1)S(1)}, u32[]{:S(2)}, u32[]{:S(2)}) collective-permute-start(bf16[5,128,128]{2,1,0:T(8,128)(2,1)S(1)} %get-tuple-element.29), channel_id=1, source_target_pairs={{16,0},{32,16},{48,32},{64,48},{80,64},{96,80},{112,96},{17,1},{33... | collective-permute-start | bytes 491528 | tf_op jit(solution)/shard_map/ppermute | solution.py:526
  11.1 31.7 %all-to-all-start = ((bf16[128,24,128]{2,1,0:T(8,128)(2,1)}), bf16[128,24,128]{2,1,0:T(8,128)(2,1)S(1)}, u32[]{:S(2)}, u32[]{:S(2)}) async-start(bf16[128,24,128]{2,1,0:T(8,128)(2,1)} %pack.1), calls=%async_computation | async-start | bytes 1572864 | tf_op jit(solution)/shard_map/all_to_all | solution.py:547
  24.2 12.2 %copy-start.6 = (bf16[5,128,128]{2,1,0:T(8,128)(2,1)}, bf16[5,128,128]{2,1,0:T(8,128)(2,1)S(1)}, u32[]{:S(2)}) copy-start(bf16[5,128,128]{2,1,0:T(8,128)(2,1)S(1)} %collective-permute-done.above_ref) | copy-start | bytes 491524
  24.2 12.2 %copy-start.7 = (bf16[5,128,128]{2,1,0:T(8,128)(2,1)}, bf16[5,128,128]{2,1,0:T(8,128)(2,1)S(1)}, u32[]{:S(2)}) copy-start(bf16[5,128,128]{2,1,0:T(8,128)(2,1)S(1)} %collective-permute-done.1.below_ref) | copy-start | bytes 491524
  24.3 12.1 %copy-start.4 = (bf16[74,8,128]{2,1,0:T(8,128)(2,1)}, bf16[74,8,128]{2,1,0:T(8,128)(2,1)S(1)}, u32[]{:S(2)}) copy-start(bf16[74,8,128]{2,1,0:T(8,128)(2,1)S(1)} %pad_maximum_fusion.head_ref) | copy-start | bytes 454660
  24.3 14.0 %collective-permute-start.3 = (bf16[74,8,128]{2,1,0:T(8,128)(2,1)S(1)}, bf16[74,8,128]{2,1,0:T(8,128)(2,1)S(1)}, u32[]{:S(2)}, u32[]{:S(2)}) collective-permute-start(bf16[74,8,128]{2,1,0:T(8,128)(2,1)S(1)} %pad_maximum_fusion.head_ref), channel_id=1, source_target_pairs={{1,0},{2,1},{3,2},{4,3},{5,4},{6,5},{7,6},{8,7},{9,8},{10,9},{11,1... | collective-permute-start | bytes 454664 | tf_op jit(solution)/shard_map/ppermute | solution.py:526
  25.4 11.0 %copy-start.5 = (bf16[74,8,128]{2,1,0:T(8,128)(2,1)}, bf16[74,8,128]{2,1,0:T(8,128)(2,1)S(1)}, u32[]{:S(2)}) copy-start(bf16[74,8,128]{2,1,0:T(8,128)(2,1)S(1)} %pad_maximum_fusion.1.last_ref) | copy-start | bytes 454660
  25.4 12.9 %collective-permute-start.2 = (bf16[74,8,128]{2,1,0:T(8,128)(2,1)S(1)}, bf16[74,8,128]{2,1,0:T(8,128)(2,1)S(1)}, u32[]{:S(2)}, u32[]{:S(2)}) collective-permute-start(bf16[74,8,128]{2,1,0:T(8,128)(2,1)S(1)} %pad_maximum_fusion.1.last_ref), channel_id=1, source_target_pairs={{0,1},{1,2},{2,3},{3,4},{4,5},{5,6},{6,7},{7,8},{8,9},{9,10},{10,1... | collective-permute-start | bytes 454664 | tf_op jit(solution)/shard_map/ppermute | solution.py:525
  38.3 0.7 copy-start.8
  39.0 0.7 copy-start.9
  42.9 0.9 copy-start.3
  63.9 24.4 %all-to-all-start.1 = ((bf16[128,16,128]{2,1,0:T(8,128)(2,1)}), bf16[128,16,128]{2,1,0:T(8,128)(2,1)S(1)}, u32[]{:S(2)}, u32[]{:S(2)}) async-start(bf16[128,16,128]{2,1,0:T(8,128)(2,1)} %bitcast.9), calls=%async_computation.1 | async-start | bytes 1048576 | tf_op jit(solution)/shard_map/all_to_all | solution.py:557
  74.2 11.5 %collective-permute-start.4 = (bf16[5,136,128]{2,1,0:T(8,128)(2,1)}, bf16[5,136,128]{2,1,0:T(8,128)(2,1)S(1)}, u32[]{:S(2)}, u32[]{:S(2)}) collective-permute-start(bf16[5,136,128]{2,1,0:T(8,128)(2,1)} %get-tuple-element.17), channel_id=1, source_target_pairs={{0,16},{16,32},{32,48},{48,64},{64,80},{80,96},{96,112},{1,17},{17... | collective-permute-start | bytes 522248 | tf_op jit(solution)/shard_map/ppermute | solution.py:525
  77.5 8.2 %collective-permute-start.5 = (bf16[4,136,128]{2,1,0:T(8,128)(2,1)}, bf16[4,136,128]{2,1,0:T(8,128)(2,1)S(1)}, u32[]{:S(2)}, u32[]{:S(2)}) collective-permute-start(bf16[4,136,128]{2,1,0:T(8,128)(2,1)} %get-tuple-element.18), channel_id=1, source_target_pairs={{16,0},{32,16},{48,32},{64,48},{80,64},{96,80},{112,96},{17,1},{33... | collective-permute-start | bytes 417800 | tf_op jit(solution)/shard_map/ppermute | solution.py:526
  85.7 24.8 %copy-start.2 = (bf16[4,136,128]{2,1,0:T(8,128)(2,1)}, bf16[4,136,128]{2,1,0:T(8,128)(2,1)S(1)}, u32[]{:S(2)}) copy-start(bf16[4,136,128]{2,1,0:T(8,128)(2,1)S(1)} %collective-permute-done.5.below_ref) | copy-start | bytes 417796
  85.7 24.8 %copy-start.1 = (bf16[5,136,128]{2,1,0:T(8,128)(2,1)}, bf16[5,136,128]{2,1,0:T(8,128)(2,1)S(1)}, u32[]{:S(2)}) copy-start(bf16[5,136,128]{2,1,0:T(8,128)(2,1)S(1)} %collective-permute-done.4.above_ref) | copy-start | bytes 522244
  85.7 1.1 copy-start
  89.3 31.0 %all-to-all-start.2 = ((bf16[128,16,128]{2,1,0:T(8,128)(2,1)}), bf16[128,16,128]{2,1,0:T(8,128)(2,1)S(1)}, u32[]{:S(2)}, u32[]{:S(2)}) async-start(bf16[128,16,128]{2,1,0:T(8,128)(2,1)} %share.1), calls=%async_computation.2 | async-start | bytes 1048576 | tf_op jit(solution)/shard_map/all_to_all | solution.py:562
  98.6 6.9 %collective-permute-start.6 = (bf16[66,8,128]{2,1,0:T(8,128)(2,1)S(1)}, bf16[66,8,128]{2,1,0:T(8,128)(2,1)S(1)}, u32[]{:S(2)}, u32[]{:S(2)}) collective-permute-start(bf16[66,8,128]{2,1,0:T(8,128)(2,1)S(1)} %get-tuple-element.23), channel_id=1, source_target_pairs={{0,1},{1,2},{2,3},{3,4},{4,5},{5,6},{6,7},{7,8},{8,9},{9,10},{10,1... | collective-permute-start | bytes 405512 | tf_op jit(solution)/shard_map/ppermute | solution.py:525
  101.8 8.8 %collective-permute-start.7 = (bf16[66,8,128]{2,1,0:T(8,128)(2,1)S(1)}, bf16[66,8,128]{2,1,0:T(8,128)(2,1)S(1)}, u32[]{:S(2)}, u32[]{:S(2)}) collective-permute-start(bf16[66,8,128]{2,1,0:T(8,128)(2,1)S(1)} %get-tuple-element.24), channel_id=1, source_target_pairs={{1,0},{2,1},{3,2},{4,3},{5,4},{6,5},{7,6},{8,7},{9,8},{10,9},{11,1... | collective-permute-start | bytes 405512 | tf_op jit(solution)/shard_map/ppermute | solution.py:526
  105.5 5.1 %copy-start.10 = (bf16[66,8,128]{2,1,0:T(8,128)(2,1)}, bf16[66,8,128]{2,1,0:T(8,128)(2,1)S(1)}, u32[]{:S(2)}) copy-start(bf16[66,8,128]{2,1,0:T(8,128)(2,1)S(1)} %collective-permute-done.6.left_ref) | copy-start | bytes 405508
  110.5 0.6 copy-start.11

commit v4 on v3

--- a/solution.py
+++ b/solution.py
@@ -117,8 +117,13 @@
     return [moved[:, b * 128 : (b + 1) * 128].reshape(len(lines), 128, 128) for b in range(3)]
 
 
-def prep_kernel(feat_ref, out_ref):
-    moved = turn_lines([feat_ref[i] for i in range(8)], identity(), column_shift())
+def prep_kernel(feat_ref, out_ref, eye_ref, shift_ref):
+    @pl.when(pl.program_id(0) == 0)
+    def _():
+        eye_ref[...] = identity()
+        shift_ref[...] = column_shift()
+
+    moved = turn_lines([feat_ref[i] for i in range(8)], eye_ref[...], shift_ref[...])
     for b in range(3):
         out_ref[b] = moved[b]
 
@@ -130,6 +135,7 @@
         out_shape=jax.ShapeDtypeStruct((3, 64, 128, 128), BF16),
         in_specs=[pl.BlockSpec((8, 128, 128), lambda i: (i, 0, 0))],
         out_specs=pl.BlockSpec((3, 8, 128, 128), lambda i: (0, i, 0, 0)),
+        scratch_shapes=[pltpu.VMEM((128, 128), BF16), pltpu.VMEM((128, 384), BF16)],
         cost_estimate=pl.CostEstimate(
             flops=2_200_000_000, bytes_accessed=8_000_000, transcendentals=0
         ),
@@ -554,11 +560,12 @@
     feat = prep(features)
     feat_edge, feat_side = prep_edge(head, last, above, below, left, right)
     canvas, rim, up, down, part = scatter(edge, incoming, feat, feat_edge, feat_side)
+    grid_above, grid_below = both_ways(down, up, "lat", False)
+    part, grid_above, grid_below = lax.optimization_barrier((part, grid_above, grid_below))
     got = lax.all_to_all(part.reshape(TILES, 16, 128), AXES, 0, 0, tiled=True)
-    grid_above, grid_below = both_ways(down, up, "lat", False)
     send_right, send_left = sides(rim, grid_above, grid_below)
-    got, send_right, send_left = lax.optimization_barrier((got, send_right, send_left))
     from_left, from_right = both_ways(send_right, send_left, "lon", True)
+    got, from_left, from_right = lax.optimization_barrier((got, from_left, from_right))
     every = lax.all_to_all(share(got), AXES, 0, 0, tiled=True)
     input_grad = conv(canvas, grid_above, grid_below, from_left, from_right, conv_weight)
     weight_grad = finish(every)

time: 124 us -> 122 us (0.984); the launches traced: 122 us -> 121 us
  starting transfers between devices: 48.1 us -> 46 us
  waiting for transfers between devices: 18.4 us -> 20.4 us
    all_to_all x1, waiting for transfers between devices: 0.01 us -> 4.67 us  [shards(): every = lax.all_to_all(share(got), AXES, 0, 0, tiled=True)]
    all_to_all x1, starting transfers between devices: 9.25 us -> 5.95 us  [shards(): every = lax.all_to_all(share(got), AXES, 0, 0, tiled=True)]
    ppermute x4, waiting for transfers between devices: 13.3 us -> 11.1 us  [both_ways(): lax.ppermute(back, axis, [((i + 1) % count, i) for i in range(ends)])]
    all_to_all x1, starting transfers between devices: 10.3 us -> 11.7 us  [shards(): got = lax.all_to_all(part.reshape(TILES, 16, 128), AXES, 0, 0, tiled=True)]
  transfers between devices with their start and end apart: 11 -> 11, of which waited for: 5 -> 6; matrix products, arithmetic and copies ran while one was open for 1% -> 1% of each run, Pallas kernels for 20% -> 20%
where the time goes in v4:
time: 122 us; the launch traced here: 121 us
  Pallas kernels  47.2 us (39%)
  starting transfers between devices  46 us (38%)
  waiting for transfers between devices  20.4 us (17%)
  local copies, waits for them, and re-layouts  5.31 us (4%)
  between operations  1.5 us (1%)
    pallas_call x1, Pallas kernels, scatter(): pl.pallas_call(scatter_kernel, out_shape=(jax.ShapeDtypeStruct((72, 136,...  20.1 us
    ppermute x4, starting transfers between devices, both_ways(): lax.ppermute(forth, axis, [(i, (i + 1) % count) for i in range(ends)])  12.6 us
    all_to_all x1, starting transfers between devices, shards(): incoming = lax.all_to_all(outgoing, AXES, 0, 0, tiled=True)  12 us
    all_to_all x1, starting transfers between devices, shards(): got = lax.all_to_all(part.reshape(TILES, 16, 128), AXES, 0, 0, tiled=True)  11.7 us
    ppermute x4, waiting for transfers between devices, both_ways(): lax.ppermute(back, axis, [((i + 1) % count, i) for i in range(ends)])  11.1 us
    pallas_call x1, Pallas kernels, conv(): pl.pallas_call(conv_kernel, grid=(8,), out_shape=jax.ShapeDtypeStruct((64...  9.14 us
    pallas_call x1, Pallas kernels, prep(): pl.pallas_call(prep_kernel, grid=(8,), out_shape=jax.ShapeDtypeStruct((3,...  8.73 us
    all_to_all x1, starting transfers between devices, shards(): every = lax.all_to_all(share(got), AXES, 0, 0, tiled=True)  5.95 us
  transfers between devices with their start and end apart: 11, of which 6 were waited for; matrix products, arithmetic and copies ran while one was open for 1% of the time, Pallas kernels for 20%

profile of v4, /device:TPU:1, one launch (start us, length us, event | category | flops | bytes accessed | tf_op | source)
XLA Modules:
  0.0 121.0 jit_solution(11530027620502264821)
XLA Ops:
  0.6 1.0 fusion.1
  1.7 4.0 %collective-permute-start = (bf16[5,128,128]{2,1,0:T(8,128)(2,1)S(1)}, bf16[5,128,128]{2,1,0:T(8,128)(2,1)S(1)}, u32[]{:S(2)}, u32[]{:S(2)}) collective-permute-start(bf16[5,128,128]{2,1,0:T(8,128)(2,1)S(1)} %get-tuple-element.34), channel_id=1, source_target_pairs={{0,16},{16,32},{32,48},{48,64},{64,80},{80,96},{96,112},{1,17},{17... | collective-permute-start | bytes 491528 | tf_op jit(solution)/shard_map/ppermute | solution.py:531
  5.7 1.3 %collective-permute-start.1 = (bf16[5,128,128]{2,1,0:T(8,128)(2,1)S(1)}, bf16[5,128,128]{2,1,0:T(8,128)(2,1)S(1)}, u32[]{:S(2)}, u32[]{:S(2)}) collective-permute-start(bf16[5,128,128]{2,1,0:T(8,128)(2,1)S(1)} %get-tuple-element.35), channel_id=1, source_target_pairs={{16,0},{32,16},{48,32},{64,48},{80,64},{96,80},{112,96},{17,1},{33... | collective-permute-start | bytes 491528 | tf_op jit(solution)/shard_map/ppermute | solution.py:532
  7.6 3.5 %pack.1 = bf16[128,24,128]{2,1,0:T(8,128)(2,1)} custom-call(s32[1]{0:T(128)S(6)} %copy.10.live_ref, s32[1,1024]{1,0:T(1,128)} %bitcast.10, s32[1,1024]{1,0:T(1,128)} %bitcast.11, s32[1,1024]{1,0:T(1,128)} %bitcast.12, bf16[2,1024]{1,0:T(2,128)(2,1)} %bitcast.13, bf16[1024,128]{1,0:T(8,128)(2,1)} %rows_ref.1), custom_call_target="tpu_custom_call" | custom-call | flops 700000000 | bytes 1500000 | tf_op jit(solution)/shard_map/pack/pallas_call | solution.py:81
  11.1 12.0 %all-to-all-start = ((bf16[128,24,128]{2,1,0:T(8,128)(2,1)}), bf16[128,24,128]{2,1,0:T(8,128)(2,1)S(1)}, u32[]{:S(2)}, u32[]{:S(2)}) async-start(bf16[128,24,128]{2,1,0:T(8,128)(2,1)} %pack.1), calls=%async_computation | async-start | bytes 1572864 | tf_op jit(solution)/shard_map/all_to_all | solution.py:553
  23.2 1.0 fusion
  24.2 0.0 copy-start.6
  24.3 1.1 collective-permute-start.3
  25.4 2.3 %collective-permute-start.2 = (bf16[74,8,128]{2,1,0:T(8,128)(2,1)S(1)}, bf16[74,8,128]{2,1,0:T(8,128)(2,1)S(1)}, u32[]{:S(2)}, u32[]{:S(2)}) collective-permute-start(bf16[74,8,128]{2,1,0:T(8,128)(2,1)S(1)} %pad_maximum_fusion.1.last_ref), channel_id=1, source_target_pairs={{0,1},{1,2},{2,3},{3,4},{4,5},{5,6},{6,7},{7,8},{8,9},{9,10},{10,1... | collective-permute-start | bytes 454664 | tf_op jit(solution)/shard_map/ppermute | solution.py:531
  27.7 8.7 %prep.1.feat_hbm = bf16[3,64,128,128]{3,2,1,0:T(8,128)(2,1)} custom-call(bf16[64,128,128]{2,1,0:T(8,128)(2,1)} %feat_ref.1), custom_call_target="tpu_custom_call" | custom-call | flops 2200000000 | bytes 8000000 | tf_op jit(solution)/shard_map/prep/pallas_call | solution.py:132
  36.5 0.6 pad_add_fusion.edge_ref
  37.0 1.3 %collective-permute-done.3.right_ref = bf16[74,8,128]{2,1,0:T(8,128)(2,1)S(1)} collective-permute-done((bf16[74,8,128]{2,1,0:T(8,128)(2,1)S(1)}, bf16[74,8,128]{2,1,0:T(8,128)(2,1)S(1)}, u32[]{:S(2)}, u32[]{:S(2)}) %collective-permute-start.3) | collective-permute-done | bytes 151584 | tf_op jit(solution)/shard_map/ppermute | solution.py:532
  38.3 0.7 copy-done.8
  39.0 0.6 copy-done.9
  39.6 3.2 %prep_edge.1 = (bf16[3,10,128,128]{3,2,1,0:T(8,128)(2,1)}, bf16[384,1280]{1,0:T(8,128)(2,1)}) custom-call(bf16[74,8,128]{2,1,0:T(8,128)(2,1)} %copy-done.4, bf16[74,8,128]{2,1,0:T(8,128)(2,1)} %copy-done.5, bf16[5,128,128]{2,1,0:T(8,128)(2,1)} %copy-done.6, bf16[5,128,128]{2,1,0:T(8,128)(2,1)} %copy-done.7, bf16[74,8,128]{2,1,0:T(8,128)(2,1)} %copy-done.9, ...), custom_call_target="tpu_custom_call" | custom-call | flops 500000000 | bytes 3000000 | tf_op jit(solution)/shard_map/prep_edge/pallas_call | solution.py:172
  42.9 0.9 copy-done.3
  43.8 20.1 %scatter.1 = (bf16[72,136,128]{2,1,0:T(8,128)(2,1)}, bf16[72,24,128]{2,1,0:T(8,128)(2,1)}, bf16[4,136,128]{2,1,0:T(8,128)(2,1)}, bf16[5,136,128]{2,1,0:T(8,128)(2,1)}, bf16[2048,128]{1,0:T(8,128)(2,1)}) custom-call(s32[2]{0:T(128)} %pad_add_fusion.edge_ref, bf16[128,24,128]{2,1,0:T(8,128)(2,1)} %copy-done.3, bf16[3,64,128,128]{3,2,1,0:T(8,128)(2,1)} %prep.1.feat_hbm, ...), custom_call_target="tpu_custom_call" | custom-call | flops 8200000000 | bytes 12000000 | tf_op jit(solution)/shard_map/scatter/pallas_call | solution.py:348
  63.9 3.1 %collective-permute-start.4 = (bf16[5,136,128]{2,1,0:T(8,128)(2,1)}, bf16[5,136,128]{2,1,0:T(8,128)(2,1)S(1)}, u32[]{:S(2)}, u32[]{:S(2)}) collective-permute-start(bf16[5,136,128]{2,1,0:T(8,128)(2,1)} %get-tuple-element.21), channel_id=1, source_target_pairs={{0,16},{16,32},{32,48},{48,64},{64,80},{80,96},{96,112},{1,17},{17... | collective-permute-start | bytes 522248 | tf_op jit(solution)/shard_map/ppermute | solution.py:531
  67.0 1.3 %collective-permute-start.5 = (bf16[4,136,128]{2,1,0:T(8,128)(2,1)}, bf16[4,136,128]{2,1,0:T(8,128)(2,1)S(1)}, u32[]{:S(2)}, u32[]{:S(2)}) collective-permute-start(bf16[4,136,128]{2,1,0:T(8,128)(2,1)} %get-tuple-element.22), channel_id=1, source_target_pairs={{16,0},{32,16},{48,32},{64,48},{80,64},{96,80},{112,96},{17,1},{33... | collective-permute-start | bytes 417800 | tf_op jit(solution)/shard_map/ppermute | solution.py:532
  68.3 4.7 %collective-permute-done.5.below_ref = bf16[4,136,128]{2,1,0:T(8,128)(2,1)S(1)} collective-permute-done((bf16[4,136,128]{2,1,0:T(8,128)(2,1)}, bf16[4,136,128]{2,1,0:T(8,128)(2,1)S(1)}, u32[]{:S(2)}, u32[]{:S(2)}) %collective-permute-start.5) | collective-permute-done | bytes 139296 | tf_op jit(solution)/shard_map/ppermute | solution.py:532
  73.0 11.7 %all-to-all-start.1 = ((bf16[128,16,128]{2,1,0:T(8,128)(2,1)}), bf16[128,16,128]{2,1,0:T(8,128)(2,1)S(1)}, u32[]{:S(2)}, u32[]{:S(2)}) async-start(bf16[128,16,128]{2,1,0:T(8,128)(2,1)} %bitcast.9), calls=%async_computation.1 | async-start | bytes 1048576 | tf_op jit(solution)/shard_map/all_to_all | solution.py:565
  84.8 1.0 copy-done
  85.8 0.1 sides.1
  85.9 3.2 %collective-permute-start.6 = (bf16[66,8,128]{2,1,0:T(8,128)(2,1)S(1)}, bf16[66,8,128]{2,1,0:T(8,128)(2,1)S(1)}, u32[]{:S(2)}, u32[]{:S(2)}) collective-permute-start(bf16[66,8,128]{2,1,0:T(8,128)(2,1)S(1)} %get-tuple-element.27), channel_id=1, source_target_pairs={{0,1},{1,2},{2,3},{3,4},{4,5},{5,6},{6,7},{7,8},{8,9},{9,10},{10,1... | collective-permute-start | bytes 405512 | tf_op jit(solution)/shard_map/ppermute | solution.py:531
  89.1 2.6 %collective-permute-done.6.left_ref = bf16[66,8,128]{2,1,0:T(8,128)(2,1)S(1)} collective-permute-done((bf16[66,8,128]{2,1,0:T(8,128)(2,1)S(1)}, bf16[66,8,128]{2,1,0:T(8,128)(2,1)S(1)}, u32[]{:S(2)}, u32[]{:S(2)}) %collective-permute-start.6) | collective-permute-done | bytes 135200 | tf_op jit(solution)/shard_map/ppermute | solution.py:531
  91.7 5.1 %collective-permute-done.7.right_ref = bf16[66,8,128]{2,1,0:T(8,128)(2,1)S(1)} collective-permute-done((bf16[66,8,128]{2,1,0:T(8,128)(2,1)S(1)}, bf16[66,8,128]{2,1,0:T(8,128)(2,1)S(1)}, u32[]{:S(2)}, u32[]{:S(2)}) %collective-permute-start.7) | collective-permute-done | bytes 135200 | tf_op jit(solution)/shard_map/ppermute | solution.py:532
  96.8 2.1 %all-to-all-done.1.in_ref = bf16[128,16,128]{2,1,0:T(8,128)(2,1)S(1)} async-done(((bf16[128,16,128]{2,1,0:T(8,128)(2,1)}), bf16[128,16,128]{2,1,0:T(8,128)(2,1)S(1)}, u32[]{:S(2)}, u32[]{:S(2)}) %all-to-all-start.1) | async-done | bytes 524320 | tf_op jit(solution)/shard_map/all_to_all | solution.py:565
  98.9 1.0 share.1
  99.9 6.0 %all-to-all-start.2 = ((bf16[128,16,128]{2,1,0:T(8,128)(2,1)}), bf16[128,16,128]{2,1,0:T(8,128)(2,1)S(1)}, u32[]{:S(2)}, u32[]{:S(2)}) async-start(bf16[128,16,128]{2,1,0:T(8,128)(2,1)} %share.1), calls=%async_computation.2 | async-start | bytes 1048576 | tf_op jit(solution)/shard_map/all_to_all | solution.py:569
  105.9 9.1 %conv.1 = bf16[64,128,128]{2,1,0:T(8,128)(2,1)} custom-call(bf16[72,136,128]{2,1,0:T(8,128)(2,1)} %get-tuple-element.19.canvas_ref, bf16[5,136,128]{2,1,0:T(8,128)(2,1)} %copy-done.1, bf16[4,136,128]{2,1,0:T(8,128)(2,1)} %copy-done.2, bf16[66,8,128]{2,1,0:T(8,128)(2,1)} %copy-done.10, bf16[66,8,128]{2,1,0:T(8,128)(2,1)} %copy-done.11, ...), custom_call_target="tpu_custom_call" | custom-call | flops 2700000000 | bytes 4500000 | tf_op jit(solution)/shard_map/conv/pallas_call | solution.py:477
  115.0 4.7 %all-to-all-done.2.in_ref = bf16[128,16,128]{2,1,0:T(8,128)(2,1)S(1)} async-done(((bf16[128,16,128]{2,1,0:T(8,128)(2,1)}), bf16[128,16,128]{2,1,0:T(8,128)(2,1)S(1)}, u32[]{:S(2)}, u32[]{:S(2)}) %all-to-all-start.2) | async-done | bytes 524320 | tf_op jit(solution)/shard_map/all_to_all | solution.py:569
  119.7 1.4 %finish.1 = f32[1152,128]{1,0:T(8,128)} custom-call(bf16[128,16,128]{2,1,0:T(8,128)(2,1)S(1)} %all-to-all-done.2.in_ref), custom_call_target="tpu_custom_call" | custom-call | bytes 900000 | tf_op jit(solution)/shard_map/finish/pallas_call | solution.py:515
  (29 shorter events, 0.1 us)
Async XLA Ops:
  1.7 22.5 %collective-permute-start = (bf16[5,128,128]{2,1,0:T(8,128)(2,1)S(1)}, bf16[5,128,128]{2,1,0:T(8,128)(2,1)S(1)}, u32[]{:S(2)}, u32[]{:S(2)}) collective-permute-start(bf16[5,128,128]{2,1,0:T(8,128)(2,1)S(1)} %get-tuple-element.34), channel_id=1, source_target_pairs={{0,16},{16,32},{32,48},{48,64},{64,80},{80,96},{96,112},{1,17},{17... | collective-permute-start | bytes 491528 | tf_op jit(solution)/shard_map/ppermute | solution.py:531
  5.7 18.5 %collective-permute-start.1 = (bf16[5,128,128]{2,1,0:T(8,128)(2,1)S(1)}, bf16[5,128,128]{2,1,0:T(8,128)(2,1)S(1)}, u32[]{:S(2)}, u32[]{:S(2)}) collective-permute-start(bf16[5,128,128]{2,1,0:T(8,128)(2,1)S(1)} %get-tuple-element.35), channel_id=1, source_target_pairs={{16,0},{32,16},{48,32},{64,48},{80,64},{96,80},{112,96},{17,1},{33... | collective-permute-start | bytes 491528 | tf_op jit(solution)/shard_map/ppermute | solution.py:532
  11.1 31.7 %all-to-all-start = ((bf16[128,24,128]{2,1,0:T(8,128)(2,1)}), bf16[128,24,128]{2,1,0:T(8,128)(2,1)S(1)}, u32[]{:S(2)}, u32[]{:S(2)}) async-start(bf16[128,24,128]{2,1,0:T(8,128)(2,1)} %pack.1), calls=%async_computation | async-start | bytes 1572864 | tf_op jit(solution)/shard_map/all_to_all | solution.py:553
  24.2 12.3 %copy-start.6 = (bf16[5,128,128]{2,1,0:T(8,128)(2,1)}, bf16[5,128,128]{2,1,0:T(8,128)(2,1)S(1)}, u32[]{:S(2)}) copy-start(bf16[5,128,128]{2,1,0:T(8,128)(2,1)S(1)} %collective-permute-done.above_ref) | copy-start | bytes 491524
  24.2 12.2 %copy-start.7 = (bf16[5,128,128]{2,1,0:T(8,128)(2,1)}, bf16[5,128,128]{2,1,0:T(8,128)(2,1)S(1)}, u32[]{:S(2)}) copy-start(bf16[5,128,128]{2,1,0:T(8,128)(2,1)S(1)} %collective-permute-done.1.below_ref) | copy-start | bytes 491524
  24.3 12.2 %copy-start.4 = (bf16[74,8,128]{2,1,0:T(8,128)(2,1)}, bf16[74,8,128]{2,1,0:T(8,128)(2,1)S(1)}, u32[]{:S(2)}) copy-start(bf16[74,8,128]{2,1,0:T(8,128)(2,1)S(1)} %pad_maximum_fusion.head_ref) | copy-start | bytes 454660
  24.3 14.0 %collective-permute-start.3 = (bf16[74,8,128]{2,1,0:T(8,128)(2,1)S(1)}, bf16[74,8,128]{2,1,0:T(8,128)(2,1)S(1)}, u32[]{:S(2)}, u32[]{:S(2)}) collective-permute-start(bf16[74,8,128]{2,1,0:T(8,128)(2,1)S(1)} %pad_maximum_fusion.head_ref), channel_id=1, source_target_pairs={{1,0},{2,1},{3,2},{4,3},{5,4},{6,5},{7,6},{8,7},{9,8},{10,9},{11,1... | collective-permute-start | bytes 454664 | tf_op jit(solution)/shard_map/ppermute | solution.py:532
  25.4 11.0 %copy-start.5 = (bf16[74,8,128]{2,1,0:T(8,128)(2,1)}, bf16[74,8,128]{2,1,0:T(8,128)(2,1)S(1)}, u32[]{:S(2)}) copy-start(bf16[74,8,128]{2,1,0:T(8,128)(2,1)S(1)} %pad_maximum_fusion.1.last_ref) | copy-start | bytes 454660
  25.4 12.9 %collective-permute-start.2 = (bf16[74,8,128]{2,1,0:T(8,128)(2,1)S(1)}, bf16[74,8,128]{2,1,0:T(8,128)(2,1)S(1)}, u32[]{:S(2)}, u32[]{:S(2)}) collective-permute-start(bf16[74,8,128]{2,1,0:T(8,128)(2,1)S(1)} %pad_maximum_fusion.1.last_ref), channel_id=1, source_target_pairs={{0,1},{1,2},{2,3},{3,4},{4,5},{5,6},{6,7},{7,8},{8,9},{9,10},{10,1... | collective-permute-start | bytes 454664 | tf_op jit(solution)/shard_map/ppermute | solution.py:531
  38.3 0.7 copy-start.8
  39.0 0.7 copy-start.9
  42.9 0.9 copy-start.3
  63.9 9.1 %collective-permute-start.4 = (bf16[5,136,128]{2,1,0:T(8,128)(2,1)}, bf16[5,136,128]{2,1,0:T(8,128)(2,1)S(1)}, u32[]{:S(2)}, u32[]{:S(2)}) collective-permute-start(bf16[5,136,128]{2,1,0:T(8,128)(2,1)} %get-tuple-element.21), channel_id=1, source_target_pairs={{0,16},{16,32},{32,48},{48,64},{64,80},{80,96},{96,112},{1,17},{17... | collective-permute-start | bytes 522248 | tf_op jit(solution)/shard_map/ppermute | solution.py:531
  67.0 6.0 %collective-permute-start.5 = (bf16[4,136,128]{2,1,0:T(8,128)(2,1)}, bf16[4,136,128]{2,1,0:T(8,128)(2,1)S(1)}, u32[]{:S(2)}, u32[]{:S(2)}) collective-permute-start(bf16[4,136,128]{2,1,0:T(8,128)(2,1)} %get-tuple-element.22), channel_id=1, source_target_pairs={{16,0},{32,16},{48,32},{64,48},{80,64},{96,80},{112,96},{17,1},{33... | collective-permute-start | bytes 417800 | tf_op jit(solution)/shard_map/ppermute | solution.py:532
  73.0 32.8 %copy-start.2 = (bf16[4,136,128]{2,1,0:T(8,128)(2,1)}, bf16[4,136,128]{2,1,0:T(8,128)(2,1)S(1)}, u32[]{:S(2)}) copy-start(bf16[4,136,128]{2,1,0:T(8,128)(2,1)S(1)} %collective-permute-done.5.below_ref) | copy-start | bytes 417796
  73.0 32.8 %copy-start.1 = (bf16[5,136,128]{2,1,0:T(8,128)(2,1)}, bf16[5,136,128]{2,1,0:T(8,128)(2,1)S(1)}, u32[]{:S(2)}) copy-start(bf16[5,136,128]{2,1,0:T(8,128)(2,1)S(1)} %collective-permute-done.4.above_ref) | copy-start | bytes 522244
  73.0 25.8 %all-to-all-start.1 = ((bf16[128,16,128]{2,1,0:T(8,128)(2,1)}), bf16[128,16,128]{2,1,0:T(8,128)(2,1)S(1)}, u32[]{:S(2)}, u32[]{:S(2)}) async-start(bf16[128,16,128]{2,1,0:T(8,128)(2,1)} %bitcast.9), calls=%async_computation.1 | async-start | bytes 1048576 | tf_op jit(solution)/shard_map/all_to_all | solution.py:565
  84.8 1.0 copy-start
  85.9 5.8 %collective-permute-start.6 = (bf16[66,8,128]{2,1,0:T(8,128)(2,1)S(1)}, bf16[66,8,128]{2,1,0:T(8,128)(2,1)S(1)}, u32[]{:S(2)}, u32[]{:S(2)}) collective-permute-start(bf16[66,8,128]{2,1,0:T(8,128)(2,1)S(1)} %get-tuple-element.27), channel_id=1, source_target_pairs={{0,1},{1,2},{2,3},{3,4},{4,5},{5,6},{6,7},{7,8},{8,9},{9,10},{10,1... | collective-permute-start | bytes 405512 | tf_op jit(solution)/shard_map/ppermute | solution.py:531
  89.1 7.6 %collective-permute-start.7 = (bf16[66,8,128]{2,1,0:T(8,128)(2,1)S(1)}, bf16[66,8,128]{2,1,0:T(8,128)(2,1)S(1)}, u32[]{:S(2)}, u32[]{:S(2)}) collective-permute-start(bf16[66,8,128]{2,1,0:T(8,128)(2,1)S(1)} %get-tuple-element.28), channel_id=1, source_target_pairs={{1,0},{2,1},{3,2},{4,3},{5,4},{6,5},{7,6},{8,7},{9,8},{10,9},{11,1... | collective-permute-start | bytes 405512 | tf_op jit(solution)/shard_map/ppermute | solution.py:532
  91.7 14.1 %copy-start.10 = (bf16[66,8,128]{2,1,0:T(8,128)(2,1)}, bf16[66,8,128]{2,1,0:T(8,128)(2,1)S(1)}, u32[]{:S(2)}) copy-start(bf16[66,8,128]{2,1,0:T(8,128)(2,1)S(1)} %collective-permute-done.6.left_ref) | copy-start | bytes 405508
  96.8 9.1 %copy-start.11 = (bf16[66,8,128]{2,1,0:T(8,128)(2,1)}, bf16[66,8,128]{2,1,0:T(8,128)(2,1)S(1)}, u32[]{:S(2)}) copy-start(bf16[66,8,128]{2,1,0:T(8,128)(2,1)S(1)} %collective-permute-done.7.right_ref) | copy-start | bytes 405508
  99.9 19.8 %all-to-all-start.2 = ((bf16[128,16,128]{2,1,0:T(8,128)(2,1)}), bf16[128,16,128]{2,1,0:T(8,128)(2,1)S(1)}, u32[]{:S(2)}, u32[]{:S(2)}) async-start(bf16[128,16,128]{2,1,0:T(8,128)(2,1)} %share.1), calls=%async_computation.2 | async-start | bytes 1048576 | tf_op jit(solution)/shard_map/all_to_all | solution.py:569

commit v5 on v3

--- a/solution.py
+++ b/solution.py
@@ -2,6 +2,7 @@
 
 import jax
 import jax.numpy as jnp
+import numpy as np
 from jax import lax
 from jax.experimental import pallas as pl
 from jax.experimental.pallas import tpu as pltpu
@@ -95,123 +96,100 @@
     return jnp.where((tap >= 0.0) & (tap <= 7.0), weight, 0.0)
 
 
-def column_shift():
-    spot = lax.broadcasted_iota(jnp.int32, (128, 384), 0)
-    want = lax.broadcasted_iota(jnp.int32, (128, 384), 1)
-    want = want % 128 + want // 128 - 1
-    return jnp.where(spot == want, 1.0, 0.0).astype(BF16)
-
-
-def identity():
-    return jnp.where(
-        lax.broadcasted_iota(jnp.int32, (128, 128), 0)
-        == lax.broadcasted_iota(jnp.int32, (128, 128), 1),
-        1.0,
-        0.0,
-    ).astype(BF16)
-
-
-def turn_lines(lines, eye, shift):
-    turned = jnp.concatenate([nt(eye, x).astype(BF16) for x in lines], axis=0)
-    moved = mm(turned, shift).astype(BF16)
-    return [moved[:, b * 128 : (b + 1) * 128].reshape(len(lines), 128, 128) for b in range(3)]
-
-
-def prep_kernel(feat_ref, out_ref):
-    moved = turn_lines([feat_ref[i] for i in range(8)], identity(), column_shift())
+def picks():
+    eye = np.eye(128, dtype=np.float32)
+    shift = np.concatenate([np.eye(128, k=1), np.eye(128, k=-1)], axis=1)
+    wanted = (
+        {0: 3, 1: 4, 2: 5, 3: 6, 4: 31, 5: 8, 6: 9, 7: 10, 8: 7},
+        {0: 4, 1: 5, 2: 6, 3: 7, 4: 8, 5: 9, 6: 10, 7: 11},
+        {0: 5, 1: 6, 2: 7, 3: 16, 4: 9, 5: 10, 6: 11, 7: 12, 9: 8},
+    )
+    side = np.zeros((8, 32, 3, 8, 16), np.float32)
     for b in range(3):
-        out_ref[b] = moved[b]
-
-
-def prep(features):
+        for target, source in wanted[b].items():
+            for line in range(8):
+                side[line, source, b, line, target] = 1.0
+    return [jnp.asarray(x, BF16) for x in (eye, shift, side.reshape(256, 384))]
+
+
+def prep_kernel(eye_ref, shift_ref, feat_ref, out_ref):
+    eye = eye_ref[...]
+    turned = jnp.concatenate([nt(eye, feat_ref[i]).astype(BF16) for i in range(8)], axis=0)
+    moved = mm(turned, shift_ref[...]).astype(BF16)
+    out_ref[0] = moved[:, 0:128].reshape(8, 128, 128)
+    out_ref[1] = turned.reshape(8, 128, 128)
+    out_ref[2] = moved[:, 128:256].reshape(8, 128, 128)
+
+
+def prep(eye, shift, features):
     return pl.pallas_call(
         prep_kernel,
         grid=(8,),
         out_shape=jax.ShapeDtypeStruct((3, 64, 128, 128), BF16),
-        in_specs=[pl.BlockSpec((8, 128, 128), lambda i: (i, 0, 0))],
+        in_specs=[
+            pl.BlockSpec((128, 128), lambda i: (0, 0)),
+            pl.BlockSpec((128, 256), lambda i: (0, 0)),
+            pl.BlockSpec((8, 128, 128), lambda i: (i, 0, 0)),
+        ],
         out_specs=pl.BlockSpec((3, 8, 128, 128), lambda i: (0, i, 0, 0)),
         cost_estimate=pl.CostEstimate(
             flops=2_200_000_000, bytes_accessed=8_000_000, transcendentals=0
         ),
         name="prep",
-    )(features)
-
-
-def prep_edge_kernel(head_ref, last_ref, above_ref, below_ref, left_ref, right_ref, out_ref, side_ref):
-    eye = identity()
-    shift = column_shift()
-    moved = turn_lines(
-        [above_ref[i] for i in range(5)] + [below_ref[i] for i in range(5)], eye, shift
-    )
-    for b in range(3):
-        out_ref[b] = moved[b]
-    left = left_ref[...].astype(F32)
-    right = right_ref[...].astype(F32)
-    first = head_ref[...].astype(F32)
-    last = last_ref[...].astype(F32)
-    none = jnp.zeros((74, 8, 128), F32)
-    groups = (
-        (left[:, 3:7], last[:, 7:8], right[:, 0:3], left[:, 7:8], none[:, :7]),
-        (left[:, 4:8], right[:, 0:4], none),
-        (left[:, 5:8], first[:, 0:1], right[:, 1:5], none[:, :1], right[:, 0:1], none[:, :6]),
-    )
-    for b in range(3):
-        cells = jnp.concatenate(groups[b], axis=1).reshape(1184, 128)
-        cells = jnp.concatenate([cells, jnp.zeros((96, 128), F32)], axis=0).astype(BF16)
-        side_ref[b * 128 : (b + 1) * 128, :] = nt(eye, cells).astype(BF16)
-
-
-def prep_edge(head, last, above, below, left, right):
+    )(eye, shift, features)
+
+
+def prep_side_kernel(eye_ref, pick_ref, left_ref, right_ref, head_ref, last_ref, side_ref, cells):
+    for at, ref in enumerate((left_ref, right_ref, head_ref, last_ref)):
+        cells[:, at * 8 : at * 8 + 8, :] = ref[...]
+    turned = nt(eye_ref[...], cells[...].reshape(2048, 128)).astype(BF16)
+    for g in range(8):
+        moved = mm(turned[:, g * 256 : (g + 1) * 256], pick_ref[...]).astype(BF16)
+        for b in range(3):
+            side_ref[b * 128 : (b + 1) * 128, g * 128 : (g + 1) * 128] = moved[
+                :, b * 128 : (b + 1) * 128
+            ]
+
+
+def prep_side(eye, pick, left, right, head, last):
     vmem = pl.BlockSpec(memory_space=pltpu.VMEM)
     return pl.pallas_call(
-        prep_edge_kernel,
-        out_shape=(
-            jax.ShapeDtypeStruct((3, 10, 128, 128), BF16),
-            jax.ShapeDtypeStruct((384, 1280), BF16),
+        prep_side_kernel,
+        out_shape=jax.ShapeDtypeStruct((384, 1024), BF16),
+        in_specs=[vmem] * 6,
+        out_specs=vmem,
+        scratch_shapes=[pltpu.VMEM((64, 32, 128), BF16)],
+        cost_estimate=pl.CostEstimate(
+            flops=300_000_000, bytes_accessed=1_500_000, transcendentals=0
         ),
-        in_specs=[vmem] * 6,
-        out_specs=(vmem, vmem),
-        cost_estimate=pl.CostEstimate(
-            flops=500_000_000, bytes_accessed=3_000_000, transcendentals=0
-        ),
-        name="prep_edge",
-    )(head, last, above, below, left, right)
+        name="prep_side",
+    )(eye, pick, left, right, head, last)
 
 
 def scatter_kernel(
     edge_ref,
     in_ref,
-    feat_hbm,
-    feat_edge_hbm,
-    feat_side_hbm,
     canvas_hbm,
+    side_hbm,
     rim_hbm,
     up_hbm,
     down_hbm,
-    sum_hbm,
     rows_ref,
     lat_w,
     lon_w,
     side_w,
-    three,
-    three_side,
-    acc_ref,
-    feat_ref,
-    feat_edge_ref,
-    feat_side_ref,
     canvas_ref,
+    side_ref,
     rim_ref,
-    sum_ref,
-    load_sem,
+    block_sem,
     store_sem,
 ):
-    loads = [
-        pltpu.make_async_copy(feat_hbm, feat_ref, load_sem.at[0]),
-        pltpu.make_async_copy(feat_edge_hbm, feat_edge_ref, load_sem.at[1]),
-        pltpu.make_async_copy(feat_side_hbm, feat_side_ref, load_sem.at[2]),
-    ]
-    for copy in loads:
-        copy.start()
+    def block_store(step):
+        lines = pl.ds(pl.multiple_of(step * 8, 8), 8)
+        return pltpu.make_async_copy(
+            canvas_ref.at[lines], canvas_hbm.at[lines], block_sem.at[step]
+        )
+
     total = TILES * SLOTS
     rows_ref[...] = in_ref[:, 0:SLOTS, :].reshape(total, 128)
     tail = in_ref[:, SLOTS:CHUNK, :].reshape(TILES * (CHUNK - SLOTS), 128)
@@ -248,21 +226,6 @@
     line8 = lax.broadcasted_iota(jnp.int32, (8, total), 0)
     column = jnp.where(line8 < 4, line8 - 4, line8 + 124).astype(F32)
     side_w[...] = tap_weights(cell_lon, frac_lon, column).astype(BF16).astype(F32)
-    blank = jnp.zeros((2, 128, 128), BF16)
-    three[0:2, :, 256:384] = blank
-    three[72:74, :, 0:128] = blank
-    three[0:1, :, 128:256] = blank[:1]
-    three[73:74, :, 128:256] = blank[:1]
-    three_side[...] = jnp.zeros_like(three_side)
-    acc_ref[...] = jnp.zeros_like(acc_ref)
-
-    def weight_part(take, at):
-        lhs = jnp.concatenate([jnp.concatenate(take(b), axis=1) for b in range(3)], axis=0)
-        rhs = jnp.concatenate(
-            [three[x:y].reshape((y - x) * 128, 384) for x, y in at], axis=0
-        )
-        acc_ref[...] += mm(lhs, rhs)
-
     def eight_lines(step, carry):
         start = pl.multiple_of(step * 8, 8)
         lat8 = lat_w[pl.ds(start, 8), :]
@@ -284,58 +247,36 @@
             rows = rows_ref[cols, :]
             acc = acc + mm(jnp.concatenate(parts, axis=0), rows)
             side = side + mm(jnp.concatenate(side_parts, axis=0).astype(BF16), rows)
-        main = acc.astype(BF16).reshape(8, 128, 128)
-        canvas_ref[pl.ds(start, 8), 0:128, :] = main
-        for a in range(3):
-            three[pl.ds(start + a, 8), :, a * 128 : (a + 1) * 128] = main
+        ends = acc.reshape(8, 128, 128)
         side = side.reshape(8, 8, 128)
-        canvas_ref[pl.ds(start, 8), 128:136, :] = side.astype(BF16)
-        ends = acc.reshape(8, 128, 128)
-        side = jnp.concatenate(
+        lines = pl.ds(start, 8)
+        canvas_ref[lines, 0:128, :] = ends.astype(BF16)
+        canvas_ref[lines, 128:136, :] = side.astype(BF16)
+        block_store(step).start()
+        side_ref[lines] = jnp.concatenate(
             [side, ends[:, 0:1], ends[:, 127:128], jnp.zeros((8, 6, 128), F32)], axis=1
-        )
-        for a in range(3):
-            three_side[pl.ds(start + a, 8), :, a * 128 : (a + 1) * 128] = side
-        rim_ref[pl.ds(start, 8), 0:8, :] = ends[:, 0:8].astype(BF16)
-        rim_ref[pl.ds(start, 8), 8:16, :] = ends[:, 120:128].astype(BF16)
-        rim_ref[pl.ds(start, 8), 16:24, :] = side[:, 0:8].astype(BF16)
+        ).astype(BF16)
+        rim_ref[lines, 0:8, :] = ends[:, 0:8].astype(BF16)
+        rim_ref[lines, 8:16, :] = ends[:, 120:128].astype(BF16)
+        rim_ref[lines, 16:24, :] = side.astype(BF16)
         return carry
 
     lax.fori_loop(0, 9, eight_lines, 0)
     stores = [
-        pltpu.make_async_copy(canvas_ref, canvas_hbm, store_sem.at[0]),
-        pltpu.make_async_copy(rim_ref, rim_hbm, store_sem.at[1]),
-        pltpu.make_async_copy(canvas_ref.at[1:5], up_hbm, store_sem.at[2]),
-        pltpu.make_async_copy(canvas_ref.at[67:72], down_hbm, store_sem.at[3]),
+        pltpu.make_async_copy(canvas_ref.at[1:5], up_hbm, store_sem.at[0]),
+        pltpu.make_async_copy(canvas_ref.at[67:72], down_hbm, store_sem.at[1]),
+        pltpu.make_async_copy(side_ref, side_hbm, store_sem.at[2]),
+        pltpu.make_async_copy(rim_ref, rim_hbm, store_sem.at[3]),
     ]
     for copy in stores:
         copy.start()
-    for copy in loads:
-        copy.wait()
-    for part in range(2):
-        weight_part(
-            lambda b: [feat_ref[b, part * 32 + i] for i in range(32)],
-            ((5 + part * 32, 37 + part * 32),),
-        )
-    weight_part(lambda b: [feat_edge_ref[b, i] for i in range(10)], ((0, 5), (69, 74)))
-    acc = acc_ref[...] + mm(
-        feat_side_ref[...], three_side[...].reshape(1280, 384).astype(BF16)
-    )
-    for a in range(3):
-        for b in range(3):
-            at = (a * 3 + b) * 128
-            sum_ref[at : at + 128, :] = acc[
-                b * 128 : (b + 1) * 128, a * 128 : (a + 1) * 128
-            ].astype(BF16)
-    sum_ref[1152:, :] = jnp.zeros((2048 - 1152, 128), BF16)
-    last = pltpu.make_async_copy(sum_ref, sum_hbm, store_sem.at[4])
-    last.start()
+    for step in range(9):
+        block_store(step).wait()
     for copy in stores:
         copy.wait()
-    last.wait()
-
-
-def scatter(edge, incoming, feat, feat_edge, feat_side):
+
+
+def scatter(edge, incoming):
     vmem = pl.BlockSpec(memory_space=pltpu.VMEM)
     hbm = pl.BlockSpec(memory_space=pltpu.HBM)
     total = TILES * SLOTS
@@ -343,36 +284,179 @@
         scatter_kernel,
         out_shape=(
             jax.ShapeDtypeStruct((72, 136, 128), BF16),
+            jax.ShapeDtypeStruct((72, 16, 128), BF16),
             jax.ShapeDtypeStruct((72, 24, 128), BF16),
             jax.ShapeDtypeStruct((4, 136, 128), BF16),
             jax.ShapeDtypeStruct((5, 136, 128), BF16),
-            jax.ShapeDtypeStruct((2048, 128), BF16),
         ),
-        in_specs=[pl.BlockSpec(memory_space=pltpu.SMEM), vmem] + [hbm] * 3,
+        in_specs=[pl.BlockSpec(memory_space=pltpu.SMEM), vmem],
         out_specs=(hbm,) * 5,
         scratch_shapes=[
             pltpu.VMEM((total, 128), BF16),
             pltpu.VMEM((72, total), F32),
             pltpu.VMEM((128, total), BF16),
             pltpu.VMEM((8, total), F32),
-            pltpu.VMEM((74, 128, 384), BF16),
-            pltpu.VMEM((80, 16, 384), F32),
-            pltpu.VMEM((384, 384), F32),
+            pltpu.VMEM((72, 136, 128), BF16),
+            pltpu.VMEM((72, 16, 128), BF16),
+            pltpu.VMEM((72, 24, 128), BF16),
+            pltpu.SemaphoreType.DMA((9,)),
+            pltpu.SemaphoreType.DMA((4,)),
+        ],
+        compiler_params=pltpu.CompilerParams(vmem_limit_bytes=62_000_000),
+        cost_estimate=pl.CostEstimate(
+            flops=5_200_000_000, bytes_accessed=4_000_000, transcendentals=500_000
+        ),
+        name="scatter",
+    )(edge, incoming)
+
+
+def own_grad_kernel(
+    canvas_hbm, side_hbm, feat_hbm, feat_side_hbm, acc_ref, canvas, side, feat, feat_side, sem
+):
+    step = 16
+    loads = [
+        pltpu.make_async_copy(canvas_hbm.at[3:69], canvas, sem.at[4]),
+        *[
+            pltpu.make_async_copy(
+                feat_hbm.at[:, k * step : (k + 1) * step],
+                feat.at[:, k * step : (k + 1) * step],
+                sem.at[k],
+            )
+            for k in range(4)
+        ],
+        pltpu.make_async_copy(side_hbm.at[3:69], side, sem.at[5]),
+        pltpu.make_async_copy(feat_side_hbm, feat_side, sem.at[6]),
+    ]
+    for copy in loads:
+        copy.start()
+    loads[0].wait()
+    total = jnp.zeros((384, 384), F32)
+    for k in range(4):
+        loads[1 + k].wait()
+        lines = range(k * step, (k + 1) * step)
+        lhs = jnp.concatenate(
+            [jnp.concatenate([feat[b, i] for i in lines], axis=1) for b in range(3)], axis=0
+        )
+        rhs = jnp.concatenate(
+            [
+                canvas[k * step + 2 - a : (k + 1) * step + 2 - a, 0:128, :].reshape(
+                    step * 128, 128
+                )
+                for a in range(3)
+            ],
+            axis=1,
+        )
+        total = total + mm(lhs, rhs)
+    loads[5].wait()
+    loads[6].wait()
+    rhs = jnp.concatenate(
+        [side[2 - a : 66 - a].reshape(1024, 128) for a in range(3)], axis=1
+    )
+    acc_ref[...] = total + mm(feat_side[...], rhs)
+
+
+def own_grad(canvas, side, feat, feat_side):
+    hbm = pl.BlockSpec(memory_space=pltpu.HBM)
+    return pl.pallas_call(
+        own_grad_kernel,
+        out_shape=jax.ShapeDtypeStruct((384, 384), F32),
+        in_specs=[hbm] * 4,
+        out_specs=pl.BlockSpec(memory_space=pltpu.VMEM),
+        scratch_shapes=[
+            pltpu.VMEM((66, 136, 128), BF16),
+            pltpu.VMEM((66, 16, 128), BF16),
             pltpu.VMEM((3, 64, 128, 128), BF16),
-            pltpu.VMEM((3, 10, 128, 128), BF16),
-            pltpu.VMEM((384, 1280), BF16),
-            pltpu.VMEM((72, 136, 128), BF16),
-            pltpu.VMEM((72, 24, 128), BF16),
+            pltpu.VMEM((384, 1024), BF16),
+            pltpu.SemaphoreType.DMA((7,)),
+        ],
+        cost_estimate=pl.CostEstimate(
+            flops=2_800_000_000, bytes_accessed=10_000_000, transcendentals=0
+        ),
+        compiler_params=pltpu.CompilerParams(vmem_limit_bytes=62_000_000),
+        name="own_grad",
+    )(canvas, side, feat, feat_side)
+
+
+def halo_grad_kernel(
+    acc_ref, above_ref, below_ref, feat_hbm, feat_side_ref, sum_hbm, feat, sums, sem
+):
+    top = pltpu.make_async_copy(feat_hbm.at[:, 0:5], feat.at[:, 0:5], sem.at[0])
+    bottom = pltpu.make_async_copy(feat_hbm.at[:, 60:64], feat.at[:, 5:9], sem.at[1])
+    top.start()
+    bottom.start()
+    sums[1152:, :] = jnp.zeros((2048 - 1152, 128), BF16)
+
+    def beside(ref, count):
+        eight = ref[:, 128:136, :].astype(F32)
+        first = ref[:, 0:8, :].astype(F32)
+        last = ref[:, 120:128, :].astype(F32)
+        return jnp.concatenate(
+            [eight, first[:, 0:1], last[:, 7:8], jnp.zeros((count, 6, 128), F32)], axis=1
+        ).astype(BF16)
+
+    def lines(count, width):
+        return jnp.zeros((count, width, 128), BF16)
+
+    above = jnp.concatenate([above_ref[:, 0:128, :], lines(2, 128)], axis=0)
+    below = jnp.concatenate([lines(2, 128), below_ref[:, 0:128, :]], axis=0)
+    rhs = jnp.concatenate(
+        [
+            jnp.concatenate([above[2 - a : 7 - a], below[2 - a : 6 - a]], axis=0).reshape(
+                9 * 128, 128
+            )
+            for a in range(3)
+        ],
+        axis=1,
+    )
+    above = jnp.concatenate([beside(above_ref, 5), lines(5, 16)], axis=0)
+    below = jnp.concatenate([lines(6, 16), beside(below_ref, 4)], axis=0)
+    rhs_side = jnp.concatenate(
+        [
+            jnp.concatenate([above[2 - a : 10 - a], below[2 - a : 10 - a]], axis=0).reshape(
+                256, 128
+            )
+            for a in range(3)
+        ],
+        axis=1,
+    )
+    lhs_side = jnp.concatenate([feat_side_ref[:, 0:128], feat_side_ref[:, 896:1024]], axis=1)
+    total = acc_ref[...] + mm(lhs_side, rhs_side)
+    top.wait()
+    bottom.wait()
+    lhs = jnp.concatenate(
+        [jnp.concatenate([feat[b, i] for i in range(9)], axis=1) for b in range(3)], axis=0
+    )
+    total = total + mm(lhs, rhs)
+    for a in range(3):
+        for b in range(3):
+            at = (a * 3 + b) * 128
+            sums[at : at + 128, :] = total[
+                b * 128 : (b + 1) * 128, a * 128 : (a + 1) * 128
+            ].astype(BF16)
+    store = pltpu.make_async_copy(sums, sum_hbm, sem.at[2])
+    store.start()
+    store.wait()
+
+
+def halo_grad(acc, above, below, feat, feat_side):
+    vmem = pl.BlockSpec(memory_space=pltpu.VMEM)
+    hbm = pl.BlockSpec(memory_space=pltpu.HBM)
+    return pl.pallas_call(
+        halo_grad_kernel,
+        out_shape=jax.ShapeDtypeStruct((2048, 128), BF16),
+        in_specs=[vmem, vmem, vmem, hbm, vmem],
+        out_specs=hbm,
+        scratch_shapes=[
+            pltpu.VMEM((3, 9, 128, 128), BF16),
             pltpu.VMEM((2048, 128), BF16),
             pltpu.SemaphoreType.DMA((3,)),
-            pltpu.SemaphoreType.DMA((5,)),
         ],
-        compiler_params=pltpu.CompilerParams(vmem_limit_bytes=MOST_VMEM),
         cost_estimate=pl.CostEstimate(
-            flops=8_200_000_000, bytes_accessed=12_000_000, transcendentals=500_000
+            flops=420_000_000, bytes_accessed=3_500_000, transcendentals=0
         ),
-        name="scatter",
-    )(edge, incoming, feat, feat_edge, feat_side)
+        compiler_params=pltpu.CompilerParams(vmem_limit_bytes=58_000_000),
+        name="halo_grad",
+    )(acc, above, below, feat, feat_side)
 
 
 def sides_kernel(rim_ref, above_ref, below_ref, right_ref, left_ref):
@@ -545,20 +629,19 @@
         grad_rows,
     )
     incoming = lax.all_to_all(outgoing, AXES, 0, 0, tiled=True)
-    above, below = both_ways(features[59:64], features[0:5], "lat", False)
-    last, head = [
-        jnp.concatenate([x[:, c : c + 8] for x in (above, features, below)], axis=0)
-        for c in (120, 0)
-    ]
+    eye, shift, pick = picks()
+    last, head = features[:, 120:128], features[:, 0:8]
     left, right = both_ways(last, head, "lon", True)
-    feat = prep(features)
-    feat_edge, feat_side = prep_edge(head, last, above, below, left, right)
-    canvas, rim, up, down, part = scatter(edge, incoming, feat, feat_edge, feat_side)
+    feat = prep(eye, shift, features)
+    feat_side = prep_side(eye, pick, left, right, head, last)
+    canvas, side, rim, up, down = scatter(edge, incoming)
+    grid_above, grid_below = both_ways(down, up, "lat", False)
+    acc = own_grad(canvas, side, feat, feat_side)
+    part = halo_grad(acc, grid_above, grid_below, feat, feat_side)
     got = lax.all_to_all(part.reshape(TILES, 16, 128), AXES, 0, 0, tiled=True)
-    grid_above, grid_below = both_ways(down, up, "lat", False)
     send_right, send_left = sides(rim, grid_above, grid_below)
-    got, send_right, send_left = lax.optimization_barrier((got, send_right, send_left))
     from_left, from_right = both_ways(send_right, send_left, "lon", True)
+    got, from_left, from_right = lax.optimization_barrier((got, from_left, from_right))
     every = lax.all_to_all(share(got), AXES, 0, 0, tiled=True)
     input_grad = conv(canvas, grid_above, grid_below, from_left, from_right, conv_weight)
     weight_grad = finish(every)

time: 124 us -> 119 us (0.960); the launches traced: 122 us -> 119 us
  starting transfers between devices: 48.1 us -> 41.6 us
  Pallas kernels: 47.1 us -> 53.5 us
  waiting for transfers between devices: 18.4 us -> 15.1 us
    pallas_call x1 -> x3, Pallas kernels: 3.23 us -> 14.2 us  [the longest x1 7.41 us: own_grad(): pl.pallas_call(own_grad_kernel, out_shape=jax.ShapeDtypeStruct((384, 384)...]
    ppermute x4 -> x3, waiting for transfers between devices: 13.3 us -> 6.33 us  [both_ways(): lax.ppermute(back, axis, [((i + 1) % count, i) for i in range(ends)])]
    all_to_all x1, waiting for transfers between devices: 0.01 us -> 4.69 us  [shards(): every = lax.all_to_all(share(got), AXES, 0, 0, tiled=True)]
    pallas_call x1, Pallas kernels: 20.1 us -> 16 us  [scatter(): pl.pallas_call(scatter_kernel, out_shape=(jax.ShapeDtypeStruct((72, 136,...]
    ppermute x4 -> x3, starting transfers between devices: 12.8 us -> 9.38 us  [both_ways(): lax.ppermute(forth, axis, [(i, (i + 1) % count) for i in range(ends)])]
    all_to_all x1, starting transfers between devices: 9.25 us -> 6.27 us  [shards(): every = lax.all_to_all(share(got), AXES, 0, 0, tiled=True)]
    ppermute x4 -> x3, waiting for transfers between devices: 3.71 us -> 1.99 us  [both_ways(): lax.ppermute(forth, axis, [(i, (i + 1) % count) for i in range(ends)])]
    all_to_all x1, starting transfers between devices: 10.3 us -> 12 us  [shards(): got = lax.all_to_all(part.reshape(TILES, 16, 128), AXES, 0, 0, tiled=True)]
  transfers between devices with their start and end apart: 11 -> 9, of which waited for: 5 -> 5; matrix products, arithmetic and copies ran while one was open for 1% -> 1% of each run, Pallas kernels for 20% -> 23%
where the time goes in v5:
time: 119 us
  Pallas kernels  53.5 us (45%)
  starting transfers between devices  41.6 us (35%)
  waiting for transfers between devices  15.1 us (13%)
  local copies, waits for them, and re-layouts  6.31 us (5%)
  between operations  1.44 us (1%)
    pallas_call x1, Pallas kernels, scatter(): pl.pallas_call(scatter_kernel, out_shape=(jax.ShapeDtypeStruct((72, 136,...  16 us
    all_to_all x1, starting transfers between devices, shards(): got = lax.all_to_all(part.reshape(TILES, 16, 128), AXES, 0, 0, tiled=True)  12 us
    all_to_all x1, starting transfers between devices, shards(): incoming = lax.all_to_all(outgoing, AXES, 0, 0, tiled=True)  11.5 us
    ppermute x3, starting transfers between devices, both_ways(): lax.ppermute(forth, axis, [(i, (i + 1) % count) for i in range(ends)])  9.38 us
    pallas_call x1, Pallas kernels, conv(): pl.pallas_call(conv_kernel, grid=(8,), out_shape=jax.ShapeDtypeStruct((64...  9.14 us
    pallas_call x1, Pallas kernels, prep(): pl.pallas_call(prep_kernel, grid=(8,), out_shape=jax.ShapeDtypeStruct((3,...  8.25 us
    pallas_call x1, Pallas kernels, own_grad(): pl.pallas_call(own_grad_kernel, out_shape=jax.ShapeDtypeStruct((384, 384)...  7.41 us
    ppermute x3, waiting for transfers between devices, both_ways(): lax.ppermute(back, axis, [((i + 1) % count, i) for i in range(ends)])  6.33 us
  transfers between devices with their start and end apart: 9, of which 5 were waited for; matrix products, arithmetic and copies ran while one was open for 1% of the time, Pallas kernels for 23%

profile of v5, /device:TPU:1, one launch (start us, length us, event | category | flops | bytes accessed | tf_op | source)
XLA Modules:
  0.0 118.6 jit_solution(12601283528308825025)
XLA Ops:
  1.3 3.5 %pack.1 = bf16[128,24,128]{2,1,0:T(8,128)(2,1)} custom-call(s32[1]{0:T(128)S(6)} %copy.13.live_ref, s32[1,1024]{1,0:T(1,128)} %bitcast.10, s32[1,1024]{1,0:T(1,128)} %bitcast.11, s32[1,1024]{1,0:T(1,128)} %bitcast.12, bf16[2,1024]{1,0:T(2,128)(2,1)} %bitcast.13, bf16[1024,128]{1,0:T(8,128)(2,1)} %rows_ref.1), custom_call_target="tpu_custom_call" | custom-call | flops 700000000 | bytes 1500000 | tf_op jit(solution)/shard_map/pack/pallas_call | solution.py:82
  4.8 11.5 %all-to-all-start = ((bf16[128,24,128]{2,1,0:T(8,128)(2,1)}), bf16[128,24,128]{2,1,0:T(8,128)(2,1)S(1)}, u32[]{:S(2)}, u32[]{:S(2)}) async-start(bf16[128,24,128]{2,1,0:T(8,128)(2,1)} %pack.1), calls=%async_computation | async-start | bytes 1572864 | tf_op jit(solution)/shard_map/all_to_all | solution.py:631
  16.3 1.0 fusion
  17.3 1.1 collective-permute-start.3
  18.4 2.2 %collective-permute-start.2 = (bf16[64,8,128]{2,1,0:T(8,128)(2,1)S(1)}, bf16[64,8,128]{2,1,0:T(8,128)(2,1)S(1)}, u32[]{:S(2)}, u32[]{:S(2)}) collective-permute-start(bf16[64,8,128]{2,1,0:T(8,128)(2,1)S(1)} %get-tuple-element.23.last_ref), channel_id=1, source_target_pairs={{0,1},{1,2},{2,3},{3,4},{4,5},{5,6},{6,7},{7,8},{8,9},{9,10},{10,1... | collective-permute-start | bytes 393224 | tf_op jit(solution)/shard_map/ppermute | solution.py:609
  20.6 8.3 %prep.1.feat_hbm = bf16[3,64,128,128]{3,2,1,0:T(8,128)(2,1)} custom-call(bf16[128,128]{1,0:T(8,128)(2,1)} %constant.22.clone.eye_ref, bf16[128,256]{1,0:T(8,128)(2,1)} %constant.23.clone.shift_ref, bf16[64,128,128]{2,1,0:T(8,128)(2,1)} %feat_ref.1), custom_call_target="tpu_custom_call" | custom-call | flops 2200000000 | bytes 8000000 | tf_op jit(solution)/shard_map/prep/pallas_call | solution.py:125
  28.9 0.6 pad_add_fusion.edge_ref
  29.5 1.5 %collective-permute-done.3.right_ref = bf16[64,8,128]{2,1,0:T(8,128)(2,1)S(1)} collective-permute-done((bf16[64,8,128]{2,1,0:T(8,128)(2,1)S(1)}, bf16[64,8,128]{2,1,0:T(8,128)(2,1)S(1)}, u32[]{:S(2)}, u32[]{:S(2)}) %collective-permute-start.3) | collective-permute-done | bytes 131104 | tf_op jit(solution)/shard_map/ppermute | solution.py:610
  31.0 0.6 copy-done.8
  31.6 0.7 copy-done.9
  32.3 2.7 %prep_side.1.feat_side_hbm.feat_side_ref = bf16[384,1024]{1,0:T(8,128)(2,1)} custom-call(bf16[128,128]{1,0:T(8,128)(2,1)} %constant.22.clone.eye_ref, bf16[256,384]{1,0:T(8,128)(2,1)} %constant.24.clone.pick_ref, bf16[64,8,128]{2,1,0:T(8,128)(2,1)} %copy-done.9, bf16[64,8,128]{2,1,0:T(8,128)(2,1)} %copy-done.8, bf16[64,8,128]{2,1,0:T(8,128)(2,1)} %copy-done.6, ...), custom_call_target="tpu_custom_call" | custom-call | flops 300000000 | bytes 1500000 | tf_op jit(solution)/shard_map/prep_side/pallas_call | solution.py:156
  35.0 0.9 copy-done.5
  35.9 16.0 %scatter.1 = (bf16[72,136,128]{2,1,0:T(8,128)(2,1)}, bf16[72,16,128]{2,1,0:T(8,128)(2,1)}, bf16[72,24,128]{2,1,0:T(8,128)(2,1)}, bf16[4,136,128]{2,1,0:T(8,128)(2,1)}, bf16[5,136,128]{2,1,0:T(8,128)(2,1)}) custom-call(s32[2]{0:T(128)} %pad_add_fusion.edge_ref, bf16[128,24,128]{2,1,0:T(8,128)(2,1)} %copy-done.5), custom_call_target="tpu_custom_call" | custom-call | flops 5200000000 | bytes 4000000 | tf_op jit(solution)/shard_map/scatter/pallas_call | solution.py:283
  51.8 1.3 %collective-permute-start.1 = (bf16[4,136,128]{2,1,0:T(8,128)(2,1)}, bf16[4,136,128]{2,1,0:T(8,128)(2,1)S(1)}, u32[]{:S(2)}, u32[]{:S(2)}) collective-permute-start(bf16[4,136,128]{2,1,0:T(8,128)(2,1)} %get-tuple-element.14), channel_id=1, source_target_pairs={{16,0},{32,16},{48,32},{64,48},{80,64},{96,80},{112,96},{17,1},{33... | collective-permute-start | bytes 417800 | tf_op jit(solution)/shard_map/ppermute | solution.py:610
  53.1 4.0 %collective-permute-start = (bf16[5,136,128]{2,1,0:T(8,128)(2,1)}, bf16[5,136,128]{2,1,0:T(8,128)(2,1)S(1)}, u32[]{:S(2)}, u32[]{:S(2)}) collective-permute-start(bf16[5,136,128]{2,1,0:T(8,128)(2,1)} %get-tuple-element.13), channel_id=1, source_target_pairs={{0,16},{16,32},{32,48},{48,64},{64,80},{80,96},{96,112},{1,17},{17... | collective-permute-start | bytes 522248 | tf_op jit(solution)/shard_map/ppermute | solution.py:609
  57.1 7.4 %own_grad.1.acc_ref = f32[384,384]{1,0:T(8,128)} custom-call(bf16[72,136,128]{2,1,0:T(8,128)(2,1)} %get-tuple-element.12.canvas_hbm.canvas_ref, bf16[72,16,128]{2,1,0:T(8,128)(2,1)} %get-tuple-element.15.side_hbm, bf16[3,64,128,128]{3,2,1,0:T(8,128)(2,1)} %prep.1.feat_hbm, bf16[384,1024]{1,0:T(8,128)(2,1)} %prep_side.1.feat_side_hbm.feat_side_ref), custom_call_target="tpu_custom_call" | custom-call | flops 2800000000 | bytes 10000000 | tf_op jit(solution)/shard_map/own_grad/pallas_call | solution.py:360
  64.6 0.6 copy-done.2
  65.2 0.7 copy-done
  65.9 4.1 %halo_grad.1 = bf16[2048,128]{1,0:T(8,128)(2,1)} custom-call(f32[384,384]{1,0:T(8,128)} %own_grad.1.acc_ref, bf16[5,136,128]{2,1,0:T(8,128)(2,1)} %copy-done, bf16[4,136,128]{2,1,0:T(8,128)(2,1)} %copy-done.2, bf16[3,64,128,128]{3,2,1,0:T(8,128)(2,1)} %prep.1.feat_hbm, bf16[384,1024]{1,0:T(8,128)(2,1)} %prep_side.1.feat_side_hbm.feat_side_ref), custom_call_target="tpu_custom_call" | custom-call | flops 420000000 | bytes 3500000 | tf_op jit(solution)/shard_map/halo_grad/pallas_call | solution.py:444
  70.0 12.0 %all-to-all-start.1 = ((bf16[128,16,128]{2,1,0:T(8,128)(2,1)}), bf16[128,16,128]{2,1,0:T(8,128)(2,1)S(1)}, u32[]{:S(2)}, u32[]{:S(2)}) async-start(bf16[128,16,128]{2,1,0:T(8,128)(2,1)} %bitcast.8), calls=%async_computation.1 | async-start | bytes 1048576 | tf_op jit(solution)/shard_map/all_to_all | solution.py:641
  82.0 0.9 copy-done.1
  82.9 0.9 copy-done.3
  83.8 0.1 sides.1
  84.0 3.2 %collective-permute-start.4 = (bf16[66,8,128]{2,1,0:T(8,128)(2,1)S(1)}, bf16[66,8,128]{2,1,0:T(8,128)(2,1)S(1)}, u32[]{:S(2)}, u32[]{:S(2)}) collective-permute-start(bf16[66,8,128]{2,1,0:T(8,128)(2,1)S(1)} %get-tuple-element.17), channel_id=1, source_target_pairs={{0,1},{1,2},{2,3},{3,4},{4,5},{5,6},{6,7},{7,8},{8,9},{9,10},{10,1... | collective-permute-start | bytes 405512 | tf_op jit(solution)/shard_map/ppermute | solution.py:609
  87.2 2.0 %collective-permute-done.4.left_ref = bf16[66,8,128]{2,1,0:T(8,128)(2,1)S(1)} collective-permute-done((bf16[66,8,128]{2,1,0:T(8,128)(2,1)S(1)}, bf16[66,8,128]{2,1,0:T(8,128)(2,1)S(1)}, u32[]{:S(2)}, u32[]{:S(2)}) %collective-permute-start.4) | collective-permute-done | bytes 135200 | tf_op jit(solution)/shard_map/ppermute | solution.py:609
  89.2 4.8 %collective-permute-done.5.right_ref = bf16[66,8,128]{2,1,0:T(8,128)(2,1)S(1)} collective-permute-done((bf16[66,8,128]{2,1,0:T(8,128)(2,1)S(1)}, bf16[66,8,128]{2,1,0:T(8,128)(2,1)S(1)}, u32[]{:S(2)}, u32[]{:S(2)}) %collective-permute-start.5) | collective-permute-done | bytes 135200 | tf_op jit(solution)/shard_map/ppermute | solution.py:610
  94.0 2.1 %all-to-all-done.1.in_ref = bf16[128,16,128]{2,1,0:T(8,128)(2,1)S(1)} async-done(((bf16[128,16,128]{2,1,0:T(8,128)(2,1)}), bf16[128,16,128]{2,1,0:T(8,128)(2,1)S(1)}, u32[]{:S(2)}, u32[]{:S(2)}) %all-to-all-start.1) | async-done | bytes 524320 | tf_op jit(solution)/shard_map/all_to_all | solution.py:641
  96.1 1.0 share.1
  97.1 6.3 %all-to-all-start.2 = ((bf16[128,16,128]{2,1,0:T(8,128)(2,1)}), bf16[128,16,128]{2,1,0:T(8,128)(2,1)S(1)}, u32[]{:S(2)}, u32[]{:S(2)}) async-start(bf16[128,16,128]{2,1,0:T(8,128)(2,1)} %share.1), calls=%async_computation.2 | async-start | bytes 1048576 | tf_op jit(solution)/shard_map/all_to_all | solution.py:645
  103.4 9.1 %conv.1 = bf16[64,128,128]{2,1,0:T(8,128)(2,1)} custom-call(bf16[72,136,128]{2,1,0:T(8,128)(2,1)} %get-tuple-element.12.canvas_hbm.canvas_ref, bf16[5,136,128]{2,1,0:T(8,128)(2,1)} %copy-done, bf16[4,136,128]{2,1,0:T(8,128)(2,1)} %copy-done.2, bf16[66,8,128]{2,1,0:T(8,128)(2,1)} %copy-done.10, bf16[66,8,128]{2,1,0:T(8,128)(2,1)} %copy-done.11, ...), custom_call_target="tpu_custom_call" | custom-call | flops 2700000000 | bytes 4500000 | tf_op jit(solution)/shard_map/conv/pallas_call | solution.py:555
  112.5 4.7 %all-to-all-done.2.in_ref = bf16[128,16,128]{2,1,0:T(8,128)(2,1)S(1)} async-done(((bf16[128,16,128]{2,1,0:T(8,128)(2,1)}), bf16[128,16,128]{2,1,0:T(8,128)(2,1)S(1)}, u32[]{:S(2)}, u32[]{:S(2)}) %all-to-all-start.2) | async-done | bytes 524320 | tf_op jit(solution)/shard_map/all_to_all | solution.py:645
  117.2 1.4 %finish.1 = f32[1152,128]{1,0:T(8,128)} custom-call(bf16[128,16,128]{2,1,0:T(8,128)(2,1)S(1)} %all-to-all-done.2.in_ref), custom_call_target="tpu_custom_call" | custom-call | bytes 900000 | tf_op jit(solution)/shard_map/finish/pallas_call | solution.py:593
  (22 shorter events, 0.0 us)
Async XLA Ops:
  4.8 30.2 %all-to-all-start = ((bf16[128,24,128]{2,1,0:T(8,128)(2,1)}), bf16[128,24,128]{2,1,0:T(8,128)(2,1)S(1)}, u32[]{:S(2)}, u32[]{:S(2)}) async-start(bf16[128,24,128]{2,1,0:T(8,128)(2,1)} %pack.1), calls=%async_computation | async-start | bytes 1572864 | tf_op jit(solution)/shard_map/all_to_all | solution.py:631
  17.3 11.6 %copy-start.6 = (bf16[64,8,128]{2,1,0:T(8,128)(2,1)}, bf16[64,8,128]{2,1,0:T(8,128)(2,1)S(1)}, u32[]{:S(2)}) copy-start(bf16[64,8,128]{2,1,0:T(8,128)(2,1)S(1)} %get-tuple-element.22.head_ref) | copy-start | bytes 393220
  17.3 11.6 %copy-start.7 = (bf16[64,8,128]{2,1,0:T(8,128)(2,1)}, bf16[64,8,128]{2,1,0:T(8,128)(2,1)S(1)}, u32[]{:S(2)}) copy-start(bf16[64,8,128]{2,1,0:T(8,128)(2,1)S(1)} %get-tuple-element.23.last_ref) | copy-start | bytes 393220
  17.3 13.7 %collective-permute-start.3 = (bf16[64,8,128]{2,1,0:T(8,128)(2,1)S(1)}, bf16[64,8,128]{2,1,0:T(8,128)(2,1)S(1)}, u32[]{:S(2)}, u32[]{:S(2)}) collective-permute-start(bf16[64,8,128]{2,1,0:T(8,128)(2,1)S(1)} %get-tuple-element.22.head_ref), channel_id=1, source_target_pairs={{1,0},{2,1},{3,2},{4,3},{5,4},{6,5},{7,6},{8,7},{9,8},{10,9},{11,1... | collective-permute-start | bytes 393224 | tf_op jit(solution)/shard_map/ppermute | solution.py:610
  18.4 12.6 %collective-permute-start.2 = (bf16[64,8,128]{2,1,0:T(8,128)(2,1)S(1)}, bf16[64,8,128]{2,1,0:T(8,128)(2,1)S(1)}, u32[]{:S(2)}, u32[]{:S(2)}) collective-permute-start(bf16[64,8,128]{2,1,0:T(8,128)(2,1)S(1)} %get-tuple-element.23.last_ref), channel_id=1, source_target_pairs={{0,1},{1,2},{2,3},{3,4},{4,5},{5,6},{6,7},{7,8},{8,9},{9,10},{10,1... | collective-permute-start | bytes 393224 | tf_op jit(solution)/shard_map/ppermute | solution.py:609
  31.0 0.6 copy-start.8
  31.6 0.7 copy-start.9
  35.0 0.9 copy-start.5
  51.8 12.7 %collective-permute-start.1 = (bf16[4,136,128]{2,1,0:T(8,128)(2,1)}, bf16[4,136,128]{2,1,0:T(8,128)(2,1)S(1)}, u32[]{:S(2)}, u32[]{:S(2)}) collective-permute-start(bf16[4,136,128]{2,1,0:T(8,128)(2,1)} %get-tuple-element.14), channel_id=1, source_target_pairs={{16,0},{32,16},{48,32},{64,48},{80,64},{96,80},{112,96},{17,1},{33... | collective-permute-start | bytes 417800 | tf_op jit(solution)/shard_map/ppermute | solution.py:610
  53.1 11.5 %collective-permute-start = (bf16[5,136,128]{2,1,0:T(8,128)(2,1)}, bf16[5,136,128]{2,1,0:T(8,128)(2,1)S(1)}, u32[]{:S(2)}, u32[]{:S(2)}) collective-permute-start(bf16[5,136,128]{2,1,0:T(8,128)(2,1)} %get-tuple-element.13), channel_id=1, source_target_pairs={{0,16},{16,32},{32,48},{48,64},{64,80},{80,96},{96,112},{1,17},{17... | collective-permute-start | bytes 522248 | tf_op jit(solution)/shard_map/ppermute | solution.py:609
  64.6 17.4 %copy-start.4 = (bf16[72,24,128]{2,1,0:T(8,128)(2,1)S(1)}, bf16[72,24,128]{2,1,0:T(8,128)(2,1)}, u32[]{:S(2)}) copy-start(bf16[72,24,128]{2,1,0:T(8,128)(2,1)} %get-tuple-element.16.rim_ref) | copy-start | bytes 1327108
  64.6 0.6 copy-start.2
  65.2 0.7 copy-start
  70.0 26.1 %all-to-all-start.1 = ((bf16[128,16,128]{2,1,0:T(8,128)(2,1)}), bf16[128,16,128]{2,1,0:T(8,128)(2,1)S(1)}, u32[]{:S(2)}, u32[]{:S(2)}) async-start(bf16[128,16,128]{2,1,0:T(8,128)(2,1)} %bitcast.8), calls=%async_computation.1 | async-start | bytes 1048576 | tf_op jit(solution)/shard_map/all_to_all | solution.py:641
  82.0 0.9 copy-start.1
  82.9 0.9 copy-start.3
  84.0 5.2 %collective-permute-start.4 = (bf16[66,8,128]{2,1,0:T(8,128)(2,1)S(1)}, bf16[66,8,128]{2,1,0:T(8,128)(2,1)S(1)}, u32[]{:S(2)}, u32[]{:S(2)}) collective-permute-start(bf16[66,8,128]{2,1,0:T(8,128)(2,1)S(1)} %get-tuple-element.17), channel_id=1, source_target_pairs={{0,1},{1,2},{2,3},{3,4},{4,5},{5,6},{6,7},{7,8},{8,9},{9,10},{10,1... | collective-permute-start | bytes 405512 | tf_op jit(solution)/shard_map/ppermute | solution.py:609
  87.2 6.8 %collective-permute-start.5 = (bf16[66,8,128]{2,1,0:T(8,128)(2,1)S(1)}, bf16[66,8,128]{2,1,0:T(8,128)(2,1)S(1)}, u32[]{:S(2)}, u32[]{:S(2)}) collective-permute-start(bf16[66,8,128]{2,1,0:T(8,128)(2,1)S(1)} %get-tuple-element.18), channel_id=1, source_target_pairs={{1,0},{2,1},{3,2},{4,3},{5,4},{6,5},{7,6},{8,7},{9,8},{10,9},{11,1... | collective-permute-start | bytes 405512 | tf_op jit(solution)/shard_map/ppermute | solution.py:610
  89.2 14.2 %copy-start.10 = (bf16[66,8,128]{2,1,0:T(8,128)(2,1)}, bf16[66,8,128]{2,1,0:T(8,128)(2,1)S(1)}, u32[]{:S(2)}) copy-start(bf16[66,8,128]{2,1,0:T(8,128)(2,1)S(1)} %collective-permute-done.4.left_ref) | copy-start | bytes 405508
  94.0 9.4 %copy-start.11 = (bf16[66,8,128]{2,1,0:T(8,128)(2,1)}, bf16[66,8,128]{2,1,0:T(8,128)(2,1)S(1)}, u32[]{:S(2)}) copy-start(bf16[66,8,128]{2,1,0:T(8,128)(2,1)S(1)} %collective-permute-done.5.right_ref) | copy-start | bytes 405508
  97.1 20.1 %all-to-all-start.2 = ((bf16[128,16,128]{2,1,0:T(8,128)(2,1)}), bf16[128,16,128]{2,1,0:T(8,128)(2,1)S(1)}, u32[]{:S(2)}, u32[]{:S(2)}) async-start(bf16[128,16,128]{2,1,0:T(8,128)(2,1)} %share.1), calls=%async_computation.2 | async-start | bytes 1048576 | tf_op jit(solution)/shard_map/all_to_all | solution.py:645

commit v6 on v5

--- a/solution.py
+++ b/solution.py
@@ -14,7 +14,6 @@
 SLOTS = 16
 CHUNK = 24
 TILES = 128
-MOST_VMEM = 62_600_000
 GAUSS = 2.0 * 1.5 * 1.5
 
 
@@ -112,31 +111,31 @@
     return [jnp.asarray(x, BF16) for x in (eye, shift, side.reshape(256, 384))]
 
 
-def prep_kernel(eye_ref, shift_ref, feat_ref, out_ref):
-    eye = eye_ref[...]
-    turned = jnp.concatenate([nt(eye, feat_ref[i]).astype(BF16) for i in range(8)], axis=0)
+def prep_kernel(shift_ref, feat_ref, out_ref):
+    count = feat_ref.shape[0]
+    turned = jnp.concatenate([feat_ref[i].T for i in range(count)], axis=0)
     moved = mm(turned, shift_ref[...]).astype(BF16)
-    out_ref[0] = moved[:, 0:128].reshape(8, 128, 128)
-    out_ref[1] = turned.reshape(8, 128, 128)
-    out_ref[2] = moved[:, 128:256].reshape(8, 128, 128)
-
-
-def prep(eye, shift, features):
+    out_ref[:, 0] = moved[:, 0:128].reshape(count, 128, 128)
+    out_ref[:, 1] = turned.reshape(count, 128, 128)
+    out_ref[:, 2] = moved[:, 128:256].reshape(count, 128, 128)
+
+
+def prep(shift, features):
     return pl.pallas_call(
         prep_kernel,
-        grid=(8,),
-        out_shape=jax.ShapeDtypeStruct((3, 64, 128, 128), BF16),
+        grid=(4,),
+        out_shape=jax.ShapeDtypeStruct((64, 3, 128, 128), BF16),
         in_specs=[
-            pl.BlockSpec((128, 128), lambda i: (0, 0)),
             pl.BlockSpec((128, 256), lambda i: (0, 0)),
-            pl.BlockSpec((8, 128, 128), lambda i: (i, 0, 0)),
+            pl.BlockSpec((16, 128, 128), lambda i: (i, 0, 0)),
         ],
-        out_specs=pl.BlockSpec((3, 8, 128, 128), lambda i: (0, i, 0, 0)),
+        out_specs=pl.BlockSpec((16, 3, 128, 128), lambda i: (i, 0, 0, 0)),
         cost_estimate=pl.CostEstimate(
             flops=2_200_000_000, bytes_accessed=8_000_000, transcendentals=0
         ),
+        compiler_params=pltpu.CompilerParams(vmem_limit_bytes=12 << 20),
         name="prep",
-    )(eye, shift, features)
+    )(shift, features)
 
 
 def prep_side_kernel(eye_ref, pick_ref, left_ref, right_ref, head_ref, last_ref, side_ref, cells):
@@ -162,12 +161,12 @@
         cost_estimate=pl.CostEstimate(
             flops=300_000_000, bytes_accessed=1_500_000, transcendentals=0
         ),
+        compiler_params=pltpu.CompilerParams(vmem_limit_bytes=6 << 20),
         name="prep_side",
     )(eye, pick, left, right, head, last)
 
 
 def scatter_kernel(
-    edge_ref,
     in_ref,
     canvas_hbm,
     side_hbm,
@@ -217,7 +216,10 @@
         for f in range(4)
     ]
     line = lax.broadcasted_iota(jnp.int32, (72, total), 0)
-    kept = (line >= edge_ref[0]) & (line < edge_ref[1])
+    lat_index = lax.axis_index("lat")
+    first_line = jnp.where(lat_index == 0, 4, 0)
+    end_line = jnp.where(lat_index == lax.axis_size("lat") - 1, 68, 72)
+    kept = (line >= first_line) & (line < end_line)
     lat_w[...] = jnp.where(
         kept, tap_weights(cell_lat, frac_lat, line.astype(F32) - 4.0), 0.0
     )
@@ -276,7 +278,7 @@
         copy.wait()
 
 
-def scatter(edge, incoming):
+def scatter(incoming):
     vmem = pl.BlockSpec(memory_space=pltpu.VMEM)
     hbm = pl.BlockSpec(memory_space=pltpu.HBM)
     total = TILES * SLOTS
@@ -289,7 +291,7 @@
             jax.ShapeDtypeStruct((4, 136, 128), BF16),
             jax.ShapeDtypeStruct((5, 136, 128), BF16),
         ),
-        in_specs=[pl.BlockSpec(memory_space=pltpu.SMEM), vmem],
+        in_specs=[vmem],
         out_specs=(hbm,) * 5,
         scratch_shapes=[
             pltpu.VMEM((total, 128), BF16),
@@ -302,40 +304,50 @@
             pltpu.SemaphoreType.DMA((9,)),
             pltpu.SemaphoreType.DMA((4,)),
         ],
-        compiler_params=pltpu.CompilerParams(vmem_limit_bytes=62_000_000),
+        compiler_params=pltpu.CompilerParams(vmem_limit_bytes=24 << 20),
         cost_estimate=pl.CostEstimate(
             flops=5_200_000_000, bytes_accessed=4_000_000, transcendentals=500_000
         ),
         name="scatter",
-    )(edge, incoming)
+    )(incoming)
 
 
 def own_grad_kernel(
     canvas_hbm, side_hbm, feat_hbm, feat_side_hbm, acc_ref, canvas, side, feat, feat_side, sem
 ):
     step = 16
-    loads = [
-        pltpu.make_async_copy(canvas_hbm.at[3:69], canvas, sem.at[4]),
-        *[
+    ends = (0, 18, 34, 50, 66)
+    parts = [
+        (
             pltpu.make_async_copy(
-                feat_hbm.at[:, k * step : (k + 1) * step],
-                feat.at[:, k * step : (k + 1) * step],
-                sem.at[k],
-            )
-            for k in range(4)
-        ],
-        pltpu.make_async_copy(side_hbm.at[3:69], side, sem.at[5]),
-        pltpu.make_async_copy(feat_side_hbm, feat_side, sem.at[6]),
+                canvas_hbm.at[3 + ends[k] : 3 + ends[k + 1]],
+                canvas.at[ends[k] : ends[k + 1]],
+                sem.at[2 * k],
+            ),
+            pltpu.make_async_copy(
+                feat_hbm.at[k * step : (k + 1) * step],
+                feat.at[k * step : (k + 1) * step],
+                sem.at[2 * k + 1],
+            ),
+        )
+        for k in range(4)
     ]
-    for copy in loads:
+    rest = [
+        pltpu.make_async_copy(side_hbm.at[3:69], side, sem.at[8]),
+        pltpu.make_async_copy(feat_side_hbm, feat_side, sem.at[9]),
+    ]
+    for pair in parts:
+        for copy in pair:
+            copy.start()
+    for copy in rest:
         copy.start()
-    loads[0].wait()
     total = jnp.zeros((384, 384), F32)
     for k in range(4):
-        loads[1 + k].wait()
+        for copy in parts[k]:
+            copy.wait()
         lines = range(k * step, (k + 1) * step)
         lhs = jnp.concatenate(
-            [jnp.concatenate([feat[b, i] for i in lines], axis=1) for b in range(3)], axis=0
+            [jnp.concatenate([feat[i, b] for i in lines], axis=1) for b in range(3)], axis=0
         )
         rhs = jnp.concatenate(
             [
@@ -347,8 +359,8 @@
             axis=1,
         )
         total = total + mm(lhs, rhs)
-    loads[5].wait()
-    loads[6].wait()
+    for copy in rest:
+        copy.wait()
     rhs = jnp.concatenate(
         [side[2 - a : 66 - a].reshape(1024, 128) for a in range(3)], axis=1
     )
@@ -365,14 +377,14 @@
         scratch_shapes=[
             pltpu.VMEM((66, 136, 128), BF16),
             pltpu.VMEM((66, 16, 128), BF16),
-            pltpu.VMEM((3, 64, 128, 128), BF16),
+            pltpu.VMEM((64, 3, 128, 128), BF16),
             pltpu.VMEM((384, 1024), BF16),
-            pltpu.SemaphoreType.DMA((7,)),
+            pltpu.SemaphoreType.DMA((10,)),
         ],
         cost_estimate=pl.CostEstimate(
             flops=2_800_000_000, bytes_accessed=10_000_000, transcendentals=0
         ),
-        compiler_params=pltpu.CompilerParams(vmem_limit_bytes=62_000_000),
+        compiler_params=pltpu.CompilerParams(vmem_limit_bytes=20 << 20),
         name="own_grad",
     )(canvas, side, feat, feat_side)
 
@@ -380,8 +392,8 @@
 def halo_grad_kernel(
     acc_ref, above_ref, below_ref, feat_hbm, feat_side_ref, sum_hbm, feat, sums, sem
 ):
-    top = pltpu.make_async_copy(feat_hbm.at[:, 0:5], feat.at[:, 0:5], sem.at[0])
-    bottom = pltpu.make_async_copy(feat_hbm.at[:, 60:64], feat.at[:, 5:9], sem.at[1])
+    top = pltpu.make_async_copy(feat_hbm.at[0:5], feat.at[0:5], sem.at[0])
+    bottom = pltpu.make_async_copy(feat_hbm.at[60:64], feat.at[5:9], sem.at[1])
     top.start()
     bottom.start()
     sums[1152:, :] = jnp.zeros((2048 - 1152, 128), BF16)
@@ -424,7 +436,7 @@
     top.wait()
     bottom.wait()
     lhs = jnp.concatenate(
-        [jnp.concatenate([feat[b, i] for i in range(9)], axis=1) for b in range(3)], axis=0
+        [jnp.concatenate([feat[i, b] for i in range(9)], axis=1) for b in range(3)], axis=0
     )
     total = total + mm(lhs, rhs)
     for a in range(3):
@@ -447,14 +459,14 @@
         in_specs=[vmem, vmem, vmem, hbm, vmem],
         out_specs=hbm,
         scratch_shapes=[
-            pltpu.VMEM((3, 9, 128, 128), BF16),
+            pltpu.VMEM((9, 3, 128, 128), BF16),
             pltpu.VMEM((2048, 128), BF16),
             pltpu.SemaphoreType.DMA((3,)),
         ],
         cost_estimate=pl.CostEstimate(
             flops=420_000_000, bytes_accessed=3_500_000, transcendentals=0
         ),
-        compiler_params=pltpu.CompilerParams(vmem_limit_bytes=58_000_000),
+        compiler_params=pltpu.CompilerParams(vmem_limit_bytes=12 << 20),
         name="halo_grad",
     )(acc, above, below, feat, feat_side)
 
@@ -559,7 +571,7 @@
         in_specs=[whole(x) for x in args],
         out_specs=pl.BlockSpec((8, 128, 128), lambda i: (i, 0, 0)),
         scratch_shapes=[pltpu.VMEM((66, 144, 128), BF16)],
-        compiler_params=pltpu.CompilerParams(vmem_limit_bytes=MOST_VMEM),
+        compiler_params=pltpu.CompilerParams(vmem_limit_bytes=16 << 20),
         cost_estimate=pl.CostEstimate(
             flops=2_700_000_000, bytes_accessed=4_500_000, transcendentals=0
         ),
@@ -613,13 +625,6 @@
 
 def shards(grad_rows, owner, lat_offset, lon_offset, position, live_count, features, conv_weight):
     count = grad_rows.shape[0]
-    lat_index = lax.axis_index("lat")
-    edge = jnp.stack(
-        [
-            jnp.where(lat_index == 0, 4, 0),
-            jnp.where(lat_index == lax.axis_size("lat") - 1, 68, 72),
-        ]
-    ).astype(jnp.int32)
     outgoing = pack(
         live_count,
         owner.reshape(1, count),
@@ -632,9 +637,9 @@
     eye, shift, pick = picks()
     last, head = features[:, 120:128], features[:, 0:8]
     left, right = both_ways(last, head, "lon", True)
-    feat = prep(eye, shift, features)
+    feat = prep(shift, features)
     feat_side = prep_side(eye, pick, left, right, head, last)
-    canvas, side, rim, up, down = scatter(edge, incoming)
+    canvas, side, rim, up, down = scatter(incoming)
     grid_above, grid_below = both_ways(down, up, "lat", False)
     acc = own_grad(canvas, side, feat, feat_side)
     part = halo_grad(acc, grid_above, grid_below, feat, feat_side)

time: 119 us -> 108 us (0.908)
  Pallas kernels: 53.5 us -> 38.5 us
  waiting for transfers between devices: 15.1 us -> 19.5 us
  local copies, waits for them, and re-layouts: 6.31 us -> 9.47 us
  starting transfers between devices: 41.6 us -> 38.8 us
    pallas_call x1, Pallas kernels: 8.25 us -> 1.92 us  [prep(): pl.pallas_call(prep_kernel, grid=(4,), out_shape=jax.ShapeDtypeStruct((64...]
    ppermute x3, waiting for transfers between devices: 6.33 us -> 10.6 us  [both_ways(): lax.ppermute(back, axis, [((i + 1) % count, i) for i in range(ends)])]
    unnamed x24 -> x32, local copies, waits for them, and re-layouts: 5.31 us -> 9.43 us
    all_to_all x1, starting transfers between devices: 12 us -> 8.13 us  [shards(): got = lax.all_to_all(part.reshape(TILES, 16, 128), AXES, 0, 0, tiled=True)]
    pallas_call x1, Pallas kernels: 4.1 us -> 1.54 us  [halo_grad(): pl.pallas_call(halo_grad_kernel, out_shape=jax.ShapeDtypeStruct((2048, 12...]
    pallas_call x1, Pallas kernels: 7.41 us -> 5.13 us  [own_grad(): pl.pallas_call(own_grad_kernel, out_shape=jax.ShapeDtypeStruct((384, 384)...]
    pallas_call x1, Pallas kernels: 2.72 us -> 0.61 us  [prep_side(): pl.pallas_call(prep_side_kernel, out_shape=jax.ShapeDtypeStruct((384, 102...]
    pallas_call x1, Pallas kernels: 9.14 us -> 7.09 us  [conv(): pl.pallas_call(conv_kernel, grid=(8,), out_shape=jax.ShapeDtypeStruct((64...]
  transfers between devices with their start and end apart: 9 -> 9, of which waited for: 5 -> 6; matrix products, arithmetic and copies ran while one was open for 1% -> 0% of each run, Pallas kernels for 23% -> 14%
where the time goes in v6:
time: 108 us
  starting transfers between devices  38.8 us (36%)
  Pallas kernels  38.5 us (36%)
  waiting for transfers between devices  19.5 us (18%)
  local copies, waits for them, and re-layouts  9.47 us (9%)
  between operations  1.65 us (2%)
    pallas_call x1, Pallas kernels, scatter(): pl.pallas_call(scatter_kernel, out_shape=(jax.ShapeDtypeStruct((72, 136,...  16.2 us
    all_to_all x1, starting transfers between devices, shards(): incoming = lax.all_to_all(outgoing, AXES, 0, 0, tiled=True)  11.9 us
    ppermute x3, waiting for transfers between devices, both_ways(): lax.ppermute(back, axis, [((i + 1) % count, i) for i in range(ends)])  10.6 us
    unnamed x32, local copies, waits for them, and re-layouts  9.43 us
    ppermute x3, starting transfers between devices, both_ways(): lax.ppermute(forth, axis, [(i, (i + 1) % count) for i in range(ends)])  9.32 us
    all_to_all x1, starting transfers between devices, shards(): got = lax.all_to_all(part.reshape(TILES, 16, 128), AXES, 0, 0, tiled=True)  8.13 us
    pallas_call x1, Pallas kernels, conv(): pl.pallas_call(conv_kernel, grid=(8,), out_shape=jax.ShapeDtypeStruct((64...  7.09 us
    all_to_all x1, starting transfers between devices, shards(): every = lax.all_to_all(share(got), AXES, 0, 0, tiled=True)  7.01 us
  transfers between devices with their start and end apart: 9, of which 6 were waited for; matrix products, arithmetic and copies ran while one was open for 0% of the time, Pallas kernels for 14%

profile of v6, /device:TPU:1, one launch (start us, length us, event | category | flops | bytes accessed | tf_op | source)
XLA Modules:
  0.0 107.9 jit_solution(4744436573942872375)
XLA Ops:
  1.4 3.5 %pack.1 = bf16[128,24,128]{2,1,0:T(8,128)(2,1)} custom-call(s32[1]{0:T(128)S(6)} %copy.13.live_ref, s32[1,1024]{1,0:T(1,128)} %bitcast.8, s32[1,1024]{1,0:T(1,128)} %bitcast.9, s32[1,1024]{1,0:T(1,128)} %bitcast.10, bf16[2,1024]{1,0:T(2,128)(2,1)} %bitcast.11, bf16[1024,128]{1,0:T(8,128)(2,1)} %rows_ref.1), custom_call_target="tpu_custom_call" | custom-call | flops 700000000 | bytes 1500000 | tf_op jit(solution)/shard_map/pack/pallas_call | solution.py:81
  5.0 11.9 %all-to-all-start = ((bf16[128,24,128]{2,1,0:T(8,128)(2,1)}), bf16[128,24,128]{2,1,0:T(8,128)(2,1)}, u32[]{:S(2)}, u32[]{:S(2)}) async-start(bf16[128,24,128]{2,1,0:T(8,128)(2,1)} %pack.1), calls=%async_computation | async-start | bytes 1572864 | tf_op jit(solution)/shard_map/all_to_all | solution.py:636
  16.9 1.2 %collective-permute-start.3 = (bf16[64,8,128]{2,1,0:T(8,128)(2,1)S(1)}, bf16[64,8,128]{2,1,0:T(8,128)(2,1)S(1)}, u32[]{:S(2)}, u32[]{:S(2)}) collective-permute-start(bf16[64,8,128]{2,1,0:T(8,128)(2,1)S(1)} %get-tuple-element.22.head_ref), channel_id=1, source_target_pairs={{1,0},{2,1},{3,2},{4,3},{5,4},{6,5},{7,6},{8,7},{9,8},{10,9},{11,1... | collective-permute-start | bytes 393224 | tf_op jit(solution)/shard_map/ppermute | solution.py:622
  18.1 2.1 %collective-permute-start.2 = (bf16[64,8,128]{2,1,0:T(8,128)(2,1)S(1)}, bf16[64,8,128]{2,1,0:T(8,128)(2,1)S(1)}, u32[]{:S(2)}, u32[]{:S(2)}) collective-permute-start(bf16[64,8,128]{2,1,0:T(8,128)(2,1)S(1)} %get-tuple-element.23.last_ref), channel_id=1, source_target_pairs={{0,1},{1,2},{2,3},{3,4},{4,5},{5,6},{6,7},{7,8},{8,9},{9,10},{10,1... | collective-permute-start | bytes 393224 | tf_op jit(solution)/shard_map/ppermute | solution.py:621
  20.2 1.9 %prep.1.feat_hbm = bf16[64,3,128,128]{3,2,1,0:T(8,128)(2,1)S(1)} custom-call(bf16[128,256]{1,0:T(8,128)(2,1)S(1)} %copy-done.9, bf16[64,128,128]{2,1,0:T(8,128)(2,1)S(1)} %copy-done.2), custom_call_target="tpu_custom_call" | custom-call | flops 2200000000 | bytes 8000000 | tf_op jit(solution)/shard_map/prep/pallas_call | solution.py:124
  22.2 2.6 %copy-done = bf16[64,3,128,128]{3,2,1,0:T(8,128)(2,1)} copy-done((bf16[64,3,128,128]{3,2,1,0:T(8,128)(2,1)}, bf16[64,3,128,128]{3,2,1,0:T(8,128)(2,1)S(1)}, u32[]{:S(2)}) %copy-start) | copy-done | bytes 6291480
  24.8 6.5 %collective-permute-done.3.right_ref = bf16[64,8,128]{2,1,0:T(8,128)(2,1)S(1)} collective-permute-done((bf16[64,8,128]{2,1,0:T(8,128)(2,1)S(1)}, bf16[64,8,128]{2,1,0:T(8,128)(2,1)S(1)}, u32[]{:S(2)}, u32[]{:S(2)}) %collective-permute-start.3) | collective-permute-done | bytes 131104 | tf_op jit(solution)/shard_map/ppermute | solution.py:622
  31.3 0.6 prep_side.1.feat_side_hbm.feat_side_ref
  31.9 1.5 %all-to-all-done.in_ref = bf16[128,24,128]{2,1,0:T(8,128)(2,1)} async-done(((bf16[128,24,128]{2,1,0:T(8,128)(2,1)}), bf16[128,24,128]{2,1,0:T(8,128)(2,1)}, u32[]{:S(2)}, u32[]{:S(2)}) %all-to-all-start) | async-done | bytes 786464 | tf_op jit(solution)/shard_map/all_to_all | solution.py:636
  33.4 16.2 %scatter.1 = (bf16[72,136,128]{2,1,0:T(8,128)(2,1)S(1)}, bf16[72,16,128]{2,1,0:T(8,128)(2,1)S(1)}, bf16[72,24,128]{2,1,0:T(8,128)(2,1)S(1)}, bf16[4,136,128]{2,1,0:T(8,128)(2,1)S(1)}, bf16[5,136,128]{2,1,0:T(8,128)(2,1)S(1)}) custom-call(bf16[128,24,128]{2,1,0:T(8,128)(2,1)} %all-to-all-done.in_ref), custom_call_target="tpu_custom_call" | custom-call | flops 5200000000 | bytes 4000000 | tf_op jit(solution)/shard_map/scatter/pallas_call | solution.py:285
  49.6 1.3 %collective-permute-start.1 = (bf16[4,136,128]{2,1,0:T(8,128)(2,1)S(1)}, bf16[4,136,128]{2,1,0:T(8,128)(2,1)S(1)}, u32[]{:S(2)}, u32[]{:S(2)}) collective-permute-start(bf16[4,136,128]{2,1,0:T(8,128)(2,1)S(1)} %get-tuple-element.14), channel_id=1, source_target_pairs={{16,0},{32,16},{48,32},{64,48},{80,64},{96,80},{112,96},{17,1},{33... | collective-permute-start | bytes 417800 | tf_op jit(solution)/shard_map/ppermute | solution.py:622
  50.9 4.0 %collective-permute-start = (bf16[5,136,128]{2,1,0:T(8,128)(2,1)S(1)}, bf16[5,136,128]{2,1,0:T(8,128)(2,1)S(1)}, u32[]{:S(2)}, u32[]{:S(2)}) collective-permute-start(bf16[5,136,128]{2,1,0:T(8,128)(2,1)S(1)} %get-tuple-element.13), channel_id=1, source_target_pairs={{0,16},{16,32},{32,48},{48,64},{64,80},{80,96},{96,112},{1,17},{17... | collective-permute-start | bytes 522248 | tf_op jit(solution)/shard_map/ppermute | solution.py:621
  54.9 5.1 %own_grad.1.acc_ref = f32[384,384]{1,0:T(8,128)S(1)} custom-call(bf16[72,136,128]{2,1,0:T(8,128)(2,1)S(1)} %get-tuple-element.12.canvas_hbm.canvas_ref, bf16[72,16,128]{2,1,0:T(8,128)(2,1)S(1)} %get-tuple-element.15.side_hbm, bf16[64,3,128,128]{3,2,1,0:T(8,128)(2,1)S(1)} %copy-done.1, bf16[384,1024]{1,0:T(8,128)(2,1)S(1)} %prep_side.1.feat_side_hbm.feat_side_ref), custom_call_target="tpu_custom_call" | custom-call | flops 2800000000 | bytes 10000000 | tf_op jit(solution)/shard_map/own_grad/pallas_call | solution.py:372
  60.1 1.5 %halo_grad.1 = bf16[2048,128]{1,0:T(8,128)(2,1)S(1)} custom-call(f32[384,384]{1,0:T(8,128)S(1)} %own_grad.1.acc_ref, bf16[5,136,128]{2,1,0:T(8,128)(2,1)S(1)} %collective-permute-done.above_ref, bf16[4,136,128]{2,1,0:T(8,128)(2,1)S(1)} %collective-permute-done.1.below_ref, bf16[64,3,128,128]{3,2,1,0:T(8,128)(2,1)S(1)} %copy-done.1, ...), custom_call_target="tpu_custom_call" | custom-call | flops 420000000 | bytes 3500000 | tf_op jit(solution)/shard_map/halo_grad/pallas_call | solution.py:456
  61.6 0.8 copy-done.3
  62.4 8.1 %all-to-all-start.1 = ((bf16[128,16,128]{2,1,0:T(8,128)(2,1)}), bf16[128,16,128]{2,1,0:T(8,128)(2,1)S(1)}, u32[]{:S(2)}, u32[]{:S(2)}) async-start(bf16[128,16,128]{2,1,0:T(8,128)(2,1)} %bitcast.6), calls=%async_computation.1 | async-start | bytes 1048576 | tf_op jit(solution)/shard_map/all_to_all | solution.py:646
  70.6 0.9 copy-done.5
  71.5 1.0 copy-done.7
  72.6 3.2 %collective-permute-start.4 = (bf16[66,8,128]{2,1,0:T(8,128)(2,1)S(1)}, bf16[66,8,128]{2,1,0:T(8,128)(2,1)S(1)}, u32[]{:S(2)}, u32[]{:S(2)}) collective-permute-start(bf16[66,8,128]{2,1,0:T(8,128)(2,1)S(1)} %get-tuple-element.17), channel_id=1, source_target_pairs={{0,1},{1,2},{2,3},{3,4},{4,5},{5,6},{6,7},{7,8},{8,9},{9,10},{10,1... | collective-permute-start | bytes 405512 | tf_op jit(solution)/shard_map/ppermute | solution.py:621
  75.8 2.0 %collective-permute-done.4.left_ref = bf16[66,8,128]{2,1,0:T(8,128)(2,1)S(1)} collective-permute-done((bf16[66,8,128]{2,1,0:T(8,128)(2,1)S(1)}, bf16[66,8,128]{2,1,0:T(8,128)(2,1)S(1)}, u32[]{:S(2)}, u32[]{:S(2)}) %collective-permute-start.4) | collective-permute-done | bytes 135200 | tf_op jit(solution)/shard_map/ppermute | solution.py:621
  77.8 0.7 copy-done.12
  78.5 4.1 %collective-permute-done.5.right_ref = bf16[66,8,128]{2,1,0:T(8,128)(2,1)S(1)} collective-permute-done((bf16[66,8,128]{2,1,0:T(8,128)(2,1)S(1)}, bf16[66,8,128]{2,1,0:T(8,128)(2,1)S(1)}, u32[]{:S(2)}, u32[]{:S(2)}) %collective-permute-start.5) | collective-permute-done | bytes 135200 | tf_op jit(solution)/shard_map/ppermute | solution.py:622
  82.6 0.6 copy-done.14
  83.2 1.5 %all-to-all-done.1.in_ref = bf16[128,16,128]{2,1,0:T(8,128)(2,1)S(1)} async-done(((bf16[128,16,128]{2,1,0:T(8,128)(2,1)}), bf16[128,16,128]{2,1,0:T(8,128)(2,1)S(1)}, u32[]{:S(2)}, u32[]{:S(2)}) %all-to-all-start.1) | async-done | bytes 524320 | tf_op jit(solution)/shard_map/all_to_all | solution.py:646
  84.7 1.0 share.1
  85.6 7.0 %all-to-all-start.2 = ((bf16[128,16,128]{2,1,0:T(8,128)(2,1)}), bf16[128,16,128]{2,1,0:T(8,128)(2,1)S(1)}, u32[]{:S(2)}, u32[]{:S(2)}) async-start(bf16[128,16,128]{2,1,0:T(8,128)(2,1)} %share.1), calls=%async_computation.2 | async-start | bytes 1048576 | tf_op jit(solution)/shard_map/all_to_all | solution.py:650
  92.7 1.0 copy-done.11
  93.6 0.9 copy-done.13
  94.5 0.9 copy-done.15
  95.4 7.1 %conv.1 = bf16[64,128,128]{2,1,0:T(8,128)(2,1)} custom-call(bf16[72,136,128]{2,1,0:T(8,128)(2,1)S(1)} %get-tuple-element.12.canvas_hbm.canvas_ref, bf16[5,136,128]{2,1,0:T(8,128)(2,1)S(1)} %collective-permute-done.above_ref, bf16[4,136,128]{2,1,0:T(8,128)(2,1)S(1)} %copy-done.5, bf16[66,8,128]{2,1,0:T(8,128)(2,1)S(1)} %copy-done.13, ...), custom_call_target="tpu_custom_call" | custom-call | flops 2700000000 | bytes 4500000 | tf_op jit(solution)/shard_map/conv/pallas_call | solution.py:567
  102.5 4.0 %all-to-all-done.2.in_ref = bf16[128,16,128]{2,1,0:T(8,128)(2,1)S(1)} async-done(((bf16[128,16,128]{2,1,0:T(8,128)(2,1)}), bf16[128,16,128]{2,1,0:T(8,128)(2,1)S(1)}, u32[]{:S(2)}, u32[]{:S(2)}) %all-to-all-start.2) | async-done | bytes 524320 | tf_op jit(solution)/shard_map/all_to_all | solution.py:650
  106.5 1.4 %finish.1 = f32[1152,128]{1,0:T(8,128)} custom-call(bf16[128,16,128]{2,1,0:T(8,128)(2,1)S(1)} %all-to-all-done.2.in_ref), custom_call_target="tpu_custom_call" | custom-call | bytes 900000 | tf_op jit(solution)/shard_map/finish/pallas_call | solution.py:605
  (29 shorter events, 0.2 us)
Async XLA Ops:
  0.6 16.2 %copy-start.2 = (bf16[64,128,128]{2,1,0:T(8,128)(2,1)S(1)}, bf16[64,128,128]{2,1,0:T(8,128)(2,1)}, u32[]{:S(2)}) copy-start(bf16[64,128,128]{2,1,0:T(8,128)(2,1)} %feat_ref.1) | copy-start | bytes 6291460
  1.4 18.8 %copy-start.9 = (bf16[128,256]{1,0:T(8,128)(2,1)S(1)}, bf16[128,256]{1,0:T(8,128)(2,1)}, u32[]{:S(2)}) copy-start(bf16[128,256]{1,0:T(8,128)(2,1)} %constant.7.clone.shift_ref) | copy-start | bytes 196612
  5.0 28.4 %all-to-all-start = ((bf16[128,24,128]{2,1,0:T(8,128)(2,1)}), bf16[128,24,128]{2,1,0:T(8,128)(2,1)}, u32[]{:S(2)}, u32[]{:S(2)}) async-start(bf16[128,24,128]{2,1,0:T(8,128)(2,1)} %pack.1), calls=%async_computation | async-start | bytes 1572864 | tf_op jit(solution)/shard_map/all_to_all | solution.py:636
  16.9 14.4 %collective-permute-start.3 = (bf16[64,8,128]{2,1,0:T(8,128)(2,1)S(1)}, bf16[64,8,128]{2,1,0:T(8,128)(2,1)S(1)}, u32[]{:S(2)}, u32[]{:S(2)}) collective-permute-start(bf16[64,8,128]{2,1,0:T(8,128)(2,1)S(1)} %get-tuple-element.22.head_ref), channel_id=1, source_target_pairs={{1,0},{2,1},{3,2},{4,3},{5,4},{6,5},{7,6},{8,7},{9,8},{10,9},{11,1... | collective-permute-start | bytes 393224 | tf_op jit(solution)/shard_map/ppermute | solution.py:622
  18.1 13.2 %copy-start.8 = (bf16[256,384]{1,0:T(8,128)(2,1)S(1)}, bf16[256,384]{1,0:T(8,128)(2,1)}, u32[]{:S(2)}) copy-start(bf16[256,384]{1,0:T(8,128)(2,1)} %constant.8.clone.pick_ref) | copy-start | bytes 589828
  18.1 13.2 %copy-start.10 = (bf16[128,128]{1,0:T(8,128)(2,1)S(1)}, bf16[128,128]{1,0:T(8,128)(2,1)}, u32[]{:S(2)}) copy-start(bf16[128,128]{1,0:T(8,128)(2,1)} %constant.6.clone.eye_ref) | copy-start | bytes 98308
  18.1 13.2 %collective-permute-start.2 = (bf16[64,8,128]{2,1,0:T(8,128)(2,1)S(1)}, bf16[64,8,128]{2,1,0:T(8,128)(2,1)S(1)}, u32[]{:S(2)}, u32[]{:S(2)}) collective-permute-start(bf16[64,8,128]{2,1,0:T(8,128)(2,1)S(1)} %get-tuple-element.23.last_ref), channel_id=1, source_target_pairs={{0,1},{1,2},{2,3},{3,4},{4,5},{5,6},{6,7},{7,8},{8,9},{9,10},{10,1... | collective-permute-start | bytes 393224 | tf_op jit(solution)/shard_map/ppermute | solution.py:621
  22.2 2.6 %copy-start = (bf16[64,3,128,128]{3,2,1,0:T(8,128)(2,1)}, bf16[64,3,128,128]{3,2,1,0:T(8,128)(2,1)S(1)}, u32[]{:S(2)}) copy-start(bf16[64,3,128,128]{3,2,1,0:T(8,128)(2,1)S(1)} %prep.1.feat_hbm) | copy-start | bytes 18874372
  33.4 21.5 %copy-start.1 = (bf16[64,3,128,128]{3,2,1,0:T(8,128)(2,1)S(1)}, bf16[64,3,128,128]{3,2,1,0:T(8,128)(2,1)}, u32[]{:S(2)}) copy-start(bf16[64,3,128,128]{3,2,1,0:T(8,128)(2,1)} %copy-done) | copy-start | bytes 18874372
  49.6 10.5 %copy-start.6 = (bf16[72,24,128]{2,1,0:T(8,128)(2,1)}, bf16[72,24,128]{2,1,0:T(8,128)(2,1)S(1)}, u32[]{:S(2)}) copy-start(bf16[72,24,128]{2,1,0:T(8,128)(2,1)S(1)} %get-tuple-element.16.rim_ref) | copy-start | bytes 1327108
  49.6 10.5 %collective-permute-start.1 = (bf16[4,136,128]{2,1,0:T(8,128)(2,1)S(1)}, bf16[4,136,128]{2,1,0:T(8,128)(2,1)S(1)}, u32[]{:S(2)}, u32[]{:S(2)}) collective-permute-start(bf16[4,136,128]{2,1,0:T(8,128)(2,1)S(1)} %get-tuple-element.14), channel_id=1, source_target_pairs={{16,0},{32,16},{48,32},{64,48},{80,64},{96,80},{112,96},{17,1},{33... | collective-permute-start | bytes 417800 | tf_op jit(solution)/shard_map/ppermute | solution.py:622
  50.9 9.2 %collective-permute-start = (bf16[5,136,128]{2,1,0:T(8,128)(2,1)S(1)}, bf16[5,136,128]{2,1,0:T(8,128)(2,1)S(1)}, u32[]{:S(2)}, u32[]{:S(2)}) collective-permute-start(bf16[5,136,128]{2,1,0:T(8,128)(2,1)S(1)} %get-tuple-element.13), channel_id=1, source_target_pairs={{0,16},{16,32},{32,48},{48,64},{64,80},{80,96},{96,112},{1,17},{17... | collective-permute-start | bytes 522248 | tf_op jit(solution)/shard_map/ppermute | solution.py:621
  60.1 1.6 %copy-start.4 = (bf16[4,136,128]{2,1,0:T(8,128)(2,1)}, bf16[4,136,128]{2,1,0:T(8,128)(2,1)S(1)}, u32[]{:S(2)}) copy-start(bf16[4,136,128]{2,1,0:T(8,128)(2,1)S(1)} %collective-permute-done.1.below_ref) | copy-start | bytes 417796
  61.6 0.8 copy-start.3
  62.4 22.3 %all-to-all-start.1 = ((bf16[128,16,128]{2,1,0:T(8,128)(2,1)}), bf16[128,16,128]{2,1,0:T(8,128)(2,1)S(1)}, u32[]{:S(2)}, u32[]{:S(2)}) async-start(bf16[128,16,128]{2,1,0:T(8,128)(2,1)} %bitcast.6), calls=%async_computation.1 | async-start | bytes 1048576 | tf_op jit(solution)/shard_map/all_to_all | solution.py:646
  70.6 0.9 copy-start.5
  71.5 1.0 copy-start.7
  72.6 5.2 %collective-permute-start.4 = (bf16[66,8,128]{2,1,0:T(8,128)(2,1)S(1)}, bf16[66,8,128]{2,1,0:T(8,128)(2,1)S(1)}, u32[]{:S(2)}, u32[]{:S(2)}) collective-permute-start(bf16[66,8,128]{2,1,0:T(8,128)(2,1)S(1)} %get-tuple-element.17), channel_id=1, source_target_pairs={{0,1},{1,2},{2,3},{3,4},{4,5},{5,6},{6,7},{7,8},{8,9},{9,10},{10,1... | collective-permute-start | bytes 405512 | tf_op jit(solution)/shard_map/ppermute | solution.py:621
  75.8 6.7 %collective-permute-start.5 = (bf16[66,8,128]{2,1,0:T(8,128)(2,1)S(1)}, bf16[66,8,128]{2,1,0:T(8,128)(2,1)S(1)}, u32[]{:S(2)}, u32[]{:S(2)}) collective-permute-start(bf16[66,8,128]{2,1,0:T(8,128)(2,1)S(1)} %get-tuple-element.18), channel_id=1, source_target_pairs={{1,0},{2,1},{3,2},{4,3},{5,4},{6,5},{7,6},{8,7},{9,8},{10,9},{11,1... | collective-permute-start | bytes 405512 | tf_op jit(solution)/shard_map/ppermute | solution.py:622
  77.8 0.7 copy-start.12
  82.5 0.7 copy-start.14
  85.6 20.9 %all-to-all-start.2 = ((bf16[128,16,128]{2,1,0:T(8,128)(2,1)}), bf16[128,16,128]{2,1,0:T(8,128)(2,1)S(1)}, u32[]{:S(2)}, u32[]{:S(2)}) async-start(bf16[128,16,128]{2,1,0:T(8,128)(2,1)} %share.1), calls=%async_computation.2 | async-start | bytes 1048576 | tf_op jit(solution)/shard_map/all_to_all | solution.py:650
  92.7 1.0 copy-start.11
  93.6 0.9 copy-start.13
  94.5 0.9 copy-start.15

commit v7 on v6

--- a/solution.py
+++ b/solution.py
@@ -12,7 +12,8 @@
 BF16 = jnp.bfloat16
 F32 = jnp.float32
 SLOTS = 16
-CHUNK = 24
+CHUNK = 18
+SHARE = 10
 TILES = 128
 GAUSS = 2.0 * 1.5 * 1.5
 
@@ -50,16 +51,6 @@
         )
         before = before + mm(part, ones)
     rank = jnp.concatenate(ranks, axis=1).astype(jnp.int32)
-    slot = own * SLOTS + rank
-    rows = rows_ref[...]
-    step = 1024
-    for q in range(TILES * SLOTS // step):
-        line = lax.broadcasted_iota(jnp.int32, (step, count), 0) + q * step
-        picked = jnp.where(slot == line, 1.0, 0.0).astype(BF16)
-        moved = mm(picked, rows).astype(BF16)
-        out_ref[q * step // SLOTS : (q + 1) * step // SLOTS, 0:SLOTS, :] = moved.reshape(
-            step // SLOTS, SLOTS, 128
-        )
     at_rank = lax.broadcasted_iota(jnp.int32, (SLOTS, count), 0) == rank
     pos = pos_ref[...].astype(F32)
     fields = (
@@ -71,16 +62,25 @@
     spots = [jnp.where(at_rank, f, 0.0) for f in fields]
     spots.append(jnp.zeros((128 - SLOTS * len(fields), count), F32))
     cells = nt(named_b, jnp.concatenate(spots, axis=0).astype(BF16)).astype(BF16)
-    out_ref[:, SLOTS:CHUNK, :] = jnp.broadcast_to(
-        cells.astype(F32)[:, None, :], (TILES, CHUNK - SLOTS, 128)
-    ).astype(BF16)
+    slot = own * CHUNK + rank
+    rows = rows_ref[...]
+    step = 64 * CHUNK
+    for q in range(TILES // 64):
+        line = lax.broadcasted_iota(jnp.int32, (step, count), 0) + q * step
+        picked = jnp.where(slot == line, 1.0, 0.0).astype(BF16)
+        line = lax.broadcasted_iota(jnp.int32, (step, TILES), 0) + q * step
+        tile = lax.broadcasted_iota(jnp.int32, (step, TILES), 1)
+        cell_row = jnp.where(line == tile * CHUNK + SLOTS, 1.0, 0.0).astype(BF16)
+        out_ref[q * step : (q + 1) * step, :] = (mm(picked, rows) + mm(cell_row, cells)).astype(
+            BF16
+        )
 
 
 def pack(live, own, lat, lon, pos, rows):
     vmem = pl.BlockSpec(memory_space=pltpu.VMEM)
     return pl.pallas_call(
         pack_kernel,
-        out_shape=jax.ShapeDtypeStruct((TILES, CHUNK, 128), BF16),
+        out_shape=jax.ShapeDtypeStruct((TILES * CHUNK, 128), BF16),
         in_specs=[pl.BlockSpec(memory_space=pltpu.SMEM)] + [vmem] * 5,
         out_specs=vmem,
         cost_estimate=pl.CostEstimate(flops=700_000_000, bytes_accessed=1_500_000, transcendentals=0),
@@ -190,23 +190,25 @@
         )
 
     total = TILES * SLOTS
-    rows_ref[...] = in_ref[:, 0:SLOTS, :].reshape(total, 128)
-    tail = in_ref[:, SLOTS:CHUNK, :].reshape(TILES * (CHUNK - SLOTS), 128)
+    for source in range(TILES):
+        rows_ref[source * SLOTS : (source + 1) * SLOTS, :] = in_ref[
+            source * CHUNK : source * CHUNK + SLOTS, :
+        ]
     first = jnp.where(
-        lax.broadcasted_iota(jnp.int32, (TILES, tail.shape[0]), 1)
-        == (CHUNK - SLOTS) * lax.broadcasted_iota(jnp.int32, (TILES, tail.shape[0]), 0),
+        lax.broadcasted_iota(jnp.int32, (TILES, TILES * CHUNK), 1)
+        == CHUNK * lax.broadcasted_iota(jnp.int32, (TILES, TILES * CHUNK), 0) + SLOTS,
         1.0,
         0.0,
     ).astype(BF16)
-    cells = mm(first, tail)
+    cells = mm(first, in_ref[...])
     cells_t = cells.T.astype(BF16)[: 4 * SLOTS]
     slot_lane = lax.broadcasted_iota(jnp.int32, (TILES, total), 1)
     spread = jnp.where(
-        (slot_lane // SLOTS) == lax.broadcasted_iota(jnp.int32, (TILES, total), 0), 1.0, 0.0
+        lax.shift_right_logical(slot_lane, 4) == lax.broadcasted_iota(jnp.int32, (TILES, total), 0), 1.0, 0.0
     ).astype(BF16)
     wide = mm(cells_t, spread)
     own_slot = (
-        lax.broadcasted_iota(jnp.int32, (SLOTS, total), 1) % SLOTS
+        (lax.broadcasted_iota(jnp.int32, (SLOTS, total), 1) & (SLOTS - 1))
         == lax.broadcasted_iota(jnp.int32, (SLOTS, total), 0)
     )
     cell_lat, cell_lon, frac_lat, frac_lon = [
@@ -396,7 +398,7 @@
     bottom = pltpu.make_async_copy(feat_hbm.at[60:64], feat.at[5:9], sem.at[1])
     top.start()
     bottom.start()
-    sums[1152:, :] = jnp.zeros((2048 - 1152, 128), BF16)
+    sums[1152:, :] = jnp.zeros((TILES * SHARE - 1152, 128), BF16)
 
     def beside(ref, count):
         eight = ref[:, 128:136, :].astype(F32)
@@ -455,12 +457,12 @@
     hbm = pl.BlockSpec(memory_space=pltpu.HBM)
     return pl.pallas_call(
         halo_grad_kernel,
-        out_shape=jax.ShapeDtypeStruct((2048, 128), BF16),
+        out_shape=jax.ShapeDtypeStruct((TILES * SHARE, 128), BF16),
         in_specs=[vmem, vmem, vmem, hbm, vmem],
         out_specs=hbm,
         scratch_shapes=[
             pltpu.VMEM((9, 3, 128, 128), BF16),
-            pltpu.VMEM((2048, 128), BF16),
+            pltpu.VMEM((TILES * SHARE, 128), BF16),
             pltpu.SemaphoreType.DMA((3,)),
         ],
         cost_estimate=pl.CostEstimate(
@@ -579,39 +581,54 @@
     )(*args)
 
 
-def gather_kernel(in_ref, out_ref):
-    mine = jnp.sum(in_ref[...].astype(F32), axis=0)
-    out_ref[...] = jnp.broadcast_to(mine.astype(BF16)[None], out_ref.shape)
+def share_rows():
+    which = np.arange(TILES * SHARE)[:, None] % SHARE == np.arange(16)[None, :]
+    return jnp.asarray(which.astype(np.float32), BF16)
+
+
+def share_kernel(spread_ref, in_ref, out_ref):
+    shape = (16, TILES * SHARE)
+    row = lax.broadcasted_iota(jnp.int32, shape, 1)
+    pick = jnp.where(
+        lax.rem(row, SHARE) == lax.broadcasted_iota(jnp.int32, shape, 0), 1.0, 0.0
+    ).astype(BF16)
+    mine = mm(pick, in_ref[...]).astype(BF16)
+    out_ref[...] = mm(spread_ref[...], mine).astype(BF16)
 
 
 def share(got):
     vmem = pl.BlockSpec(memory_space=pltpu.VMEM)
     return pl.pallas_call(
-        gather_kernel,
+        share_kernel,
         out_shape=jax.ShapeDtypeStruct(got.shape, BF16),
+        in_specs=[vmem] * 2,
+        out_specs=vmem,
+        compiler_params=pltpu.CompilerParams(vmem_limit_bytes=3 << 20),
+        cost_estimate=pl.CostEstimate(flops=10_000_000, bytes_accessed=1_000_000, transcendentals=0),
+        name="share",
+    )(share_rows(), got)
+
+
+def finish_kernel(in_ref, out_ref):
+    out_ref[...] = in_ref[0:1152, :].astype(F32)
+
+
+def finish(every):
+    vmem = pl.BlockSpec(memory_space=pltpu.VMEM)
+    return pl.pallas_call(
+        finish_kernel,
+        out_shape=jax.ShapeDtypeStruct((1152, 128), F32),
         in_specs=[vmem],
         out_specs=vmem,
-        cost_estimate=pl.CostEstimate(flops=300_000, bytes_accessed=1_000_000, transcendentals=0),
-        compiler_params=pltpu.CompilerParams(vmem_limit_bytes=3 << 20),
-        name="share",
-    )(got)
-
-
-def finish_kernel(in_ref, out_ref):
-    out_ref[...] = in_ref[...].reshape(384, 128).astype(F32)
-
-
-def finish(every):
-    return pl.pallas_call(
-        finish_kernel,
-        grid=(3,),
-        out_shape=jax.ShapeDtypeStruct((1152, 128), F32),
-        in_specs=[pl.BlockSpec((24, 16, 128), lambda i: (i, 0, 0))],
-        out_specs=pl.BlockSpec((384, 128), lambda i: (i, 0)),
         compiler_params=pltpu.CompilerParams(vmem_limit_bytes=2 << 20),
         cost_estimate=pl.CostEstimate(flops=0, bytes_accessed=900_000, transcendentals=0),
         name="finish",
     )(every)
+
+
+def exchange(rows):
+    pairs = rows.reshape(TILES, -1, 2, rows.shape[1])
+    return lax.all_to_all(pairs, AXES, 0, 0, tiled=True).reshape(rows.shape)
 
 
 def both_ways(forth, back, axis, closed):
@@ -633,7 +650,7 @@
         position.T,
         grad_rows,
     )
-    incoming = lax.all_to_all(outgoing, AXES, 0, 0, tiled=True)
+    incoming = exchange(outgoing)
     eye, shift, pick = picks()
     last, head = features[:, 120:128], features[:, 0:8]
     left, right = both_ways(last, head, "lon", True)
@@ -643,11 +660,11 @@
     grid_above, grid_below = both_ways(down, up, "lat", False)
     acc = own_grad(canvas, side, feat, feat_side)
     part = halo_grad(acc, grid_above, grid_below, feat, feat_side)
-    got = lax.all_to_all(part.reshape(TILES, 16, 128), AXES, 0, 0, tiled=True)
+    got = exchange(part)
     send_right, send_left = sides(rim, grid_above, grid_below)
     from_left, from_right = both_ways(send_right, send_left, "lon", True)
     got, from_left, from_right = lax.optimization_barrier((got, from_left, from_right))
-    every = lax.all_to_all(share(got), AXES, 0, 0, tiled=True)
+    every = exchange(share(got))
     input_grad = conv(canvas, grid_above, grid_below, from_left, from_right, conv_weight)
     weight_grad = finish(every)
     return input_grad, weight_grad.reshape(3, 3, 128, 128)

time: 108 us -> 102 us (0.944)
  waiting for transfers between devices: 19.5 us -> 14.4 us
  local copies, waits for them, and re-layouts: 9.47 us -> 7.79 us
    all_to_all x3, waiting for transfers between devices: 6.91 us -> 4.16 us  [exchange(): return lax.all_to_all(pairs, AXES, 0, 0, tiled=True).reshape(rows.shape)]
    ppermute x3, waiting for transfers between devices: 10.6 us -> 8.26 us  [both_ways(): lax.ppermute(back, axis, [((i + 1) % count, i) for i in range(ends)])]
    unnamed x32 -> x34, local copies, waits for them, and re-layouts: 9.43 us -> 7.75 us
    pallas_call x1, Pallas kernels: 16.2 us -> 15.1 us  [scatter(): pl.pallas_call(scatter_kernel, out_shape=(jax.ShapeDtypeStruct((72, 136,...]
  transfers between devices with their start and end apart: 9 -> 9, of which waited for: 6 -> 6; matrix products, arithmetic and copies ran while one was open for 0% -> 0% of each run, Pallas kernels for 14% -> 15%
where the time goes in v7:
time: 102 us
  starting transfers between devices  39.8 us (39%)
  Pallas kernels  38 us (37%)
  waiting for transfers between devices  14.4 us (14%)
  local copies, waits for them, and re-layouts  7.79 us (8%)
  between operations  1.69 us (2%)
    all_to_all x3, starting transfers between devices, exchange(): return lax.all_to_all(pairs, AXES, 0, 0, tiled=True).reshape(rows.shape)  28 us
    pallas_call x1, Pallas kernels, scatter(): pl.pallas_call(scatter_kernel, out_shape=(jax.ShapeDtypeStruct((72, 136,...  15.1 us
    ppermute x3, starting transfers between devices, both_ways(): lax.ppermute(forth, axis, [(i, (i + 1) % count) for i in range(ends)])  9.39 us
    ppermute x3, waiting for transfers between devices, both_ways(): lax.ppermute(back, axis, [((i + 1) % count, i) for i in range(ends)])  8.26 us
    unnamed x34, local copies, waits for them, and re-layouts  7.75 us
    pallas_call x1, Pallas kernels, conv(): pl.pallas_call(conv_kernel, grid=(8,), out_shape=jax.ShapeDtypeStruct((64...  7.1 us
    pallas_call x1, Pallas kernels, own_grad(): pl.pallas_call(own_grad_kernel, out_shape=jax.ShapeDtypeStruct((384, 384)...  5.13 us
    all_to_all x3, waiting for transfers between devices, exchange(): return lax.all_to_all(pairs, AXES, 0, 0, tiled=True).reshape(rows.shape)  4.16 us
  transfers between devices with their start and end apart: 9, of which 6 were waited for; matrix products, arithmetic and copies ran while one was open for 0% of the time, Pallas kernels for 15%

profile of v7, /device:TPU:1, one launch (start us, length us, event | category | flops | bytes accessed | tf_op | source)
XLA Modules:
  0.0 101.7 jit_solution(11475333780343729210)
XLA Ops:
  1.4 0.0 copy-start.8
  1.4 3.9 %pack.1 = bf16[2304,128]{1,0:T(8,128)(2,1)} custom-call(s32[1]{0:T(128)S(6)} %copy.14.live_ref, s32[1,1024]{1,0:T(1,128)} %bitcast.18, s32[1,1024]{1,0:T(1,128)} %bitcast.19, s32[1,1024]{1,0:T(1,128)} %bitcast.20, bf16[2,1024]{1,0:T(2,128)(2,1)} %bitcast.21, bf16[1024,128]{1,0:T(8,128)(2,1)} %rows_ref.1), custom_call_target="tpu_custom_call" | custom-call | flops 700000000 | bytes 1500000 | tf_op jit(solution)/shard_map/pack/pallas_call | solution.py:81
  5.4 11.5 %all-to-all-start = ((bf16[128,9,2,128]{3,2,1,0:T(2,128)(2,1)}), bf16[128,9,2,128]{3,2,1,0:T(2,128)(2,1)S(1)}, u32[]{:S(2)}, u32[]{:S(2)}) async-start(bf16[128,9,2,128]{3,2,1,0:T(2,128)(2,1)} %bitcast.16), calls=%async_computation | async-start | bytes 1179648 | tf_op jit(solution)/shard_map/all_to_all | solution.py:631
  16.9 1.1 %collective-permute-start.3 = (bf16[64,8,128]{2,1,0:T(8,128)(2,1)S(1)}, bf16[64,8,128]{2,1,0:T(8,128)(2,1)S(1)}, u32[]{:S(2)}, u32[]{:S(2)}) collective-permute-start(bf16[64,8,128]{2,1,0:T(8,128)(2,1)S(1)} %get-tuple-element.22.head_ref), channel_id=1, source_target_pairs={{1,0},{2,1},{3,2},{4,3},{5,4},{6,5},{7,6},{8,7},{9,8},{10,9},{11,1... | collective-permute-start | bytes 393224 | tf_op jit(solution)/shard_map/ppermute | solution.py:639
  18.1 2.2 %collective-permute-start.2 = (bf16[64,8,128]{2,1,0:T(8,128)(2,1)S(1)}, bf16[64,8,128]{2,1,0:T(8,128)(2,1)S(1)}, u32[]{:S(2)}, u32[]{:S(2)}) collective-permute-start(bf16[64,8,128]{2,1,0:T(8,128)(2,1)S(1)} %get-tuple-element.23.last_ref), channel_id=1, source_target_pairs={{0,1},{1,2},{2,3},{3,4},{4,5},{5,6},{6,7},{7,8},{8,9},{9,10},{10,1... | collective-permute-start | bytes 393224 | tf_op jit(solution)/shard_map/ppermute | solution.py:638
  20.3 1.9 %prep.1.feat_hbm = bf16[64,3,128,128]{3,2,1,0:T(8,128)(2,1)S(1)} custom-call(bf16[128,256]{1,0:T(8,128)(2,1)S(1)} %copy-done.8, bf16[64,128,128]{2,1,0:T(8,128)(2,1)S(1)} %copy-done.1), custom_call_target="tpu_custom_call" | custom-call | flops 2200000000 | bytes 8000000 | tf_op jit(solution)/shard_map/prep/pallas_call | solution.py:124
  22.2 2.6 %copy-done = bf16[64,3,128,128]{3,2,1,0:T(8,128)(2,1)} copy-done((bf16[64,3,128,128]{3,2,1,0:T(8,128)(2,1)}, bf16[64,3,128,128]{3,2,1,0:T(8,128)(2,1)S(1)}, u32[]{:S(2)}) %copy-start) | copy-done | bytes 6291480
  24.8 4.7 %collective-permute-done.3.right_ref = bf16[64,8,128]{2,1,0:T(8,128)(2,1)S(1)} collective-permute-done((bf16[64,8,128]{2,1,0:T(8,128)(2,1)S(1)}, bf16[64,8,128]{2,1,0:T(8,128)(2,1)S(1)}, u32[]{:S(2)}, u32[]{:S(2)}) %collective-permute-start.3) | collective-permute-done | bytes 131104 | tf_op jit(solution)/shard_map/ppermute | solution.py:639
  29.5 0.6 prep_side.1.feat_side_hbm.feat_side_ref
  30.1 1.3 %all-to-all-done = bf16[128,9,2,128]{3,2,1,0:T(2,128)(2,1)S(1)} async-done(((bf16[128,9,2,128]{3,2,1,0:T(2,128)(2,1)}), bf16[128,9,2,128]{3,2,1,0:T(2,128)(2,1)S(1)}, u32[]{:S(2)}, u32[]{:S(2)}) %all-to-all-start) | async-done | bytes 589856 | tf_op jit(solution)/shard_map/all_to_all | solution.py:631
  31.4 15.1 %scatter.1 = (bf16[72,136,128]{2,1,0:T(8,128)(2,1)S(1)}, bf16[72,16,128]{2,1,0:T(8,128)(2,1)S(1)}, bf16[72,24,128]{2,1,0:T(8,128)(2,1)S(1)}, bf16[4,136,128]{2,1,0:T(8,128)(2,1)S(1)}, bf16[5,136,128]{2,1,0:T(8,128)(2,1)S(1)}) custom-call(bf16[2304,128]{1,0:T(8,128)(2,1)S(1)} %bitcast.15), custom_call_target="tpu_custom_call" | custom-call | flops 5200000000 | bytes 4000000 | tf_op jit(solution)/shard_map/scatter/pallas_call | solution.py:287
  46.5 1.3 %collective-permute-start.1 = (bf16[4,136,128]{2,1,0:T(8,128)(2,1)S(1)}, bf16[4,136,128]{2,1,0:T(8,128)(2,1)S(1)}, u32[]{:S(2)}, u32[]{:S(2)}) collective-permute-start(bf16[4,136,128]{2,1,0:T(8,128)(2,1)S(1)} %get-tuple-element.14), channel_id=1, source_target_pairs={{16,0},{32,16},{48,32},{64,48},{80,64},{96,80},{112,96},{17,1},{33... | collective-permute-start | bytes 417800 | tf_op jit(solution)/shard_map/ppermute | solution.py:639
  47.8 4.0 %collective-permute-start = (bf16[5,136,128]{2,1,0:T(8,128)(2,1)S(1)}, bf16[5,136,128]{2,1,0:T(8,128)(2,1)S(1)}, u32[]{:S(2)}, u32[]{:S(2)}) collective-permute-start(bf16[5,136,128]{2,1,0:T(8,128)(2,1)S(1)} %get-tuple-element.13), channel_id=1, source_target_pairs={{0,16},{16,32},{32,48},{48,64},{64,80},{80,96},{96,112},{1,17},{17... | collective-permute-start | bytes 522248 | tf_op jit(solution)/shard_map/ppermute | solution.py:638
  51.8 5.1 %own_grad.1.acc_ref = f32[384,384]{1,0:T(8,128)S(1)} custom-call(bf16[72,136,128]{2,1,0:T(8,128)(2,1)S(1)} %get-tuple-element.12.canvas_hbm.canvas_ref, bf16[72,16,128]{2,1,0:T(8,128)(2,1)S(1)} %get-tuple-element.15.side_hbm, bf16[64,3,128,128]{3,2,1,0:T(8,128)(2,1)S(1)} %bitcast.12, bf16[384,1024]{1,0:T(8,128)(2,1)S(1)} %prep_side.1.feat_side_hbm.feat_side_ref), custom_call_target="tpu_custom_call" | custom-call | flops 2800000000 | bytes 10000000 | tf_op jit(solution)/shard_map/own_grad/pallas_call | solution.py:374
  57.0 2.2 %halo_grad.1 = bf16[1280,128]{1,0:T(8,128)(2,1)} custom-call(f32[384,384]{1,0:T(8,128)S(1)} %own_grad.1.acc_ref, bf16[5,136,128]{2,1,0:T(8,128)(2,1)S(1)} %collective-permute-done.above_ref, bf16[4,136,128]{2,1,0:T(8,128)(2,1)S(1)} %collective-permute-done.1.below_ref, bf16[64,3,128,128]{3,2,1,0:T(8,128)(2,1)S(1)} %bitcast.12, ...), custom_call_target="tpu_custom_call" | custom-call | flops 420000000 | bytes 3500000 | tf_op jit(solution)/shard_map/halo_grad/pallas_call | solution.py:458
  59.2 8.4 %all-to-all-start.1 = ((bf16[128,5,2,128]{3,2,1,0:T(2,128)(2,1)}), bf16[128,5,2,128]{3,2,1,0:T(2,128)(2,1)S(1)}, u32[]{:S(2)}, u32[]{:S(2)}) async-start(bf16[128,5,2,128]{3,2,1,0:T(2,128)(2,1)} %bitcast.6), calls=%async_computation.1 | async-start | bytes 655360 | tf_op jit(solution)/shard_map/all_to_all | solution.py:631
  67.7 1.0 copy-done.5
  68.7 0.1 sides.1
  68.8 3.2 %collective-permute-start.4 = (bf16[66,8,128]{2,1,0:T(8,128)(2,1)S(1)}, bf16[66,8,128]{2,1,0:T(8,128)(2,1)S(1)}, u32[]{:S(2)}, u32[]{:S(2)}) collective-permute-start(bf16[66,8,128]{2,1,0:T(8,128)(2,1)S(1)} %get-tuple-element.17), channel_id=1, source_target_pairs={{0,1},{1,2},{2,3},{3,4},{4,5},{5,6},{6,7},{7,8},{8,9},{9,10},{10,1... | collective-permute-start | bytes 405512 | tf_op jit(solution)/shard_map/ppermute | solution.py:638
  72.0 2.0 %collective-permute-done.4.left_ref = bf16[66,8,128]{2,1,0:T(8,128)(2,1)S(1)} collective-permute-done((bf16[66,8,128]{2,1,0:T(8,128)(2,1)S(1)}, bf16[66,8,128]{2,1,0:T(8,128)(2,1)S(1)}, u32[]{:S(2)}, u32[]{:S(2)}) %collective-permute-start.4) | collective-permute-done | bytes 135200 | tf_op jit(solution)/shard_map/ppermute | solution.py:638
  74.0 0.6 copy-done.11
  74.6 3.6 %collective-permute-done.5.right_ref = bf16[66,8,128]{2,1,0:T(8,128)(2,1)S(1)} collective-permute-done((bf16[66,8,128]{2,1,0:T(8,128)(2,1)S(1)}, bf16[66,8,128]{2,1,0:T(8,128)(2,1)S(1)}, u32[]{:S(2)}, u32[]{:S(2)}) %collective-permute-start.5) | collective-permute-done | bytes 135200 | tf_op jit(solution)/shard_map/ppermute | solution.py:639
  78.2 0.6 copy-done.13
  78.9 0.9 all-to-all-done.1
  79.8 1.1 %share.1 = bf16[1280,128]{1,0:T(8,128)(2,1)} custom-call(bf16[1280,16]{1,0:T(8,128)(2,1)S(1)} %copy-done.6, bf16[1280,128]{1,0:T(8,128)(2,1)S(1)} %bitcast.14), custom_call_target="tpu_custom_call" | custom-call | flops 10000000 | bytes 1000000 | tf_op jit(solution)/shard_map/share/pallas_call | solution.py:601
  80.9 8.1 %all-to-all-start.2 = ((bf16[128,5,2,128]{3,2,1,0:T(2,128)(2,1)}), bf16[128,5,2,128]{3,2,1,0:T(2,128)(2,1)S(1)}, u32[]{:S(2)}, u32[]{:S(2)}) async-start(bf16[128,5,2,128]{3,2,1,0:T(2,128)(2,1)} %bitcast.8), calls=%async_computation.2 | async-start | bytes 655360 | tf_op jit(solution)/shard_map/all_to_all | solution.py:631
  89.0 1.0 copy-done.10
  90.0 0.9 copy-done.12
  90.9 0.9 copy-done.14
  91.8 7.1 %conv.1 = bf16[64,128,128]{2,1,0:T(8,128)(2,1)} custom-call(bf16[72,136,128]{2,1,0:T(8,128)(2,1)S(1)} %copy-done.3, bf16[5,136,128]{2,1,0:T(8,128)(2,1)S(1)} %collective-permute-done.above_ref, bf16[4,136,128]{2,1,0:T(8,128)(2,1)S(1)} %collective-permute-done.1.below_ref, bf16[66,8,128]{2,1,0:T(8,128)(2,1)S(1)} %copy-done.12, ...), custom_call_target="tpu_custom_call" | custom-call | flops 2700000000 | bytes 4500000 | tf_op jit(solution)/shard_map/conv/pallas_call | solution.py:569
  98.9 2.0 %all-to-all-done.2 = bf16[128,5,2,128]{3,2,1,0:T(2,128)(2,1)S(1)} async-done(((bf16[128,5,2,128]{3,2,1,0:T(2,128)(2,1)}), bf16[128,5,2,128]{3,2,1,0:T(2,128)(2,1)S(1)}, u32[]{:S(2)}, u32[]{:S(2)}) %all-to-all-start.2) | async-done | bytes 327712 | tf_op jit(solution)/shard_map/all_to_all | solution.py:631
  100.9 0.9 finish.1
  (32 shorter events, 0.1 us)
Async XLA Ops:
  0.6 16.3 %copy-start.1 = (bf16[64,128,128]{2,1,0:T(8,128)(2,1)S(1)}, bf16[64,128,128]{2,1,0:T(8,128)(2,1)}, u32[]{:S(2)}) copy-start(bf16[64,128,128]{2,1,0:T(8,128)(2,1)} %feat_ref.1) | copy-start | bytes 6291460
  1.4 18.8 %copy-start.8 = (bf16[128,256]{1,0:T(8,128)(2,1)S(1)}, bf16[128,256]{1,0:T(8,128)(2,1)}, u32[]{:S(2)}) copy-start(bf16[128,256]{1,0:T(8,128)(2,1)} %constant.9.clone.shift_ref) | copy-start | bytes 196612
  5.4 26.0 %all-to-all-start = ((bf16[128,9,2,128]{3,2,1,0:T(2,128)(2,1)}), bf16[128,9,2,128]{3,2,1,0:T(2,128)(2,1)S(1)}, u32[]{:S(2)}, u32[]{:S(2)}) async-start(bf16[128,9,2,128]{3,2,1,0:T(2,128)(2,1)} %bitcast.16), calls=%async_computation | async-start | bytes 1179648 | tf_op jit(solution)/shard_map/all_to_all | solution.py:631
  16.9 12.5 %collective-permute-start.3 = (bf16[64,8,128]{2,1,0:T(8,128)(2,1)S(1)}, bf16[64,8,128]{2,1,0:T(8,128)(2,1)S(1)}, u32[]{:S(2)}, u32[]{:S(2)}) collective-permute-start(bf16[64,8,128]{2,1,0:T(8,128)(2,1)S(1)} %get-tuple-element.22.head_ref), channel_id=1, source_target_pairs={{1,0},{2,1},{3,2},{4,3},{5,4},{6,5},{7,6},{8,7},{9,8},{10,9},{11,1... | collective-permute-start | bytes 393224 | tf_op jit(solution)/shard_map/ppermute | solution.py:639
  18.1 11.4 %copy-start.7 = (bf16[256,384]{1,0:T(8,128)(2,1)S(1)}, bf16[256,384]{1,0:T(8,128)(2,1)}, u32[]{:S(2)}) copy-start(bf16[256,384]{1,0:T(8,128)(2,1)} %constant.10.clone.pick_ref) | copy-start | bytes 589828
  18.1 11.4 %copy-start.9 = (bf16[128,128]{1,0:T(8,128)(2,1)S(1)}, bf16[128,128]{1,0:T(8,128)(2,1)}, u32[]{:S(2)}) copy-start(bf16[128,128]{1,0:T(8,128)(2,1)} %constant.8.clone.eye_ref) | copy-start | bytes 98308
  18.1 11.4 %collective-permute-start.2 = (bf16[64,8,128]{2,1,0:T(8,128)(2,1)S(1)}, bf16[64,8,128]{2,1,0:T(8,128)(2,1)S(1)}, u32[]{:S(2)}, u32[]{:S(2)}) collective-permute-start(bf16[64,8,128]{2,1,0:T(8,128)(2,1)S(1)} %get-tuple-element.23.last_ref), channel_id=1, source_target_pairs={{0,1},{1,2},{2,3},{3,4},{4,5},{5,6},{6,7},{7,8},{8,9},{9,10},{10,1... | collective-permute-start | bytes 393224 | tf_op jit(solution)/shard_map/ppermute | solution.py:638
  22.2 2.6 %copy-start = (bf16[64,3,128,128]{3,2,1,0:T(8,128)(2,1)}, bf16[64,3,128,128]{3,2,1,0:T(8,128)(2,1)S(1)}, u32[]{:S(2)}) copy-start(bf16[64,3,128,128]{3,2,1,0:T(8,128)(2,1)S(1)} %prep.1.feat_hbm) | copy-start | bytes 18874372
  29.5 22.3 %slice-start = ((s8[6291456]{0:T(1024)(128)(4,1)}), s8[2097152]{0:T(1024)(128)(4,1)S(1)}, s32[]{:S(2)}) async-start(s8[6291456]{0:T(1024)(128)(4,1)} %bitcast.11), calls=%async_computation.3 | async-start | bytes 4194304
  31.4 20.4 %slice-start.1 = ((s8[6291456]{0:T(1024)(128)(4,1)}), s8[4194304]{0:T(1024)(128)(4,1)S(1)}, s32[]{:S(2)}) async-start(s8[6291456]{0:T(1024)(128)(4,1)} %bitcast.11), calls=%async_computation.4 | async-start | bytes 8388608
  46.5 10.5 %copy-start.2 = (bf16[72,136,128]{2,1,0:T(8,128)(2,1)}, bf16[72,136,128]{2,1,0:T(8,128)(2,1)S(1)}, u32[]{:S(2)}) copy-start(bf16[72,136,128]{2,1,0:T(8,128)(2,1)S(1)} %get-tuple-element.12.canvas_hbm.canvas_ref) | copy-start | bytes 7520260
  46.5 10.5 %copy-start.4 = (bf16[72,24,128]{2,1,0:T(8,128)(2,1)}, bf16[72,24,128]{2,1,0:T(8,128)(2,1)S(1)}, u32[]{:S(2)}) copy-start(bf16[72,24,128]{2,1,0:T(8,128)(2,1)S(1)} %get-tuple-element.16.rim_ref) | copy-start | bytes 1327108
  46.5 10.5 %collective-permute-start.1 = (bf16[4,136,128]{2,1,0:T(8,128)(2,1)S(1)}, bf16[4,136,128]{2,1,0:T(8,128)(2,1)S(1)}, u32[]{:S(2)}, u32[]{:S(2)}) collective-permute-start(bf16[4,136,128]{2,1,0:T(8,128)(2,1)S(1)} %get-tuple-element.14), channel_id=1, source_target_pairs={{16,0},{32,16},{48,32},{64,48},{80,64},{96,80},{112,96},{17,1},{33... | collective-permute-start | bytes 417800 | tf_op jit(solution)/shard_map/ppermute | solution.py:639
  47.8 9.2 %collective-permute-start = (bf16[5,136,128]{2,1,0:T(8,128)(2,1)S(1)}, bf16[5,136,128]{2,1,0:T(8,128)(2,1)S(1)}, u32[]{:S(2)}, u32[]{:S(2)}) collective-permute-start(bf16[5,136,128]{2,1,0:T(8,128)(2,1)S(1)} %get-tuple-element.13), channel_id=1, source_target_pairs={{0,16},{16,32},{32,48},{48,64},{64,80},{80,96},{96,112},{1,17},{17... | collective-permute-start | bytes 522248 | tf_op jit(solution)/shard_map/ppermute | solution.py:638
  57.0 22.8 %copy-start.6 = (bf16[1280,16]{1,0:T(8,128)(2,1)S(1)}, bf16[1280,16]{1,0:T(8,128)(2,1)}, u32[]{:S(2)}) copy-start(bf16[1280,16]{1,0:T(8,128)(2,1)} %constant.11.clone.spread_ref) | copy-start | bytes 122884
  59.2 29.8 %copy-start.3 = (bf16[72,136,128]{2,1,0:T(8,128)(2,1)S(1)}, bf16[72,136,128]{2,1,0:T(8,128)(2,1)}, u32[]{:S(2)}) copy-start(bf16[72,136,128]{2,1,0:T(8,128)(2,1)} %copy-done.2) | copy-start | bytes 7520260
  59.2 20.6 %all-to-all-start.1 = ((bf16[128,5,2,128]{3,2,1,0:T(2,128)(2,1)}), bf16[128,5,2,128]{3,2,1,0:T(2,128)(2,1)S(1)}, u32[]{:S(2)}, u32[]{:S(2)}) async-start(bf16[128,5,2,128]{3,2,1,0:T(2,128)(2,1)} %bitcast.6), calls=%async_computation.1 | async-start | bytes 655360 | tf_op jit(solution)/shard_map/all_to_all | solution.py:631
  67.7 1.0 copy-start.5
  68.8 5.2 %collective-permute-start.4 = (bf16[66,8,128]{2,1,0:T(8,128)(2,1)S(1)}, bf16[66,8,128]{2,1,0:T(8,128)(2,1)S(1)}, u32[]{:S(2)}, u32[]{:S(2)}) collective-permute-start(bf16[66,8,128]{2,1,0:T(8,128)(2,1)S(1)} %get-tuple-element.17), channel_id=1, source_target_pairs={{0,1},{1,2},{2,3},{3,4},{4,5},{5,6},{6,7},{7,8},{8,9},{9,10},{10,1... | collective-permute-start | bytes 405512 | tf_op jit(solution)/shard_map/ppermute | solution.py:638
  72.0 6.2 %collective-permute-start.5 = (bf16[66,8,128]{2,1,0:T(8,128)(2,1)S(1)}, bf16[66,8,128]{2,1,0:T(8,128)(2,1)S(1)}, u32[]{:S(2)}, u32[]{:S(2)}) collective-permute-start(bf16[66,8,128]{2,1,0:T(8,128)(2,1)S(1)} %get-tuple-element.18), channel_id=1, source_target_pairs={{1,0},{2,1},{3,2},{4,3},{5,4},{6,5},{7,6},{8,7},{9,8},{10,9},{11,1... | collective-permute-start | bytes 405512 | tf_op jit(solution)/shard_map/ppermute | solution.py:639
  74.0 0.7 copy-start.11
  78.2 0.6 copy-start.13
  80.9 20.0 %all-to-all-start.2 = ((bf16[128,5,2,128]{3,2,1,0:T(2,128)(2,1)}), bf16[128,5,2,128]{3,2,1,0:T(2,128)(2,1)S(1)}, u32[]{:S(2)}, u32[]{:S(2)}) async-start(bf16[128,5,2,128]{3,2,1,0:T(2,128)(2,1)} %bitcast.8), calls=%async_computation.2 | async-start | bytes 655360 | tf_op jit(solution)/shard_map/all_to_all | solution.py:631
  89.0 1.0 copy-start.10
  90.0 0.9 copy-start.12
  90.9 0.9 copy-start.14

commit v8 on v7

--- a/solution.py
+++ b/solution.py
@@ -655,15 +655,16 @@
     last, head = features[:, 120:128], features[:, 0:8]
     left, right = both_ways(last, head, "lon", True)
     feat = prep(shift, features)
+    canvas, side, rim, up, down = scatter(incoming)
+    side, left, right = lax.optimization_barrier((side, left, right))
     feat_side = prep_side(eye, pick, left, right, head, last)
-    canvas, side, rim, up, down = scatter(incoming)
     grid_above, grid_below = both_ways(down, up, "lat", False)
     acc = own_grad(canvas, side, feat, feat_side)
     part = halo_grad(acc, grid_above, grid_below, feat, feat_side)
     got = exchange(part)
     send_right, send_left = sides(rim, grid_above, grid_below)
     from_left, from_right = both_ways(send_right, send_left, "lon", True)
-    got, from_left, from_right = lax.optimization_barrier((got, from_left, from_right))
+    got, _, _ = lax.optimization_barrier((got, send_right, send_left))
     every = exchange(share(got))
     input_grad = conv(canvas, grid_above, grid_below, from_left, from_right, conv_weight)
     weight_grad = finish(every)

time: 102 us -> 97.5 us (0.956)
  starting transfers between devices: 39.8 us -> 33.2 us
  local copies, waits for them, and re-layouts: 7.79 us -> 4.69 us
  Pallas kernels: 38 us -> 40.6 us
  waiting for transfers between devices: 14.4 us -> 16.9 us
    all_to_all x3, waiting for transfers between devices: 4.16 us -> 16.9 us  [exchange(): return lax.all_to_all(pairs, AXES, 0, 0, tiled=True).reshape(rows.shape)]
    ppermute x3, waiting for transfers between devices: 8.26 us -> 0.01 us  [both_ways(): lax.ppermute(back, axis, [((i + 1) % count, i) for i in range(ends)])]
    all_to_all x3, starting transfers between devices: 28 us -> 24.3 us  [exchange(): return lax.all_to_all(pairs, AXES, 0, 0, tiled=True).reshape(rows.shape)]
    unnamed x34 -> x20, local copies, waits for them, and re-layouts: 7.75 us -> 4.66 us
    ppermute x3, waiting for transfers between devices: 1.99 us -> 0.01 us  [both_ways(): lax.ppermute(forth, axis, [(i, (i + 1) % count) for i in range(ends)])]
    ppermute x3, starting transfers between devices: 9.39 us -> 7.64 us  [both_ways(): lax.ppermute(forth, axis, [(i, (i + 1) % count) for i in range(ends)])]
    ppermute x3, starting transfers between devices: 2.43 us -> 1.3 us  [both_ways(): lax.ppermute(back, axis, [((i + 1) % count, i) for i in range(ends)])]
  transfers between devices with their start and end apart: 9 -> 9, of which waited for: 6 -> 3; matrix products, arithmetic and copies ran while one was open for 0% -> 0% of each run, Pallas kernels for 15% -> 35%
where the time goes in v8:
time: 97.5 us; the launch traced here: 97.1 us
  Pallas kernels  40.6 us (42%)
  starting transfers between devices  33.2 us (34%)
  waiting for transfers between devices  16.9 us (17%)
  local copies, waits for them, and re-layouts  4.69 us (5%)
  between operations  1.67 us (2%)
    all_to_all x3, starting transfers between devices, exchange(): return lax.all_to_all(pairs, AXES, 0, 0, tiled=True).reshape(rows.shape)  24.3 us
    all_to_all x3, waiting for transfers between devices, exchange(): return lax.all_to_all(pairs, AXES, 0, 0, tiled=True).reshape(rows.shape)  16.9 us
    pallas_call x1, Pallas kernels, scatter(): pl.pallas_call(scatter_kernel, out_shape=(jax.ShapeDtypeStruct((72, 136,...  15.1 us
    pallas_call x1, Pallas kernels, conv(): pl.pallas_call(conv_kernel, grid=(8,), out_shape=jax.ShapeDtypeStruct((64...  8.1 us
    ppermute x3, starting transfers between devices, both_ways(): lax.ppermute(forth, axis, [(i, (i + 1) % count) for i in range(ends)])  7.64 us
    pallas_call x1, Pallas kernels, own_grad(): pl.pallas_call(own_grad_kernel, out_shape=jax.ShapeDtypeStruct((384, 384)...  5.13 us
    unnamed x20, local copies, waits for them, and re-layouts  4.66 us
    pallas_call x1, Pallas kernels, pack(): pl.pallas_call(pack_kernel, out_shape=jax.ShapeDtypeStruct((TILES * CHUNK...  3.94 us
  transfers between devices with their start and end apart: 9, of which 3 were waited for; matrix products, arithmetic and copies ran while one was open for 0% of the time, Pallas kernels for 35%

profile of v8, /device:TPU:1, one launch (start us, length us, event | category | flops | bytes accessed | tf_op | source)
XLA Modules:
  0.0 97.1 jit_solution(14249974305458503751)
XLA Ops:
  1.4 0.0 copy-start.7
  1.4 3.9 %pack.1 = bf16[2304,128]{1,0:T(8,128)(2,1)} custom-call(s32[1]{0:T(128)S(6)} %copy.14.live_ref, s32[1,1024]{1,0:T(1,128)} %bitcast.16, s32[1,1024]{1,0:T(1,128)} %bitcast.17, s32[1,1024]{1,0:T(1,128)} %bitcast.18, bf16[2,1024]{1,0:T(2,128)(2,1)} %bitcast.19, bf16[1024,128]{1,0:T(8,128)(2,1)} %rows_ref.1), custom_call_target="tpu_custom_call" | custom-call | flops 700000000 | bytes 1500000 | tf_op jit(solution)/shard_map/pack/pallas_call | solution.py:81
  5.4 11.5 %all-to-all-start = ((bf16[128,9,2,128]{3,2,1,0:T(2,128)(2,1)}), bf16[128,9,2,128]{3,2,1,0:T(2,128)(2,1)S(1)}, u32[]{:S(2)}, u32[]{:S(2)}) async-start(bf16[128,9,2,128]{3,2,1,0:T(2,128)(2,1)} %bitcast.14), calls=%async_computation | async-start | bytes 1179648 | tf_op jit(solution)/shard_map/all_to_all | solution.py:631
  16.9 3.2 %collective-permute-start.4 = (bf16[64,8,128]{2,1,0:T(8,128)(2,1)S(1)}, bf16[64,8,128]{2,1,0:T(8,128)(2,1)S(1)}, u32[]{:S(2)}, u32[]{:S(2)}) collective-permute-start(bf16[64,8,128]{2,1,0:T(8,128)(2,1)S(1)} %get-tuple-element.25.last_ref), channel_id=1, source_target_pairs={{0,1},{1,2},{2,3},{3,4},{4,5},{5,6},{6,7},{7,8},{8,9},{9,10},{10,1... | collective-permute-start | bytes 393224 | tf_op jit(solution)/shard_map/ppermute | solution.py:638
  20.1 1.9 %prep.1.feat_hbm = bf16[64,3,128,128]{3,2,1,0:T(8,128)(2,1)S(1)} custom-call(bf16[128,256]{1,0:T(8,128)(2,1)S(1)} %copy-done.7, bf16[64,128,128]{2,1,0:T(8,128)(2,1)S(1)} %copy-done.2), custom_call_target="tpu_custom_call" | custom-call | flops 2200000000 | bytes 8000000 | tf_op jit(solution)/shard_map/prep/pallas_call | solution.py:124
  22.1 2.7 %copy-done = bf16[64,3,128,128]{3,2,1,0:T(8,128)(2,1)} copy-done((bf16[64,3,128,128]{3,2,1,0:T(8,128)(2,1)}, bf16[64,3,128,128]{3,2,1,0:T(8,128)(2,1)S(1)}, u32[]{:S(2)}) %copy-start) | copy-done | bytes 6291480
  24.7 6.9 %all-to-all-done = bf16[128,9,2,128]{3,2,1,0:T(2,128)(2,1)S(1)} async-done(((bf16[128,9,2,128]{3,2,1,0:T(2,128)(2,1)}), bf16[128,9,2,128]{3,2,1,0:T(2,128)(2,1)S(1)}, u32[]{:S(2)}, u32[]{:S(2)}) %all-to-all-start) | async-done | bytes 589856 | tf_op jit(solution)/shard_map/all_to_all | solution.py:631
  31.7 15.1 %scatter.1 = (bf16[72,136,128]{2,1,0:T(8,128)(2,1)S(1)}, bf16[72,16,128]{2,1,0:T(8,128)(2,1)S(1)}, bf16[72,24,128]{2,1,0:T(8,128)(2,1)S(1)}, bf16[4,136,128]{2,1,0:T(8,128)(2,1)S(1)}, bf16[5,136,128]{2,1,0:T(8,128)(2,1)S(1)}) custom-call(bf16[2304,128]{1,0:T(8,128)(2,1)S(1)} %bitcast.13), custom_call_target="tpu_custom_call" | custom-call | flops 5200000000 | bytes 4000000 | tf_op jit(solution)/shard_map/scatter/pallas_call | solution.py:287
  46.8 0.0 copy-start.3
  46.8 0.0 collective-permute-done.4.left_ref
  46.8 1.3 %collective-permute-start = (bf16[5,136,128]{2,1,0:T(8,128)(2,1)S(1)}, bf16[5,136,128]{2,1,0:T(8,128)(2,1)S(1)}, u32[]{:S(2)}, u32[]{:S(2)}) collective-permute-start(bf16[5,136,128]{2,1,0:T(8,128)(2,1)S(1)} %get-tuple-element.14), channel_id=1, source_target_pairs={{0,16},{16,32},{32,48},{48,64},{64,80},{80,96},{96,112},{1,17},{17... | collective-permute-start | bytes 522248 | tf_op jit(solution)/shard_map/ppermute | solution.py:638
  48.1 1.3 %collective-permute-start.1 = (bf16[4,136,128]{2,1,0:T(8,128)(2,1)S(1)}, bf16[4,136,128]{2,1,0:T(8,128)(2,1)S(1)}, u32[]{:S(2)}, u32[]{:S(2)}) collective-permute-start(bf16[4,136,128]{2,1,0:T(8,128)(2,1)S(1)} %get-tuple-element.15), channel_id=1, source_target_pairs={{16,0},{32,16},{48,32},{64,48},{80,64},{96,80},{112,96},{17,1},{33... | collective-permute-start | bytes 417800 | tf_op jit(solution)/shard_map/ppermute | solution.py:639
  49.4 1.5 %prep_side.1.feat_side_hbm.feat_side_ref = bf16[384,1024]{1,0:T(8,128)(2,1)S(1)} custom-call(bf16[128,128]{1,0:T(8,128)(2,1)S(1)} %copy-done.8, bf16[256,384]{1,0:T(8,128)(2,1)S(1)} %copy-done.6, bf16[64,8,128]{2,1,0:T(8,128)(2,1)S(1)} %collective-permute-done.4.left_ref, bf16[64,8,128]{2,1,0:T(8,128)(2,1)} %collective-permute-done.5.right_ref, ...), custom_call_target="tpu_custom_call" | custom-call | flops 300000000 | bytes 1500000 | tf_op jit(solution)/shard_map/prep_side/pallas_call | solution.py:155
  51.0 5.1 %own_grad.1.acc_ref = f32[384,384]{1,0:T(8,128)S(1)} custom-call(bf16[72,136,128]{2,1,0:T(8,128)(2,1)S(1)} %get-tuple-element.13.canvas_ref.canvas_hbm, bf16[72,16,128]{2,1,0:T(8,128)(2,1)S(1)} %get-tuple-element.20.side_hbm, bf16[64,3,128,128]{3,2,1,0:T(8,128)(2,1)S(1)} %copy-done.1, bf16[384,1024]{1,0:T(8,128)(2,1)S(1)} %prep_side.1.feat_side_hbm.feat_side_ref), custom_call_target="tpu_custom_call" | custom-call | flops 2800000000 | bytes 10000000 | tf_op jit(solution)/shard_map/own_grad/pallas_call | solution.py:374
  56.1 0.0 copy-start.5
  56.1 0.0 collective-permute-done.1.below_ref
  56.1 0.0 collective-permute-done.above_ref
  56.1 2.2 %halo_grad.1 = bf16[1280,128]{1,0:T(8,128)(2,1)} custom-call(f32[384,384]{1,0:T(8,128)S(1)} %own_grad.1.acc_ref, bf16[5,136,128]{2,1,0:T(8,128)(2,1)S(1)} %collective-permute-done.above_ref, bf16[4,136,128]{2,1,0:T(8,128)(2,1)S(1)} %collective-permute-done.1.below_ref, bf16[64,3,128,128]{3,2,1,0:T(8,128)(2,1)S(1)} %copy-done.1, ...), custom_call_target="tpu_custom_call" | custom-call | flops 420000000 | bytes 3500000 | tf_op jit(solution)/shard_map/halo_grad/pallas_call | solution.py:458
  58.3 8.7 %all-to-all-start.1 = ((bf16[128,5,2,128]{3,2,1,0:T(2,128)(2,1)}), bf16[128,5,2,128]{3,2,1,0:T(2,128)(2,1)S(1)}, u32[]{:S(2)}, u32[]{:S(2)}) async-start(bf16[128,5,2,128]{3,2,1,0:T(2,128)(2,1)} %bitcast.6), calls=%async_computation.1 | async-start | bytes 655360 | tf_op jit(solution)/shard_map/all_to_all | solution.py:631
  67.0 0.0 copy-start.4
  67.0 1.0 %copy-done.4 = bf16[72,24,128]{2,1,0:T(8,128)(2,1)S(1)} copy-done((bf16[72,24,128]{2,1,0:T(8,128)(2,1)S(1)}, bf16[72,24,128]{2,1,0:T(8,128)(2,1)}, u32[]{:S(2)}) %copy-start.4) | copy-done | bytes 442392
  68.0 0.8 sides.1
  68.8 3.1 %collective-permute-start.2 = (bf16[66,8,128]{2,1,0:T(8,128)(2,1)}, bf16[66,8,128]{2,1,0:T(8,128)(2,1)}, u32[]{:S(2)}, u32[]{:S(2)}) collective-permute-start(bf16[66,8,128]{2,1,0:T(8,128)(2,1)} %get-tuple-element.17), channel_id=1, source_target_pairs={{0,1},{1,2},{2,3},{3,4},{4,5},{5,6},{6,7},{7,8},{8,9},{9,10},{10,1... | collective-permute-start | bytes 405512 | tf_op jit(solution)/shard_map/ppermute | solution.py:638
  72.0 0.0 collective-permute-start.3
  72.0 7.2 %all-to-all-done.1 = bf16[128,5,2,128]{3,2,1,0:T(2,128)(2,1)S(1)} async-done(((bf16[128,5,2,128]{3,2,1,0:T(2,128)(2,1)}), bf16[128,5,2,128]{3,2,1,0:T(2,128)(2,1)S(1)}, u32[]{:S(2)}, u32[]{:S(2)}) %all-to-all-start.1) | async-done | bytes 327712 | tf_op jit(solution)/shard_map/all_to_all | solution.py:631
  79.2 1.1 %share.1 = bf16[1280,128]{1,0:T(8,128)(2,1)} custom-call(bf16[1280,16]{1,0:T(8,128)(2,1)S(1)} %copy-done.5, bf16[1280,128]{1,0:T(8,128)(2,1)S(1)} %bitcast.12), custom_call_target="tpu_custom_call" | custom-call | flops 10000000 | bytes 1000000 | tf_op jit(solution)/shard_map/share/pallas_call | solution.py:601
  80.3 4.1 %all-to-all-start.2 = ((bf16[128,5,2,128]{3,2,1,0:T(2,128)(2,1)}), bf16[128,5,2,128]{3,2,1,0:T(2,128)(2,1)S(1)}, u32[]{:S(2)}, u32[]{:S(2)}) async-start(bf16[128,5,2,128]{3,2,1,0:T(2,128)(2,1)} %bitcast.8), calls=%async_computation.2 | async-start | bytes 655360 | tf_op jit(solution)/shard_map/all_to_all | solution.py:631
  84.4 0.0 copy-start.9
  84.4 1.0 copy-done.9
  85.4 8.1 %conv.1 = bf16[64,128,128]{2,1,0:T(8,128)(2,1)} custom-call(bf16[72,136,128]{2,1,0:T(8,128)(2,1)S(1)} %get-tuple-element.13.canvas_ref.canvas_hbm, bf16[5,136,128]{2,1,0:T(8,128)(2,1)S(1)} %collective-permute-done.above_ref, bf16[4,136,128]{2,1,0:T(8,128)(2,1)S(1)} %collective-permute-done.1.below_ref, bf16[66,8,128]{2,1,0:T(8,128)(2,1)} %collective-permute-done.2.left_ref, ...), custom_call_target="tpu_custom_call" | custom-call | flops 2700000000 | bytes 4500000 | tf_op jit(solution)/shard_map/conv/pallas_call | solution.py:569
  93.5 2.8 %all-to-all-done.2 = bf16[128,5,2,128]{3,2,1,0:T(2,128)(2,1)S(1)} async-done(((bf16[128,5,2,128]{3,2,1,0:T(2,128)(2,1)}), bf16[128,5,2,128]{3,2,1,0:T(2,128)(2,1)S(1)}, u32[]{:S(2)}, u32[]{:S(2)}) %all-to-all-start.2) | async-done | bytes 327712 | tf_op jit(solution)/shard_map/all_to_all | solution.py:631
  96.2 0.9 finish.1
  (17 shorter events, 0.1 us)
Async XLA Ops:
  0.6 16.3 %copy-start.2 = (bf16[64,128,128]{2,1,0:T(8,128)(2,1)S(1)}, bf16[64,128,128]{2,1,0:T(8,128)(2,1)}, u32[]{:S(2)}) copy-start(bf16[64,128,128]{2,1,0:T(8,128)(2,1)} %feat_ref.1) | copy-start | bytes 6291460
  1.4 18.7 %copy-start.7 = (bf16[128,256]{1,0:T(8,128)(2,1)S(1)}, bf16[128,256]{1,0:T(8,128)(2,1)}, u32[]{:S(2)}) copy-start(bf16[128,256]{1,0:T(8,128)(2,1)} %constant.9.clone.shift_ref) | copy-start | bytes 196612
  5.4 26.3 %all-to-all-start = ((bf16[128,9,2,128]{3,2,1,0:T(2,128)(2,1)}), bf16[128,9,2,128]{3,2,1,0:T(2,128)(2,1)S(1)}, u32[]{:S(2)}, u32[]{:S(2)}) async-start(bf16[128,9,2,128]{3,2,1,0:T(2,128)(2,1)} %bitcast.14), calls=%async_computation | async-start | bytes 1179648 | tf_op jit(solution)/shard_map/all_to_all | solution.py:631
  16.9 29.8 %collective-permute-start.4 = (bf16[64,8,128]{2,1,0:T(8,128)(2,1)S(1)}, bf16[64,8,128]{2,1,0:T(8,128)(2,1)S(1)}, u32[]{:S(2)}, u32[]{:S(2)}) collective-permute-start(bf16[64,8,128]{2,1,0:T(8,128)(2,1)S(1)} %get-tuple-element.25.last_ref), channel_id=1, source_target_pairs={{0,1},{1,2},{2,3},{3,4},{4,5},{5,6},{6,7},{7,8},{8,9},{9,10},{10,1... | collective-permute-start | bytes 393224 | tf_op jit(solution)/shard_map/ppermute | solution.py:638
  20.1 26.6 %collective-permute-start.5 = (bf16[64,8,128]{2,1,0:T(8,128)(2,1)S(1)}, bf16[64,8,128]{2,1,0:T(8,128)(2,1)}, u32[]{:S(2)}, u32[]{:S(2)}) collective-permute-start(bf16[64,8,128]{2,1,0:T(8,128)(2,1)S(1)} %get-tuple-element.24.head_ref), channel_id=1, source_target_pairs={{1,0},{2,1},{3,2},{4,3},{5,4},{6,5},{7,6},{8,7},{9,8},{10,9},{11,1... | collective-permute-start | bytes 393224 | tf_op jit(solution)/shard_map/ppermute | solution.py:639
  22.1 2.7 %copy-start = (bf16[64,3,128,128]{3,2,1,0:T(8,128)(2,1)}, bf16[64,3,128,128]{3,2,1,0:T(8,128)(2,1)S(1)}, u32[]{:S(2)}) copy-start(bf16[64,3,128,128]{3,2,1,0:T(8,128)(2,1)S(1)} %prep.1.feat_hbm) | copy-start | bytes 18874372
  31.7 17.7 %copy-start.6 = (bf16[256,384]{1,0:T(8,128)(2,1)S(1)}, bf16[256,384]{1,0:T(8,128)(2,1)}, u32[]{:S(2)}) copy-start(bf16[256,384]{1,0:T(8,128)(2,1)} %constant.10.clone.pick_ref) | copy-start | bytes 589828
  31.7 17.7 %copy-start.8 = (bf16[128,128]{1,0:T(8,128)(2,1)S(1)}, bf16[128,128]{1,0:T(8,128)(2,1)}, u32[]{:S(2)}) copy-start(bf16[128,128]{1,0:T(8,128)(2,1)} %constant.8.clone.eye_ref) | copy-start | bytes 98308
  31.7 19.3 %copy-start.1 = (bf16[64,3,128,128]{3,2,1,0:T(8,128)(2,1)S(1)}, bf16[64,3,128,128]{3,2,1,0:T(8,128)(2,1)}, u32[]{:S(2)}) copy-start(bf16[64,3,128,128]{3,2,1,0:T(8,128)(2,1)} %copy-done) | copy-start | bytes 18874372
  46.8 9.4 %copy-start.3 = (bf16[72,24,128]{2,1,0:T(8,128)(2,1)}, bf16[72,24,128]{2,1,0:T(8,128)(2,1)S(1)}, u32[]{:S(2)}) copy-start(bf16[72,24,128]{2,1,0:T(8,128)(2,1)S(1)} %get-tuple-element.16.rim_ref) | copy-start | bytes 1327108
  46.8 9.4 %collective-permute-start = (bf16[5,136,128]{2,1,0:T(8,128)(2,1)S(1)}, bf16[5,136,128]{2,1,0:T(8,128)(2,1)S(1)}, u32[]{:S(2)}, u32[]{:S(2)}) collective-permute-start(bf16[5,136,128]{2,1,0:T(8,128)(2,1)S(1)} %get-tuple-element.14), channel_id=1, source_target_pairs={{0,16},{16,32},{32,48},{48,64},{64,80},{80,96},{96,112},{1,17},{17... | collective-permute-start | bytes 522248 | tf_op jit(solution)/shard_map/ppermute | solution.py:638
  48.1 8.0 %collective-permute-start.1 = (bf16[4,136,128]{2,1,0:T(8,128)(2,1)S(1)}, bf16[4,136,128]{2,1,0:T(8,128)(2,1)S(1)}, u32[]{:S(2)}, u32[]{:S(2)}) collective-permute-start(bf16[4,136,128]{2,1,0:T(8,128)(2,1)S(1)} %get-tuple-element.15), channel_id=1, source_target_pairs={{16,0},{32,16},{48,32},{64,48},{80,64},{96,80},{112,96},{17,1},{33... | collective-permute-start | bytes 417800 | tf_op jit(solution)/shard_map/ppermute | solution.py:639
  56.1 23.1 %copy-start.5 = (bf16[1280,16]{1,0:T(8,128)(2,1)S(1)}, bf16[1280,16]{1,0:T(8,128)(2,1)}, u32[]{:S(2)}) copy-start(bf16[1280,16]{1,0:T(8,128)(2,1)} %constant.11.clone.spread_ref) | copy-start | bytes 122884
  58.3 20.8 %all-to-all-start.1 = ((bf16[128,5,2,128]{3,2,1,0:T(2,128)(2,1)}), bf16[128,5,2,128]{3,2,1,0:T(2,128)(2,1)S(1)}, u32[]{:S(2)}, u32[]{:S(2)}) async-start(bf16[128,5,2,128]{3,2,1,0:T(2,128)(2,1)} %bitcast.6), calls=%async_computation.1 | async-start | bytes 655360 | tf_op jit(solution)/shard_map/all_to_all | solution.py:631
  67.0 1.0 %copy-start.4 = (bf16[72,24,128]{2,1,0:T(8,128)(2,1)S(1)}, bf16[72,24,128]{2,1,0:T(8,128)(2,1)}, u32[]{:S(2)}) copy-start(bf16[72,24,128]{2,1,0:T(8,128)(2,1)} %copy-done.3) | copy-start | bytes 1327108
  68.8 15.5 %collective-permute-start.2 = (bf16[66,8,128]{2,1,0:T(8,128)(2,1)}, bf16[66,8,128]{2,1,0:T(8,128)(2,1)}, u32[]{:S(2)}, u32[]{:S(2)}) collective-permute-start(bf16[66,8,128]{2,1,0:T(8,128)(2,1)} %get-tuple-element.17), channel_id=1, source_target_pairs={{0,1},{1,2},{2,3},{3,4},{4,5},{5,6},{6,7},{7,8},{8,9},{9,10},{10,1... | collective-permute-start | bytes 405512 | tf_op jit(solution)/shard_map/ppermute | solution.py:638
  72.0 12.4 %collective-permute-start.3 = (bf16[66,8,128]{2,1,0:T(8,128)(2,1)}, bf16[66,8,128]{2,1,0:T(8,128)(2,1)}, u32[]{:S(2)}, u32[]{:S(2)}) collective-permute-start(bf16[66,8,128]{2,1,0:T(8,128)(2,1)} %get-tuple-element.18), channel_id=1, source_target_pairs={{1,0},{2,1},{3,2},{4,3},{5,4},{6,5},{7,6},{8,7},{9,8},{10,9},{11,1... | collective-permute-start | bytes 405512 | tf_op jit(solution)/shard_map/ppermute | solution.py:639
  80.3 16.0 %all-to-all-start.2 = ((bf16[128,5,2,128]{3,2,1,0:T(2,128)(2,1)}), bf16[128,5,2,128]{3,2,1,0:T(2,128)(2,1)S(1)}, u32[]{:S(2)}, u32[]{:S(2)}) async-start(bf16[128,5,2,128]{3,2,1,0:T(2,128)(2,1)} %bitcast.8), calls=%async_computation.2 | async-start | bytes 655360 | tf_op jit(solution)/shard_map/all_to_all | solution.py:631
  84.4 1.0 copy-start.9

commit v9 on v8

--- a/solution.py
+++ b/solution.py
@@ -233,8 +233,7 @@
     def eight_lines(step, carry):
         start = pl.multiple_of(step * 8, 8)
         lat8 = lat_w[pl.ds(start, 8), :]
-        acc = jnp.zeros((8 * 128, 128), F32)
-        side = jnp.zeros((8 * 8, 128), F32)
+        acc = jnp.zeros((8 * 136, 128), F32)
         for k in range(total // 256):
             cols = slice(k * 256, (k + 1) * 256)
             lon = lon_w[:, cols].reshape(8, 16, 256)
@@ -248,11 +247,10 @@
                     lat8[i : i + 1, cols].astype(BF16).astype(F32), (8, 256)
                 )
                 side_parts.append(side_lon * one8)
-            rows = rows_ref[cols, :]
-            acc = acc + mm(jnp.concatenate(parts, axis=0), rows)
-            side = side + mm(jnp.concatenate(side_parts, axis=0).astype(BF16), rows)
-        ends = acc.reshape(8, 128, 128)
-        side = side.reshape(8, 8, 128)
+            parts.append(jnp.concatenate(side_parts, axis=0).astype(BF16))
+            acc = acc + mm(jnp.concatenate(parts, axis=0), rows_ref[cols, :])
+        ends = acc[0:1024].reshape(8, 128, 128)
+        side = acc[1024:1088].reshape(8, 8, 128)
         lines = pl.ds(start, 8)
         canvas_ref[lines, 0:128, :] = ends.astype(BF16)
         canvas_ref[lines, 128:136, :] = side.astype(BF16)
@@ -581,19 +579,16 @@
     )(*args)
 
 
-def share_rows():
-    which = np.arange(TILES * SHARE)[:, None] % SHARE == np.arange(16)[None, :]
-    return jnp.asarray(which.astype(np.float32), BF16)
-
-
-def share_kernel(spread_ref, in_ref, out_ref):
-    shape = (16, TILES * SHARE)
-    row = lax.broadcasted_iota(jnp.int32, shape, 1)
-    pick = jnp.where(
-        lax.rem(row, SHARE) == lax.broadcasted_iota(jnp.int32, shape, 0), 1.0, 0.0
-    ).astype(BF16)
-    mine = mm(pick, in_ref[...]).astype(BF16)
-    out_ref[...] = mm(spread_ref[...], mine).astype(BF16)
+def share_kernel(in_ref, out_ref):
+    def line_of(shape, axis):
+        row = lax.broadcasted_iota(jnp.int32, shape, axis)
+        line = lax.broadcasted_iota(jnp.int32, shape, 1 - axis)
+        return jnp.where(lax.rem(row, SHARE) == line, 1.0, 0.0).astype(BF16)
+
+    mine = mm(line_of((16, TILES * SHARE), 1), in_ref[...]).astype(BF16)
+    block = mm(line_of((8 * SHARE, 16), 0), mine).astype(BF16)
+    for i in range(TILES // 8):
+        out_ref[i * 8 * SHARE : (i + 1) * 8 * SHARE, :] = block
 
 
 def share(got):
@@ -601,12 +596,12 @@
     return pl.pallas_call(
         share_kernel,
         out_shape=jax.ShapeDtypeStruct(got.shape, BF16),
-        in_specs=[vmem] * 2,
+        in_specs=[vmem],
         out_specs=vmem,
         compiler_params=pltpu.CompilerParams(vmem_limit_bytes=3 << 20),
         cost_estimate=pl.CostEstimate(flops=10_000_000, bytes_accessed=1_000_000, transcendentals=0),
         name="share",
-    )(share_rows(), got)
+    )(got)
 
 
 def finish_kernel(in_ref, out_ref):

time: 97.5 us -> 97.1 us (level)
    unnamed x20 -> x18, local copies, waits for them, and re-layouts: 4.66 us -> 3.69 us
  transfers between devices with their start and end apart: 9 -> 9, of which waited for: 3 -> 3; matrix products, arithmetic and copies ran while one was open for 0% -> 0% of each run, Pallas kernels for 35% -> 34%
where the time goes in v9:
time: 97.1 us; the launch traced here: 96.7 us
  Pallas kernels  40.3 us (42%)
  starting transfers between devices  33.2 us (34%)
  waiting for transfers between devices  17.8 us (18%)
  local copies, waits for them, and re-layouts  3.73 us (4%)
  between operations  1.66 us (2%)
    all_to_all x3, starting transfers between devices, exchange(): return lax.all_to_all(pairs, AXES, 0, 0, tiled=True).reshape(rows.shape)  24.3 us
    all_to_all x3, waiting for transfers between devices, exchange(): return lax.all_to_all(pairs, AXES, 0, 0, tiled=True).reshape(rows.shape)  17.8 us
    pallas_call x1, Pallas kernels, scatter(): pl.pallas_call(scatter_kernel, out_shape=(jax.ShapeDtypeStruct((72, 136,...  14.8 us
    pallas_call x1, Pallas kernels, conv(): pl.pallas_call(conv_kernel, grid=(8,), out_shape=jax.ShapeDtypeStruct((64...  8.15 us
    ppermute x3, starting transfers between devices, both_ways(): lax.ppermute(forth, axis, [(i, (i + 1) % count) for i in range(ends)])  7.64 us
    pallas_call x1, Pallas kernels, own_grad(): pl.pallas_call(own_grad_kernel, out_shape=jax.ShapeDtypeStruct((384, 384)...  5.13 us
    pallas_call x1, Pallas kernels, pack(): pl.pallas_call(pack_kernel, out_shape=jax.ShapeDtypeStruct((TILES * CHUNK...  3.94 us
    unnamed x18, local copies, waits for them, and re-layouts  3.69 us
  transfers between devices with their start and end apart: 9, of which 3 were waited for; matrix products, arithmetic and copies ran while one was open for 0% of the time, Pallas kernels for 34%

profile of v9, /device:TPU:1, one launch (start us, length us, event | category | flops | bytes accessed | tf_op | source)
XLA Modules:
  0.0 96.7 jit_solution(223289937342271781)
XLA Ops:
  1.4 0.0 copy-start.6
  1.4 3.9 %pack.1 = bf16[2304,128]{1,0:T(8,128)(2,1)} custom-call(s32[1]{0:T(128)S(6)} %copy.13.live_ref, s32[1,1024]{1,0:T(1,128)} %bitcast.16, s32[1,1024]{1,0:T(1,128)} %bitcast.17, s32[1,1024]{1,0:T(1,128)} %bitcast.18, bf16[2,1024]{1,0:T(2,128)(2,1)} %bitcast.19, bf16[1024,128]{1,0:T(8,128)(2,1)} %rows_ref.1), custom_call_target="tpu_custom_call" | custom-call | flops 700000000 | bytes 1500000 | tf_op jit(solution)/shard_map/pack/pallas_call | solution.py:81
  5.4 11.5 %all-to-all-start = ((bf16[128,9,2,128]{3,2,1,0:T(2,128)(2,1)}), bf16[128,9,2,128]{3,2,1,0:T(2,128)(2,1)S(1)}, u32[]{:S(2)}, u32[]{:S(2)}) async-start(bf16[128,9,2,128]{3,2,1,0:T(2,128)(2,1)} %bitcast.14), calls=%async_computation | async-start | bytes 1179648 | tf_op jit(solution)/shard_map/all_to_all | solution.py:626
  16.9 3.2 %collective-permute-start.4 = (bf16[64,8,128]{2,1,0:T(8,128)(2,1)S(1)}, bf16[64,8,128]{2,1,0:T(8,128)(2,1)S(1)}, u32[]{:S(2)}, u32[]{:S(2)}) collective-permute-start(bf16[64,8,128]{2,1,0:T(8,128)(2,1)S(1)} %get-tuple-element.25.last_ref), channel_id=1, source_target_pairs={{0,1},{1,2},{2,3},{3,4},{4,5},{5,6},{6,7},{7,8},{8,9},{9,10},{10,1... | collective-permute-start | bytes 393224 | tf_op jit(solution)/shard_map/ppermute | solution.py:633
  20.1 0.0 collective-permute-start.5
  20.1 1.9 %prep.1.feat_hbm = bf16[64,3,128,128]{3,2,1,0:T(8,128)(2,1)S(1)} custom-call(bf16[128,256]{1,0:T(8,128)(2,1)S(1)} %copy-done.6, bf16[64,128,128]{2,1,0:T(8,128)(2,1)S(1)} %copy-done.2), custom_call_target="tpu_custom_call" | custom-call | flops 2200000000 | bytes 8000000 | tf_op jit(solution)/shard_map/prep/pallas_call | solution.py:124
  22.1 2.6 %copy-done = bf16[64,3,128,128]{3,2,1,0:T(8,128)(2,1)} copy-done((bf16[64,3,128,128]{3,2,1,0:T(8,128)(2,1)}, bf16[64,3,128,128]{3,2,1,0:T(8,128)(2,1)S(1)}, u32[]{:S(2)}) %copy-start) | copy-done | bytes 6291480
  24.7 6.9 %all-to-all-done = bf16[128,9,2,128]{3,2,1,0:T(2,128)(2,1)S(1)} async-done(((bf16[128,9,2,128]{3,2,1,0:T(2,128)(2,1)}), bf16[128,9,2,128]{3,2,1,0:T(2,128)(2,1)S(1)}, u32[]{:S(2)}, u32[]{:S(2)}) %all-to-all-start) | async-done | bytes 589856 | tf_op jit(solution)/shard_map/all_to_all | solution.py:626
  31.7 14.8 %scatter.1 = (bf16[72,136,128]{2,1,0:T(8,128)(2,1)S(1)}, bf16[72,16,128]{2,1,0:T(8,128)(2,1)S(1)}, bf16[72,24,128]{2,1,0:T(8,128)(2,1)S(1)}, bf16[4,136,128]{2,1,0:T(8,128)(2,1)S(1)}, bf16[5,136,128]{2,1,0:T(8,128)(2,1)S(1)}) custom-call(bf16[2304,128]{1,0:T(8,128)(2,1)S(1)} %bitcast.13), custom_call_target="tpu_custom_call" | custom-call | flops 5200000000 | bytes 4000000 | tf_op jit(solution)/shard_map/scatter/pallas_call | solution.py:285
  46.4 0.0 copy-start.3
  46.5 0.0 collective-permute-done.5.right_ref
  46.5 1.3 %collective-permute-start = (bf16[5,136,128]{2,1,0:T(8,128)(2,1)S(1)}, bf16[5,136,128]{2,1,0:T(8,128)(2,1)S(1)}, u32[]{:S(2)}, u32[]{:S(2)}) collective-permute-start(bf16[5,136,128]{2,1,0:T(8,128)(2,1)S(1)} %get-tuple-element.14), channel_id=1, source_target_pairs={{0,16},{16,32},{32,48},{48,64},{64,80},{80,96},{96,112},{1,17},{17... | collective-permute-start | bytes 522248 | tf_op jit(solution)/shard_map/ppermute | solution.py:633
  47.8 1.3 %collective-permute-start.1 = (bf16[4,136,128]{2,1,0:T(8,128)(2,1)S(1)}, bf16[4,136,128]{2,1,0:T(8,128)(2,1)S(1)}, u32[]{:S(2)}, u32[]{:S(2)}) collective-permute-start(bf16[4,136,128]{2,1,0:T(8,128)(2,1)S(1)} %get-tuple-element.15), channel_id=1, source_target_pairs={{16,0},{32,16},{48,32},{64,48},{80,64},{96,80},{112,96},{17,1},{33... | collective-permute-start | bytes 417800 | tf_op jit(solution)/shard_map/ppermute | solution.py:634
  49.1 1.5 %prep_side.1.feat_side_hbm.feat_side_ref = bf16[384,1024]{1,0:T(8,128)(2,1)S(1)} custom-call(bf16[128,128]{1,0:T(8,128)(2,1)S(1)} %copy-done.7, bf16[256,384]{1,0:T(8,128)(2,1)S(1)} %copy-done.5, bf16[64,8,128]{2,1,0:T(8,128)(2,1)S(1)} %collective-permute-done.4.left_ref, bf16[64,8,128]{2,1,0:T(8,128)(2,1)} %collective-permute-done.5.right_ref, ...), custom_call_target="tpu_custom_call" | custom-call | flops 300000000 | bytes 1500000 | tf_op jit(solution)/shard_map/prep_side/pallas_call | solution.py:155
  50.6 5.1 %own_grad.1.acc_ref = f32[384,384]{1,0:T(8,128)S(1)} custom-call(bf16[72,136,128]{2,1,0:T(8,128)(2,1)S(1)} %get-tuple-element.13.canvas_ref.canvas_hbm, bf16[72,16,128]{2,1,0:T(8,128)(2,1)S(1)} %get-tuple-element.20.side_hbm, bf16[64,3,128,128]{3,2,1,0:T(8,128)(2,1)S(1)} %copy-done.1, bf16[384,1024]{1,0:T(8,128)(2,1)S(1)} %prep_side.1.feat_side_hbm.feat_side_ref), custom_call_target="tpu_custom_call" | custom-call | flops 2800000000 | bytes 10000000 | tf_op jit(solution)/shard_map/own_grad/pallas_call | solution.py:372
  55.8 0.0 collective-permute-done.1.below_ref
  55.8 0.0 collective-permute-done.above_ref
  55.8 2.2 %halo_grad.1 = bf16[1280,128]{1,0:T(8,128)(2,1)} custom-call(f32[384,384]{1,0:T(8,128)S(1)} %own_grad.1.acc_ref, bf16[5,136,128]{2,1,0:T(8,128)(2,1)S(1)} %collective-permute-done.above_ref, bf16[4,136,128]{2,1,0:T(8,128)(2,1)S(1)} %collective-permute-done.1.below_ref, bf16[64,3,128,128]{3,2,1,0:T(8,128)(2,1)S(1)} %copy-done.1, ...), custom_call_target="tpu_custom_call" | custom-call | flops 420000000 | bytes 3500000 | tf_op jit(solution)/shard_map/halo_grad/pallas_call | solution.py:456
  58.0 0.0 copy-start.8
  58.0 8.7 %all-to-all-start.1 = ((bf16[128,5,2,128]{3,2,1,0:T(2,128)(2,1)}), bf16[128,5,2,128]{3,2,1,0:T(2,128)(2,1)S(1)}, u32[]{:S(2)}, u32[]{:S(2)}) async-start(bf16[128,5,2,128]{3,2,1,0:T(2,128)(2,1)} %bitcast.6), calls=%async_computation.1 | async-start | bytes 655360 | tf_op jit(solution)/shard_map/all_to_all | solution.py:626
  66.8 0.0 copy-start.4
  66.8 1.0 %copy-done.4 = bf16[72,24,128]{2,1,0:T(8,128)(2,1)S(1)} copy-done((bf16[72,24,128]{2,1,0:T(8,128)(2,1)S(1)}, bf16[72,24,128]{2,1,0:T(8,128)(2,1)}, u32[]{:S(2)}) %copy-start.4) | copy-done | bytes 442392
  67.8 0.8 sides.1
  68.5 3.1 %collective-permute-start.2 = (bf16[66,8,128]{2,1,0:T(8,128)(2,1)}, bf16[66,8,128]{2,1,0:T(8,128)(2,1)}, u32[]{:S(2)}, u32[]{:S(2)}) collective-permute-start(bf16[66,8,128]{2,1,0:T(8,128)(2,1)} %get-tuple-element.17), channel_id=1, source_target_pairs={{0,1},{1,2},{2,3},{3,4},{4,5},{5,6},{6,7},{7,8},{8,9},{9,10},{10,1... | collective-permute-start | bytes 405512 | tf_op jit(solution)/shard_map/ppermute | solution.py:633
  71.7 0.0 collective-permute-start.3
  71.7 7.2 %all-to-all-done.1 = bf16[128,5,2,128]{3,2,1,0:T(2,128)(2,1)S(1)} async-done(((bf16[128,5,2,128]{3,2,1,0:T(2,128)(2,1)}), bf16[128,5,2,128]{3,2,1,0:T(2,128)(2,1)S(1)}, u32[]{:S(2)}, u32[]{:S(2)}) %all-to-all-start.1) | async-done | bytes 327712 | tf_op jit(solution)/shard_map/all_to_all | solution.py:626
  78.9 1.0 %share.1 = bf16[1280,128]{1,0:T(8,128)(2,1)} custom-call(bf16[1280,128]{1,0:T(8,128)(2,1)S(1)} %bitcast.12), custom_call_target="tpu_custom_call" | custom-call | flops 10000000 | bytes 1000000 | tf_op jit(solution)/shard_map/share/pallas_call | solution.py:596
  79.9 4.1 %all-to-all-start.2 = ((bf16[128,5,2,128]{3,2,1,0:T(2,128)(2,1)}), bf16[128,5,2,128]{3,2,1,0:T(2,128)(2,1)S(1)}, u32[]{:S(2)}, u32[]{:S(2)}) async-start(bf16[128,5,2,128]{3,2,1,0:T(2,128)(2,1)} %bitcast.8), calls=%async_computation.2 | async-start | bytes 655360 | tf_op jit(solution)/shard_map/all_to_all | solution.py:626
  84.0 0.0 collective-permute-done.2.left_ref
  84.0 8.2 %conv.1 = bf16[64,128,128]{2,1,0:T(8,128)(2,1)} custom-call(bf16[72,136,128]{2,1,0:T(8,128)(2,1)S(1)} %get-tuple-element.13.canvas_ref.canvas_hbm, bf16[5,136,128]{2,1,0:T(8,128)(2,1)S(1)} %collective-permute-done.above_ref, bf16[4,136,128]{2,1,0:T(8,128)(2,1)S(1)} %collective-permute-done.1.below_ref, bf16[66,8,128]{2,1,0:T(8,128)(2,1)} %collective-permute-done.2.left_ref, ...), custom_call_target="tpu_custom_call" | custom-call | flops 2700000000 | bytes 4500000 | tf_op jit(solution)/shard_map/conv/pallas_call | solution.py:567
  92.2 3.7 %all-to-all-done.2 = bf16[128,5,2,128]{3,2,1,0:T(2,128)(2,1)S(1)} async-done(((bf16[128,5,2,128]{3,2,1,0:T(2,128)(2,1)}), bf16[128,5,2,128]{3,2,1,0:T(2,128)(2,1)S(1)}, u32[]{:S(2)}, u32[]{:S(2)}) %all-to-all-start.2) | async-done | bytes 327712 | tf_op jit(solution)/shard_map/all_to_all | solution.py:626
  95.9 0.9 finish.1
  (15 shorter events, 0.1 us)
Async XLA Ops:
  0.6 16.3 %copy-start.2 = (bf16[64,128,128]{2,1,0:T(8,128)(2,1)S(1)}, bf16[64,128,128]{2,1,0:T(8,128)(2,1)}, u32[]{:S(2)}) copy-start(bf16[64,128,128]{2,1,0:T(8,128)(2,1)} %feat_ref.1) | copy-start | bytes 6291460
  1.4 18.7 %copy-start.6 = (bf16[128,256]{1,0:T(8,128)(2,1)S(1)}, bf16[128,256]{1,0:T(8,128)(2,1)}, u32[]{:S(2)}) copy-start(bf16[128,256]{1,0:T(8,128)(2,1)} %constant.7.clone.shift_ref) | copy-start | bytes 196612
  5.4 26.3 %all-to-all-start = ((bf16[128,9,2,128]{3,2,1,0:T(2,128)(2,1)}), bf16[128,9,2,128]{3,2,1,0:T(2,128)(2,1)S(1)}, u32[]{:S(2)}, u32[]{:S(2)}) async-start(bf16[128,9,2,128]{3,2,1,0:T(2,128)(2,1)} %bitcast.14), calls=%async_computation | async-start | bytes 1179648 | tf_op jit(solution)/shard_map/all_to_all | solution.py:626
  16.9 29.5 %collective-permute-start.4 = (bf16[64,8,128]{2,1,0:T(8,128)(2,1)S(1)}, bf16[64,8,128]{2,1,0:T(8,128)(2,1)S(1)}, u32[]{:S(2)}, u32[]{:S(2)}) collective-permute-start(bf16[64,8,128]{2,1,0:T(8,128)(2,1)S(1)} %get-tuple-element.25.last_ref), channel_id=1, source_target_pairs={{0,1},{1,2},{2,3},{3,4},{4,5},{5,6},{6,7},{7,8},{8,9},{9,10},{10,1... | collective-permute-start | bytes 393224 | tf_op jit(solution)/shard_map/ppermute | solution.py:633
  20.1 26.3 %collective-permute-start.5 = (bf16[64,8,128]{2,1,0:T(8,128)(2,1)S(1)}, bf16[64,8,128]{2,1,0:T(8,128)(2,1)}, u32[]{:S(2)}, u32[]{:S(2)}) collective-permute-start(bf16[64,8,128]{2,1,0:T(8,128)(2,1)S(1)} %get-tuple-element.24.head_ref), channel_id=1, source_target_pairs={{1,0},{2,1},{3,2},{4,3},{5,4},{6,5},{7,6},{8,7},{9,8},{10,9},{11,1... | collective-permute-start | bytes 393224 | tf_op jit(solution)/shard_map/ppermute | solution.py:634
  22.1 2.7 %copy-start = (bf16[64,3,128,128]{3,2,1,0:T(8,128)(2,1)}, bf16[64,3,128,128]{3,2,1,0:T(8,128)(2,1)S(1)}, u32[]{:S(2)}) copy-start(bf16[64,3,128,128]{3,2,1,0:T(8,128)(2,1)S(1)} %prep.1.feat_hbm) | copy-start | bytes 18874372
  31.7 17.4 %copy-start.5 = (bf16[256,384]{1,0:T(8,128)(2,1)S(1)}, bf16[256,384]{1,0:T(8,128)(2,1)}, u32[]{:S(2)}) copy-start(bf16[256,384]{1,0:T(8,128)(2,1)} %constant.8.clone.pick_ref) | copy-start | bytes 589828
  31.7 17.4 %copy-start.7 = (bf16[128,128]{1,0:T(8,128)(2,1)S(1)}, bf16[128,128]{1,0:T(8,128)(2,1)}, u32[]{:S(2)}) copy-start(bf16[128,128]{1,0:T(8,128)(2,1)} %constant.6.clone.eye_ref) | copy-start | bytes 98308
  31.7 19.0 %copy-start.1 = (bf16[64,3,128,128]{3,2,1,0:T(8,128)(2,1)S(1)}, bf16[64,3,128,128]{3,2,1,0:T(8,128)(2,1)}, u32[]{:S(2)}) copy-start(bf16[64,3,128,128]{3,2,1,0:T(8,128)(2,1)} %copy-done) | copy-start | bytes 18874372
  46.4 9.3 %copy-start.3 = (bf16[72,24,128]{2,1,0:T(8,128)(2,1)}, bf16[72,24,128]{2,1,0:T(8,128)(2,1)S(1)}, u32[]{:S(2)}) copy-start(bf16[72,24,128]{2,1,0:T(8,128)(2,1)S(1)} %get-tuple-element.16.rim_ref) | copy-start | bytes 1327108
  46.5 9.3 %collective-permute-start = (bf16[5,136,128]{2,1,0:T(8,128)(2,1)S(1)}, bf16[5,136,128]{2,1,0:T(8,128)(2,1)S(1)}, u32[]{:S(2)}, u32[]{:S(2)}) collective-permute-start(bf16[5,136,128]{2,1,0:T(8,128)(2,1)S(1)} %get-tuple-element.14), channel_id=1, source_target_pairs={{0,16},{16,32},{32,48},{48,64},{64,80},{80,96},{96,112},{1,17},{17... | collective-permute-start | bytes 522248 | tf_op jit(solution)/shard_map/ppermute | solution.py:633
  47.8 8.0 %collective-permute-start.1 = (bf16[4,136,128]{2,1,0:T(8,128)(2,1)S(1)}, bf16[4,136,128]{2,1,0:T(8,128)(2,1)S(1)}, u32[]{:S(2)}, u32[]{:S(2)}) collective-permute-start(bf16[4,136,128]{2,1,0:T(8,128)(2,1)S(1)} %get-tuple-element.15), channel_id=1, source_target_pairs={{16,0},{32,16},{48,32},{64,48},{80,64},{96,80},{112,96},{17,1},{33... | collective-permute-start | bytes 417800 | tf_op jit(solution)/shard_map/ppermute | solution.py:634
  58.0 26.0 %copy-start.8 = (bf16[3,3,128,128]{3,2,1,0:T(8,128)(2,1)S(1)}, bf16[3,3,128,128]{3,2,1,0:T(8,128)(2,1)}, u32[]{:S(2)}) copy-start(bf16[3,3,128,128]{3,2,1,0:T(8,128)(2,1)} %weight_ref.1) | copy-start | bytes 884740
  58.0 20.9 %all-to-all-start.1 = ((bf16[128,5,2,128]{3,2,1,0:T(2,128)(2,1)}), bf16[128,5,2,128]{3,2,1,0:T(2,128)(2,1)S(1)}, u32[]{:S(2)}, u32[]{:S(2)}) async-start(bf16[128,5,2,128]{3,2,1,0:T(2,128)(2,1)} %bitcast.6), calls=%async_computation.1 | async-start | bytes 655360 | tf_op jit(solution)/shard_map/all_to_all | solution.py:626
  66.8 1.0 %copy-start.4 = (bf16[72,24,128]{2,1,0:T(8,128)(2,1)S(1)}, bf16[72,24,128]{2,1,0:T(8,128)(2,1)}, u32[]{:S(2)}) copy-start(bf16[72,24,128]{2,1,0:T(8,128)(2,1)} %copy-done.3) | copy-start | bytes 1327108
  68.5 15.5 %collective-permute-start.2 = (bf16[66,8,128]{2,1,0:T(8,128)(2,1)}, bf16[66,8,128]{2,1,0:T(8,128)(2,1)}, u32[]{:S(2)}, u32[]{:S(2)}) collective-permute-start(bf16[66,8,128]{2,1,0:T(8,128)(2,1)} %get-tuple-element.17), channel_id=1, source_target_pairs={{0,1},{1,2},{2,3},{3,4},{4,5},{5,6},{6,7},{7,8},{8,9},{9,10},{10,1... | collective-permute-start | bytes 405512 | tf_op jit(solution)/shard_map/ppermute | solution.py:633
  71.7 12.3 %collective-permute-start.3 = (bf16[66,8,128]{2,1,0:T(8,128)(2,1)}, bf16[66,8,128]{2,1,0:T(8,128)(2,1)}, u32[]{:S(2)}, u32[]{:S(2)}) collective-permute-start(bf16[66,8,128]{2,1,0:T(8,128)(2,1)} %get-tuple-element.18), channel_id=1, source_target_pairs={{1,0},{2,1},{3,2},{4,3},{5,4},{6,5},{7,6},{8,7},{9,8},{10,9},{11,1... | collective-permute-start | bytes 405512 | tf_op jit(solution)/shard_map/ppermute | solution.py:634
  79.9 16.0 %all-to-all-start.2 = ((bf16[128,5,2,128]{3,2,1,0:T(2,128)(2,1)}), bf16[128,5,2,128]{3,2,1,0:T(2,128)(2,1)S(1)}, u32[]{:S(2)}, u32[]{:S(2)}) async-start(bf16[128,5,2,128]{3,2,1,0:T(2,128)(2,1)} %bitcast.8), calls=%async_computation.2 | async-start | bytes 655360 | tf_op jit(solution)/shard_map/all_to_all | solution.py:626

commit v10 on v9

--- a/solution.py
+++ b/solution.py
@@ -312,46 +312,20 @@
     )(incoming)
 
 
-def own_grad_kernel(
-    canvas_hbm, side_hbm, feat_hbm, feat_side_hbm, acc_ref, canvas, side, feat, feat_side, sem
-):
-    step = 16
-    ends = (0, 18, 34, 50, 66)
-    parts = [
-        (
-            pltpu.make_async_copy(
-                canvas_hbm.at[3 + ends[k] : 3 + ends[k + 1]],
-                canvas.at[ends[k] : ends[k + 1]],
-                sem.at[2 * k],
-            ),
-            pltpu.make_async_copy(
-                feat_hbm.at[k * step : (k + 1) * step],
-                feat.at[k * step : (k + 1) * step],
-                sem.at[2 * k + 1],
-            ),
-        )
-        for k in range(4)
-    ]
-    rest = [
-        pltpu.make_async_copy(side_hbm.at[3:69], side, sem.at[8]),
-        pltpu.make_async_copy(feat_side_hbm, feat_side, sem.at[9]),
-    ]
-    for pair in parts:
-        for copy in pair:
-            copy.start()
-    for copy in rest:
-        copy.start()
-    total = jnp.zeros((384, 384), F32)
-    for k in range(4):
-        for copy in parts[k]:
-            copy.wait()
+def own_grad_kernel(canvas, side, feat, feat_side, acc_ref):
+    step = 32
+    rhs = jnp.concatenate(
+        [side[5 - a : 69 - a].reshape(1024, 128) for a in range(3)], axis=1
+    )
+    total = mm(feat_side[...], rhs)
+    for k in range(64 // step):
         lines = range(k * step, (k + 1) * step)
         lhs = jnp.concatenate(
             [jnp.concatenate([feat[i, b] for i in lines], axis=1) for b in range(3)], axis=0
         )
         rhs = jnp.concatenate(
             [
-                canvas[k * step + 2 - a : (k + 1) * step + 2 - a, 0:128, :].reshape(
+                canvas[k * step + 5 - a : (k + 1) * step + 5 - a, 0:128, :].reshape(
                     step * 128, 128
                 )
                 for a in range(3)
@@ -359,32 +333,20 @@
             axis=1,
         )
         total = total + mm(lhs, rhs)
-    for copy in rest:
-        copy.wait()
-    rhs = jnp.concatenate(
-        [side[2 - a : 66 - a].reshape(1024, 128) for a in range(3)], axis=1
-    )
-    acc_ref[...] = total + mm(feat_side[...], rhs)
+    acc_ref[...] = total
 
 
 def own_grad(canvas, side, feat, feat_side):
-    hbm = pl.BlockSpec(memory_space=pltpu.HBM)
+    vmem = pl.BlockSpec(memory_space=pltpu.VMEM)
     return pl.pallas_call(
         own_grad_kernel,
         out_shape=jax.ShapeDtypeStruct((384, 384), F32),
-        in_specs=[hbm] * 4,
-        out_specs=pl.BlockSpec(memory_space=pltpu.VMEM),
-        scratch_shapes=[
-            pltpu.VMEM((66, 136, 128), BF16),
-            pltpu.VMEM((66, 16, 128), BF16),
-            pltpu.VMEM((64, 3, 128, 128), BF16),
-            pltpu.VMEM((384, 1024), BF16),
-            pltpu.SemaphoreType.DMA((10,)),
-        ],
+        in_specs=[vmem] * 4,
+        out_specs=vmem,
+        compiler_params=pltpu.CompilerParams(vmem_limit_bytes=20 << 20),
         cost_estimate=pl.CostEstimate(
             flops=2_800_000_000, bytes_accessed=10_000_000, transcendentals=0
         ),
-        compiler_params=pltpu.CompilerParams(vmem_limit_bytes=20 << 20),
         name="own_grad",
     )(canvas, side, feat, feat_side)
 

time: 97.1 us -> 97.1 us (level)
  Pallas kernels: 40.3 us -> 38.9 us
  starting transfers between devices: 33.2 us -> 34.6 us
    all_to_all x3, starting transfers between devices: 24.3 us -> 25.6 us  [exchange(): return lax.all_to_all(pairs, AXES, 0, 0, tiled=True).reshape(rows.shape)]
    pallas_call x1, Pallas kernels: 5.13 us -> 3.8 us  [own_grad(): pl.pallas_call(own_grad_kernel, out_shape=jax.ShapeDtypeStruct((384, 384)...]
  transfers between devices with their start and end apart: 9 -> 9, of which waited for: 3 -> 3; matrix products, arithmetic and copies ran while one was open for 0% -> 0% of each run, Pallas kernels for 34% -> 33%
where the time goes in v10:
time: 97.1 us; the launch traced here: 96.7 us
  Pallas kernels  38.9 us (40%)
  starting transfers between devices  34.6 us (36%)
  waiting for transfers between devices  17.8 us (18%)
  local copies, waits for them, and re-layouts  3.73 us (4%)
  between operations  1.66 us (2%)
    all_to_all x3, starting transfers between devices, exchange(): return lax.all_to_all(pairs, AXES, 0, 0, tiled=True).reshape(rows.shape)  25.6 us
    all_to_all x3, waiting for transfers between devices, exchange(): return lax.all_to_all(pairs, AXES, 0, 0, tiled=True).reshape(rows.shape)  17.8 us
    pallas_call x1, Pallas kernels, scatter(): pl.pallas_call(scatter_kernel, out_shape=(jax.ShapeDtypeStruct((72, 136,...  14.8 us
    pallas_call x1, Pallas kernels, conv(): pl.pallas_call(conv_kernel, grid=(8,), out_shape=jax.ShapeDtypeStruct((64...  8.15 us
    ppermute x3, starting transfers between devices, both_ways(): lax.ppermute(forth, axis, [(i, (i + 1) % count) for i in range(ends)])  7.64 us
    pallas_call x1, Pallas kernels, pack(): pl.pallas_call(pack_kernel, out_shape=jax.ShapeDtypeStruct((TILES * CHUNK...  3.94 us
    pallas_call x1, Pallas kernels, own_grad(): pl.pallas_call(own_grad_kernel, out_shape=jax.ShapeDtypeStruct((384, 384)...  3.8 us
    unnamed x18, local copies, waits for them, and re-layouts  3.69 us
  transfers between devices with their start and end apart: 9, of which 3 were waited for; matrix products, arithmetic and copies ran while one was open for 0% of the time, Pallas kernels for 33%

profile of v10, /device:TPU:1, one launch (start us, length us, event | category | flops | bytes accessed | tf_op | source)
XLA Modules:
  0.0 96.7 jit_solution(1463260428502885177)
XLA Ops:
  1.4 0.0 copy-start.6
  1.4 3.9 %pack.1 = bf16[2304,128]{1,0:T(8,128)(2,1)} custom-call(s32[1]{0:T(128)S(6)} %copy.13.live_ref, s32[1,1024]{1,0:T(1,128)} %bitcast.16, s32[1,1024]{1,0:T(1,128)} %bitcast.17, s32[1,1024]{1,0:T(1,128)} %bitcast.18, bf16[2,1024]{1,0:T(2,128)(2,1)} %bitcast.19, bf16[1024,128]{1,0:T(8,128)(2,1)} %rows_ref.1), custom_call_target="tpu_custom_call" | custom-call | flops 700000000 | bytes 1500000 | tf_op jit(solution)/shard_map/pack/pallas_call | solution.py:81
  5.4 11.5 %all-to-all-start = ((bf16[128,9,2,128]{3,2,1,0:T(2,128)(2,1)}), bf16[128,9,2,128]{3,2,1,0:T(2,128)(2,1)S(1)}, u32[]{:S(2)}, u32[]{:S(2)}) async-start(bf16[128,9,2,128]{3,2,1,0:T(2,128)(2,1)} %bitcast.14), calls=%async_computation | async-start | bytes 1179648 | tf_op jit(solution)/shard_map/all_to_all | solution.py:588
  16.9 3.2 %collective-permute-start.4 = (bf16[64,8,128]{2,1,0:T(8,128)(2,1)S(1)}, bf16[64,8,128]{2,1,0:T(8,128)(2,1)S(1)}, u32[]{:S(2)}, u32[]{:S(2)}) collective-permute-start(bf16[64,8,128]{2,1,0:T(8,128)(2,1)S(1)} %get-tuple-element.25.last_ref), channel_id=1, source_target_pairs={{0,1},{1,2},{2,3},{3,4},{4,5},{5,6},{6,7},{7,8},{8,9},{9,10},{10,1... | collective-permute-start | bytes 393224 | tf_op jit(solution)/shard_map/ppermute | solution.py:595
  20.1 0.0 collective-permute-start.5
  20.1 1.9 %prep.1.feat.feat_hbm = bf16[64,3,128,128]{3,2,1,0:T(8,128)(2,1)S(1)} custom-call(bf16[128,256]{1,0:T(8,128)(2,1)S(1)} %copy-done.6, bf16[64,128,128]{2,1,0:T(8,128)(2,1)S(1)} %copy-done.2), custom_call_target="tpu_custom_call" | custom-call | flops 2200000000 | bytes 8000000 | tf_op jit(solution)/shard_map/prep/pallas_call | solution.py:124
  22.1 2.6 %copy-done = bf16[64,3,128,128]{3,2,1,0:T(8,128)(2,1)} copy-done((bf16[64,3,128,128]{3,2,1,0:T(8,128)(2,1)}, bf16[64,3,128,128]{3,2,1,0:T(8,128)(2,1)S(1)}, u32[]{:S(2)}) %copy-start) | copy-done | bytes 6291480
  24.7 6.9 %all-to-all-done = bf16[128,9,2,128]{3,2,1,0:T(2,128)(2,1)S(1)} async-done(((bf16[128,9,2,128]{3,2,1,0:T(2,128)(2,1)}), bf16[128,9,2,128]{3,2,1,0:T(2,128)(2,1)S(1)}, u32[]{:S(2)}, u32[]{:S(2)}) %all-to-all-start) | async-done | bytes 589856 | tf_op jit(solution)/shard_map/all_to_all | solution.py:588
  31.7 14.8 %scatter.1 = (bf16[72,136,128]{2,1,0:T(8,128)(2,1)S(1)}, bf16[72,16,128]{2,1,0:T(8,128)(2,1)S(1)}, bf16[72,24,128]{2,1,0:T(8,128)(2,1)S(1)}, bf16[4,136,128]{2,1,0:T(8,128)(2,1)S(1)}, bf16[5,136,128]{2,1,0:T(8,128)(2,1)S(1)}) custom-call(bf16[2304,128]{1,0:T(8,128)(2,1)S(1)} %bitcast.13), custom_call_target="tpu_custom_call" | custom-call | flops 5200000000 | bytes 4000000 | tf_op jit(solution)/shard_map/scatter/pallas_call | solution.py:285
  46.4 0.0 copy-start.3
  46.5 0.0 collective-permute-done.5.right_ref
  46.5 1.3 %collective-permute-start = (bf16[5,136,128]{2,1,0:T(8,128)(2,1)S(1)}, bf16[5,136,128]{2,1,0:T(8,128)(2,1)S(1)}, u32[]{:S(2)}, u32[]{:S(2)}) collective-permute-start(bf16[5,136,128]{2,1,0:T(8,128)(2,1)S(1)} %get-tuple-element.14), channel_id=1, source_target_pairs={{0,16},{16,32},{32,48},{48,64},{64,80},{80,96},{96,112},{1,17},{17... | collective-permute-start | bytes 522248 | tf_op jit(solution)/shard_map/ppermute | solution.py:595
  47.8 1.3 %collective-permute-start.1 = (bf16[4,136,128]{2,1,0:T(8,128)(2,1)S(1)}, bf16[4,136,128]{2,1,0:T(8,128)(2,1)S(1)}, u32[]{:S(2)}, u32[]{:S(2)}) collective-permute-start(bf16[4,136,128]{2,1,0:T(8,128)(2,1)S(1)} %get-tuple-element.15), channel_id=1, source_target_pairs={{16,0},{32,16},{48,32},{64,48},{80,64},{96,80},{112,96},{17,1},{33... | collective-permute-start | bytes 417800 | tf_op jit(solution)/shard_map/ppermute | solution.py:596
  49.1 1.5 %prep_side.1.feat_side.feat_side_ref = bf16[384,1024]{1,0:T(8,128)(2,1)S(1)} custom-call(bf16[128,128]{1,0:T(8,128)(2,1)S(1)} %copy-done.7, bf16[256,384]{1,0:T(8,128)(2,1)S(1)} %copy-done.5, bf16[64,8,128]{2,1,0:T(8,128)(2,1)S(1)} %collective-permute-done.4.left_ref, bf16[64,8,128]{2,1,0:T(8,128)(2,1)} %collective-permute-done.5.right_ref, ...), custom_call_target="tpu_custom_call" | custom-call | flops 300000000 | bytes 1500000 | tf_op jit(solution)/shard_map/prep_side/pallas_call | solution.py:155
  50.6 3.8 %own_grad.1.acc_ref = f32[384,384]{1,0:T(8,128)S(1)} custom-call(bf16[72,136,128]{2,1,0:T(8,128)(2,1)S(1)} %get-tuple-element.13.canvas_ref.canvas, bf16[72,16,128]{2,1,0:T(8,128)(2,1)S(1)} %get-tuple-element.20.side, bf16[64,3,128,128]{3,2,1,0:T(8,128)(2,1)S(1)} %copy-done.1, bf16[384,1024]{1,0:T(8,128)(2,1)S(1)} %prep_side.1.feat_side.feat_side_ref), custom_call_target="tpu_custom_call" | custom-call | flops 2800000000 | bytes 10000000 | tf_op jit(solution)/shard_map/own_grad/pallas_call | solution.py:341
  54.5 0.0 collective-permute-done.1.below_ref
  54.5 2.2 %halo_grad.1 = bf16[1280,128]{1,0:T(8,128)(2,1)} custom-call(f32[384,384]{1,0:T(8,128)S(1)} %own_grad.1.acc_ref, bf16[5,136,128]{2,1,0:T(8,128)(2,1)S(1)} %collective-permute-done.above_ref, bf16[4,136,128]{2,1,0:T(8,128)(2,1)S(1)} %collective-permute-done.1.below_ref, bf16[64,3,128,128]{3,2,1,0:T(8,128)(2,1)S(1)} %copy-done.1, ...), custom_call_target="tpu_custom_call" | custom-call | flops 420000000 | bytes 3500000 | tf_op jit(solution)/shard_map/halo_grad/pallas_call | solution.py:418
  56.7 0.0 copy-start.8
  56.7 10.1 %all-to-all-start.1 = ((bf16[128,5,2,128]{3,2,1,0:T(2,128)(2,1)}), bf16[128,5,2,128]{3,2,1,0:T(2,128)(2,1)S(1)}, u32[]{:S(2)}, u32[]{:S(2)}) async-start(bf16[128,5,2,128]{3,2,1,0:T(2,128)(2,1)} %bitcast.6), calls=%async_computation.1 | async-start | bytes 655360 | tf_op jit(solution)/shard_map/all_to_all | solution.py:588
  66.8 0.0 copy-start.4
  66.8 1.0 %copy-done.4 = bf16[72,24,128]{2,1,0:T(8,128)(2,1)S(1)} copy-done((bf16[72,24,128]{2,1,0:T(8,128)(2,1)S(1)}, bf16[72,24,128]{2,1,0:T(8,128)(2,1)}, u32[]{:S(2)}) %copy-start.4) | copy-done | bytes 442392
  67.8 0.8 sides.1
  68.5 3.1 %collective-permute-start.2 = (bf16[66,8,128]{2,1,0:T(8,128)(2,1)}, bf16[66,8,128]{2,1,0:T(8,128)(2,1)}, u32[]{:S(2)}, u32[]{:S(2)}) collective-permute-start(bf16[66,8,128]{2,1,0:T(8,128)(2,1)} %get-tuple-element.17), channel_id=1, source_target_pairs={{0,1},{1,2},{2,3},{3,4},{4,5},{5,6},{6,7},{7,8},{8,9},{9,10},{10,1... | collective-permute-start | bytes 405512 | tf_op jit(solution)/shard_map/ppermute | solution.py:595
  71.7 0.0 collective-permute-start.3
  71.7 7.2 %all-to-all-done.1 = bf16[128,5,2,128]{3,2,1,0:T(2,128)(2,1)S(1)} async-done(((bf16[128,5,2,128]{3,2,1,0:T(2,128)(2,1)}), bf16[128,5,2,128]{3,2,1,0:T(2,128)(2,1)S(1)}, u32[]{:S(2)}, u32[]{:S(2)}) %all-to-all-start.1) | async-done | bytes 327712 | tf_op jit(solution)/shard_map/all_to_all | solution.py:588
  78.9 1.0 %share.1 = bf16[1280,128]{1,0:T(8,128)(2,1)} custom-call(bf16[1280,128]{1,0:T(8,128)(2,1)S(1)} %bitcast.12), custom_call_target="tpu_custom_call" | custom-call | flops 10000000 | bytes 1000000 | tf_op jit(solution)/shard_map/share/pallas_call | solution.py:558
  79.9 4.1 %all-to-all-start.2 = ((bf16[128,5,2,128]{3,2,1,0:T(2,128)(2,1)}), bf16[128,5,2,128]{3,2,1,0:T(2,128)(2,1)S(1)}, u32[]{:S(2)}, u32[]{:S(2)}) async-start(bf16[128,5,2,128]{3,2,1,0:T(2,128)(2,1)} %bitcast.8), calls=%async_computation.2 | async-start | bytes 655360 | tf_op jit(solution)/shard_map/all_to_all | solution.py:588
  84.0 0.0 collective-permute-done.2.left_ref
  84.0 0.0 collective-permute-done.3.right_ref
  84.0 8.2 %conv.1 = bf16[64,128,128]{2,1,0:T(8,128)(2,1)} custom-call(bf16[72,136,128]{2,1,0:T(8,128)(2,1)S(1)} %get-tuple-element.13.canvas_ref.canvas, bf16[5,136,128]{2,1,0:T(8,128)(2,1)S(1)} %collective-permute-done.above_ref, bf16[4,136,128]{2,1,0:T(8,128)(2,1)S(1)} %collective-permute-done.1.below_ref, bf16[66,8,128]{2,1,0:T(8,128)(2,1)} %collective-permute-done.2.left_ref, ...), custom_call_target="tpu_custom_call" | custom-call | flops 2700000000 | bytes 4500000 | tf_op jit(solution)/shard_map/conv/pallas_call | solution.py:529
  92.2 3.7 %all-to-all-done.2 = bf16[128,5,2,128]{3,2,1,0:T(2,128)(2,1)S(1)} async-done(((bf16[128,5,2,128]{3,2,1,0:T(2,128)(2,1)}), bf16[128,5,2,128]{3,2,1,0:T(2,128)(2,1)S(1)}, u32[]{:S(2)}, u32[]{:S(2)}) %all-to-all-start.2) | async-done | bytes 327712 | tf_op jit(solution)/shard_map/all_to_all | solution.py:588
  95.9 0.9 finish.1
  (15 shorter events, 0.1 us)
Async XLA Ops:
  0.6 16.3 %copy-start.2 = (bf16[64,128,128]{2,1,0:T(8,128)(2,1)S(1)}, bf16[64,128,128]{2,1,0:T(8,128)(2,1)}, u32[]{:S(2)}) copy-start(bf16[64,128,128]{2,1,0:T(8,128)(2,1)} %feat_ref.1) | copy-start | bytes 6291460
  1.4 18.7 %copy-start.6 = (bf16[128,256]{1,0:T(8,128)(2,1)S(1)}, bf16[128,256]{1,0:T(8,128)(2,1)}, u32[]{:S(2)}) copy-start(bf16[128,256]{1,0:T(8,128)(2,1)} %constant.7.clone.shift_ref) | copy-start | bytes 196612
  5.4 26.3 %all-to-all-start = ((bf16[128,9,2,128]{3,2,1,0:T(2,128)(2,1)}), bf16[128,9,2,128]{3,2,1,0:T(2,128)(2,1)S(1)}, u32[]{:S(2)}, u32[]{:S(2)}) async-start(bf16[128,9,2,128]{3,2,1,0:T(2,128)(2,1)} %bitcast.14), calls=%async_computation | async-start | bytes 1179648 | tf_op jit(solution)/shard_map/all_to_all | solution.py:588
  16.9 29.5 %collective-permute-start.4 = (bf16[64,8,128]{2,1,0:T(8,128)(2,1)S(1)}, bf16[64,8,128]{2,1,0:T(8,128)(2,1)S(1)}, u32[]{:S(2)}, u32[]{:S(2)}) collective-permute-start(bf16[64,8,128]{2,1,0:T(8,128)(2,1)S(1)} %get-tuple-element.25.last_ref), channel_id=1, source_target_pairs={{0,1},{1,2},{2,3},{3,4},{4,5},{5,6},{6,7},{7,8},{8,9},{9,10},{10,1... | collective-permute-start | bytes 393224 | tf_op jit(solution)/shard_map/ppermute | solution.py:595
  20.1 26.3 %collective-permute-start.5 = (bf16[64,8,128]{2,1,0:T(8,128)(2,1)S(1)}, bf16[64,8,128]{2,1,0:T(8,128)(2,1)}, u32[]{:S(2)}, u32[]{:S(2)}) collective-permute-start(bf16[64,8,128]{2,1,0:T(8,128)(2,1)S(1)} %get-tuple-element.24.head_ref), channel_id=1, source_target_pairs={{1,0},{2,1},{3,2},{4,3},{5,4},{6,5},{7,6},{8,7},{9,8},{10,9},{11,1... | collective-permute-start | bytes 393224 | tf_op jit(solution)/shard_map/ppermute | solution.py:596
  22.1 2.7 %copy-start = (bf16[64,3,128,128]{3,2,1,0:T(8,128)(2,1)}, bf16[64,3,128,128]{3,2,1,0:T(8,128)(2,1)S(1)}, u32[]{:S(2)}) copy-start(bf16[64,3,128,128]{3,2,1,0:T(8,128)(2,1)S(1)} %prep.1.feat.feat_hbm) | copy-start | bytes 18874372
  31.7 17.4 %copy-start.5 = (bf16[256,384]{1,0:T(8,128)(2,1)S(1)}, bf16[256,384]{1,0:T(8,128)(2,1)}, u32[]{:S(2)}) copy-start(bf16[256,384]{1,0:T(8,128)(2,1)} %constant.8.clone.pick_ref) | copy-start | bytes 589828
  31.7 17.4 %copy-start.7 = (bf16[128,128]{1,0:T(8,128)(2,1)S(1)}, bf16[128,128]{1,0:T(8,128)(2,1)}, u32[]{:S(2)}) copy-start(bf16[128,128]{1,0:T(8,128)(2,1)} %constant.6.clone.eye_ref) | copy-start | bytes 98308
  31.7 19.0 %copy-start.1 = (bf16[64,3,128,128]{3,2,1,0:T(8,128)(2,1)S(1)}, bf16[64,3,128,128]{3,2,1,0:T(8,128)(2,1)}, u32[]{:S(2)}) copy-start(bf16[64,3,128,128]{3,2,1,0:T(8,128)(2,1)} %copy-done) | copy-start | bytes 18874372
  46.4 8.0 %copy-start.3 = (bf16[72,24,128]{2,1,0:T(8,128)(2,1)}, bf16[72,24,128]{2,1,0:T(8,128)(2,1)S(1)}, u32[]{:S(2)}) copy-start(bf16[72,24,128]{2,1,0:T(8,128)(2,1)S(1)} %get-tuple-element.16.rim_ref) | copy-start | bytes 1327108
  46.5 8.0 %collective-permute-start = (bf16[5,136,128]{2,1,0:T(8,128)(2,1)S(1)}, bf16[5,136,128]{2,1,0:T(8,128)(2,1)S(1)}, u32[]{:S(2)}, u32[]{:S(2)}) collective-permute-start(bf16[5,136,128]{2,1,0:T(8,128)(2,1)S(1)} %get-tuple-element.14), channel_id=1, source_target_pairs={{0,16},{16,32},{32,48},{48,64},{64,80},{80,96},{96,112},{1,17},{17... | collective-permute-start | bytes 522248 | tf_op jit(solution)/shard_map/ppermute | solution.py:595
  47.8 6.7 %collective-permute-start.1 = (bf16[4,136,128]{2,1,0:T(8,128)(2,1)S(1)}, bf16[4,136,128]{2,1,0:T(8,128)(2,1)S(1)}, u32[]{:S(2)}, u32[]{:S(2)}) collective-permute-start(bf16[4,136,128]{2,1,0:T(8,128)(2,1)S(1)} %get-tuple-element.15), channel_id=1, source_target_pairs={{16,0},{32,16},{48,32},{64,48},{80,64},{96,80},{112,96},{17,1},{33... | collective-permute-start | bytes 417800 | tf_op jit(solution)/shard_map/ppermute | solution.py:596
  56.7 27.3 %copy-start.8 = (bf16[3,3,128,128]{3,2,1,0:T(8,128)(2,1)S(1)}, bf16[3,3,128,128]{3,2,1,0:T(8,128)(2,1)}, u32[]{:S(2)}) copy-start(bf16[3,3,128,128]{3,2,1,0:T(8,128)(2,1)} %weight_ref.1) | copy-start | bytes 884740
  56.7 22.2 %all-to-all-start.1 = ((bf16[128,5,2,128]{3,2,1,0:T(2,128)(2,1)}), bf16[128,5,2,128]{3,2,1,0:T(2,128)(2,1)S(1)}, u32[]{:S(2)}, u32[]{:S(2)}) async-start(bf16[128,5,2,128]{3,2,1,0:T(2,128)(2,1)} %bitcast.6), calls=%async_computation.1 | async-start | bytes 655360 | tf_op jit(solution)/shard_map/all_to_all | solution.py:588
  66.8 1.0 %copy-start.4 = (bf16[72,24,128]{2,1,0:T(8,128)(2,1)S(1)}, bf16[72,24,128]{2,1,0:T(8,128)(2,1)}, u32[]{:S(2)}) copy-start(bf16[72,24,128]{2,1,0:T(8,128)(2,1)} %copy-done.3) | copy-start | bytes 1327108
  68.5 15.5 %collective-permute-start.2 = (bf16[66,8,128]{2,1,0:T(8,128)(2,1)}, bf16[66,8,128]{2,1,0:T(8,128)(2,1)}, u32[]{:S(2)}, u32[]{:S(2)}) collective-permute-start(bf16[66,8,128]{2,1,0:T(8,128)(2,1)} %get-tuple-element.17), channel_id=1, source_target_pairs={{0,1},{1,2},{2,3},{3,4},{4,5},{5,6},{6,7},{7,8},{8,9},{9,10},{10,1... | collective-permute-start | bytes 405512 | tf_op jit(solution)/shard_map/ppermute | solution.py:595
  71.7 12.3 %collective-permute-start.3 = (bf16[66,8,128]{2,1,0:T(8,128)(2,1)}, bf16[66,8,128]{2,1,0:T(8,128)(2,1)}, u32[]{:S(2)}, u32[]{:S(2)}) collective-permute-start(bf16[66,8,128]{2,1,0:T(8,128)(2,1)} %get-tuple-element.18), channel_id=1, source_target_pairs={{1,0},{2,1},{3,2},{4,3},{5,4},{6,5},{7,6},{8,7},{9,8},{10,9},{11,1... | collective-permute-start | bytes 405512 | tf_op jit(solution)/shard_map/ppermute | solution.py:596
  79.9 16.0 %all-to-all-start.2 = ((bf16[128,5,2,128]{3,2,1,0:T(2,128)(2,1)}), bf16[128,5,2,128]{3,2,1,0:T(2,128)(2,1)S(1)}, u32[]{:S(2)}, u32[]{:S(2)}) async-start(bf16[128,5,2,128]{3,2,1,0:T(2,128)(2,1)} %bitcast.8), calls=%async_computation.2 | async-start | bytes 655360 | tf_op jit(solution)/shard_map/all_to_all | solution.py:588
